TPU v7x, 768 devices: a whole 4x8x12 slice. The times are simulated.
768 devices in a mesh: seq: 96 (over z, x, core), head: 8 (over y).
Axes of the slice: x: 4, y: 8, z: 12, core: 2. Of those that a mesh axis runs over, the one named last changes fastest.
Arguments:
- tokens: bfloat16 [24576, 2048], P('seq'), may hold values from -6 to 6
- q_weight: bfloat16 [2048, 4096], P(None, 'head'), may hold values from -0.125 to 0.125
- gate_weight: bfloat16 [2048, 4096], P(None, 'head'), may hold values from -0.125 to 0.125
- k_weight: bfloat16 [2048, 512], replicated, may hold values from -0.125 to 0.125
- v_weight: bfloat16 [2048, 512], replicated, may hold values from -0.125 to 0.125
- q_gain: float32 [256], replicated, may hold values from 0.1 to 1.9
- k_gain: float32 [256], replicated, may hold values from 0.1 to 1.9
- out_weight: bfloat16 [4096, 2048], P('head'), may hold values from -0.09375 to 0.09375
- doc_starts: int32 [48], replicated, may hold values from 0 to 24575, as said below
- readers: int32 [96, 3], replicated, may hold values from 0 to 1, as said below
Outputs:
- attended: bfloat16 [24576, 2048], P(('seq', 'head'))
Inputs may be any that keep to these rules, and one draw needn't show every extreme that they name: doc_starts[0] = 0, doc_starts[47] = 24575, and for m >= 1 doc_starts[m] lies in [m * 512, (m + 1) * 512); every document has 1 to 1023 tokens, and one has exactly 1023 and starts at a multiple of 256. readers[j, s - 1] is 1 exactly when block j and block j + s (s = 1 to 3, j + s below 96) hold tokens of one document, as given by doc_starts; some block has a reader at distance 3.
All inputs are finite; a program needn't handle non-finite values.
Results may differ from a plain program's by a relative error of at most 0.015.
Values may be sent and summed in bfloat16 or wider, within the bound.
No kernel may reach another device: no remote copies, remote signals or barrier semaphores. Data moves between devices by JAX's collectives and lax.ppermute only.
A program may use at most 64 MiB of HBM per device.

v0:
```python
import jax
import jax.numpy as jnp
from jax import lax
from jax.sharding import PartitionSpec as P

HEADS = 16


ROPE_THETA = 10000000.0
EPSILON = 1e-06


def passed_along(block, axis, distance):
    devices = range(lax.axis_size(axis))
    route = [(i - distance, i) for i in devices if i - distance in devices]
    return lax.ppermute(block, axis, route)


def normed(head_values, gain_vector):
    mean_square = jnp.mean(head_values * head_values, axis=-1, keepdims=True)
    return head_values * lax.rsqrt(mean_square + EPSILON) * gain_vector


def rotated(head_values, doc_offsets):
    rot_width = head_values.shape[-1] // 4
    rot_half = rot_width // 2
    frequency = ROPE_THETA ** (-(jnp.arange(rot_half, dtype=jnp.float32) * 2.0 / rot_width))
    angles = doc_offsets[:, None] * frequency[None, :]
    cosine = jnp.cos(angles)[:, None, :]
    sine_part = jnp.sin(angles)[:, None, :]
    front_part = head_values[..., :rot_half]
    back_part = head_values[..., rot_half:rot_width]
    return jnp.concatenate(
        [
            front_part * cosine - back_part * sine_part,
            back_part * cosine + front_part * sine_part,
            head_values[..., rot_width:],
        ],
        axis=-1,
    )


def locate(doc_starts, positions):
    before = doc_starts[None, :] <= positions[:, None]
    doc_index = jnp.sum(before.astype(jnp.int32), axis=1)
    doc_begin = jnp.max(jnp.where(before, doc_starts[None, :], 0), axis=1)
    return (doc_index, positions - doc_begin)


def key_values(row_block, key_columns, value_columns, k_gain, doc_offsets, head_dim):
    row_count = row_block.shape[0]
    key_part = jnp.dot(row_block, key_columns, preferred_element_type=jnp.float32).reshape(
        row_count, -1, head_dim
    )
    key_part = rotated(normed(key_part, k_gain), doc_offsets).astype(jnp.bfloat16)
    value_part = jnp.dot(row_block, value_columns, preferred_element_type=jnp.float32).astype(
        jnp.bfloat16
    )
    value_part = value_part.reshape(row_count, -1, head_dim)
    return jnp.concatenate([key_part, value_part], axis=-1).reshape(row_count, -1)


def shards(
    tokens,
    q_weight,
    gate_weight,
    k_weight,
    v_weight,
    q_gain,
    k_gain,
    out_weight,
    doc_starts,
    readers,
):
    tok_rows = tokens.shape[0]
    head_dim = q_gain.shape[0]
    kv_count = k_weight.shape[1] // head_dim
    local_heads = q_weight.shape[1] // head_dim
    group_size = HEADS // kv_count
    span_blocks = readers.shape[1]
    block_index = lax.axis_index("seq")
    head_index = lax.axis_index("head")
    kv_index = head_index * local_heads // group_size
    positions = block_index * tok_rows + jnp.arange(tok_rows, dtype=jnp.int32)
    query_docs, query_offsets = locate(doc_starts, positions)
    queries = jnp.dot(tokens, q_weight, preferred_element_type=jnp.float32).reshape(
        tok_rows, local_heads, head_dim
    )
    queries = rotated(normed(queries, q_gain), query_offsets.astype(jnp.float32)).astype(
        jnp.bfloat16
    )
    gate_logits = jnp.dot(tokens, gate_weight, preferred_element_type=jnp.float32).reshape(
        tok_rows, local_heads, head_dim
    )
    key_columns = lax.dynamic_slice_in_dim(k_weight, kv_index * head_dim, head_dim, 1)
    value_columns = lax.dynamic_slice_in_dim(v_weight, kv_index * head_dim, head_dim, 1)
    own_block = key_values(
        tokens, key_columns, value_columns, k_gain, query_offsets.astype(jnp.float32), head_dim
    )
    blocks = [own_block]
    for shift_by in range(1, span_blocks + 1):
        blocks.append(passed_along(own_block, "seq", shift_by))
    block_stack = jnp.stack(blocks)
    score_scale = head_dim ** (-0.5)
    numerator = jnp.zeros((tok_rows, local_heads, head_dim), jnp.float32)
    denominator = jnp.zeros((tok_rows, local_heads), jnp.float32)
    for distance in range(span_blocks + 1):
        source = block_index - distance
        key_block = block_stack[distance]
        key_positions = source * tok_rows + jnp.arange(tok_rows, dtype=jnp.int32)
        key_docs, unused_offsets = locate(doc_starts, key_positions)
        allowed = (query_docs[:, None] == key_docs[None, :]) & (
            key_positions[None, :] <= positions[:, None]
        )

        def accumulate(totals, key_block=key_block, allowed=allowed):
            scores = (
                jnp.einsum(
                    "qhd,kd->hqk",
                    queries,
                    key_block[:, :head_dim],
                    preferred_element_type=jnp.float32,
                )
                * score_scale
            )
            weights = jnp.where(allowed[None, :, :], jnp.exp(scores), 0.0).astype(jnp.bfloat16)
            summed = jnp.einsum(
                "hqk,kd->qhd", weights, key_block[:, head_dim:], preferred_element_type=jnp.float32
            )
            return (totals[0] + summed, totals[1] + jnp.sum(weights.astype(jnp.float32), axis=-1).T)

        if distance == 0:
            numerator, denominator = accumulate((numerator, denominator))
        else:
            listed = (source >= 0) & (readers[jnp.maximum(source, 0), distance - 1] == 1)
            numerator, denominator = lax.cond(
                listed, accumulate, lambda totals: totals, (numerator, denominator)
            )
    attention = numerator / denominator[..., None]
    gated = (
        (attention * jax.nn.sigmoid(gate_logits))
        .astype(jnp.bfloat16)
        .reshape(tok_rows, local_heads * head_dim)
    )
    result = lax.psum_scatter(
        jnp.dot(gated, out_weight, preferred_element_type=jnp.float32).astype(jnp.bfloat16),
        "head",
        scatter_dimension=0,
        tiled=True,
    )
    return result


def solution(mesh):
    placed = (
        P("seq", None),
        P(None, "head"),
        P(None, "head"),
        P(),
        P(),
        P(),
        P(),
        P("head", None),
        P(),
        P(),
    )
    return jax.shard_map(
        shards, mesh=mesh, in_specs=placed, out_specs=P(("seq", "head"), None), check_vma=False
    )
```

profile of v0, /device:TPU:4, one launch (start us, length us, event | category | flops | bytes accessed | tf_op | source)
XLA Modules:
  0.0 115.2 jit_solution(16842094757745718561)
XLA Ops:
  6.5 0.0 copy-start
  6.5 0.0 reduce-scatter.2.cloned.1.call-start
  6.6 2.2 %multiply_reduce_fusion.1 = (f32[256]{0:T(256)S(1)}, f32[256,256]{1,0:T(8,128)S(1)}) fusion(bf16[256,2048]{1,0:T(8,128)(2,1)} %param.16, bf16[2048,512]{1,0:T(8,128)(2,1)} %param.19, s32[]{:T(128)S(6)} %select_n.30), kind=kOutput, calls=%fused_computation.62 | convolution fusion | flops 268566272 | bytes 2360324 | tf_op jit(solution)/shard_map/dot_general | solution.py:52
  8.8 0.0 copy-done.11
  8.9 0.1 multiply_bitcast_fusion
  9.0 0.0 copy-start.12
  9.0 0.0 copy-done.8
  9.0 0.8 convert_reduce_fusion.4
  9.9 0.0 copy-done.1
  9.9 1.7 %fusion.22 = bf16[256,1,256]{0,2,1:T(8,128)(2,1)S(1)} fusion(bf16[256,2048]{1,0:T(8,128)(2,1)S(1)} %copy-done.1, bf16[2048,512]{1,0:T(8,128)(2,1)} %param.20, s32[]{:T(128)S(6)} %select_n.30), kind=kOutput, calls=%fused_computation.47 | convolution fusion | flops 268500992 | bytes 2228228 | tf_op jit(solution)/shard_map/dot_general | solution.py:56
  11.6 0.2 fusion.34
  11.8 1.9 %collective-permute-start = (bf16[256,512]{0,1:T(8,128)(2,1)S(1)}, bf16[256,512]{0,1:T(8,128)(2,1)}, u32[]{:S(2)}, u32[]{:S(2)}) collective-permute-start(bf16[256,512]{0,1:T(8,128)(2,1)S(1)} %maximum_bitcast_fusion), channel_id=1, source_target_pairs={{0,8},{8,16},{16,24},{24,32},{32,40},{40,48},{48,56},{56,64},{64,7... | collective-permute-start | bytes 786440 | tf_op jit(solution)/shard_map/ppermute | solution.py:16
  13.7 3.1 %collective-permute-start.1 = (bf16[256,512]{0,1:T(8,128)(2,1)S(1)}, bf16[256,512]{0,1:T(8,128)(2,1)}, u32[]{:S(2)}, u32[]{:S(2)}) collective-permute-start(bf16[256,512]{0,1:T(8,128)(2,1)S(1)} %maximum_bitcast_fusion), channel_id=1, source_target_pairs={{0,16},{8,24},{16,32},{24,40},{32,48},{40,56},{48,64},{56,72},{64,... | collective-permute-start | bytes 786440 | tf_op jit(solution)/shard_map/ppermute | solution.py:16
  16.9 5.1 %collective-permute-start.2 = (bf16[256,512]{0,1:T(8,128)(2,1)S(1)}, bf16[256,512]{0,1:T(8,128)(2,1)}, u32[]{:S(2)}, u32[]{:S(2)}) collective-permute-start(bf16[256,512]{0,1:T(8,128)(2,1)S(1)} %maximum_bitcast_fusion), channel_id=1, source_target_pairs={{0,24},{8,32},{16,40},{24,48},{32,56},{40,64},{48,72},{56,80},{64,... | collective-permute-start | bytes 786440 | tf_op jit(solution)/shard_map/ppermute | solution.py:16
  22.0 1.2 %multiply_cosine_fusion = (f32[256,32]{1,0:T(8,128)}, f32[256,32]{1,0:T(8,128)}) fusion(f32[32]{0:T(128)S(1)} %negate_power_fusion, f32[256]{0:T(256)S(1)} %subtract_convert_fusion.1), kind=kLoop, calls=%fused_computation.68 | loop fusion | flops 8192 | bytes 66688 | tf_op jit(solution)/shard_map/cos | solution.py:29
  23.2 0.0 copy-done.12
  23.2 1.5 %fusion.39 = f32[256,512]{1,0:T(8,128)} fusion(bf16[256,2048]{1,0:T(8,128)(2,1)S(1)} %copy-done.1, bf16[2048,512]{1,0:T(8,128)(2,1)S(1)} %copy-done.12), kind=kOutput, calls=%fused_computation.101 | convolution fusion | flops 536870912 | bytes 3670016 | tf_op jit(solution)/shard_map/dot_general | solution.py:86
  24.7 1.4 %reshape.290 = f32[256,2,256]{2,1,0:T(2,128)S(1)} reshape(f32[256,512]{1,0:T(8,128)} %fusion.39) | data formatting | bytes 1048576 | tf_op jit(solution)/shard_map/reshape | solution.py:86
  26.2 0.3 multiply_reduce_fusion
  26.5 0.0 copy-start.6
  26.5 0.0 copy-start.7
  26.5 0.1 copy.53
  26.6 0.0 copy-done.3
  26.6 0.8 fusion.26
  27.5 0.1 slice.92
  27.6 1.1 subtract_convert_fusion
  28.7 0.2 pad_maximum_fusion
  29.0 0.0 copy-done.6
  29.0 0.0 copy-done.7
  29.0 0.9 compare_and_fusion.1
  29.9 0.3 convert_reduce_fusion.3
  30.3 0.0 copy-done.5
  30.3 0.2 convolution_bitcast_fusion.3
  30.5 0.0 copy-start.10
  30.5 0.0 copy-start.9
  30.5 2.7 %fusion.17 = f32[256,512]{1,0:T(8,128)S(1)} fusion(bf16[256,2048]{1,0:T(8,128)(2,1)} %param.16, bf16[2048,512]{1,0:T(8,128)(2,1)} %param.18), kind=kOutput, calls=%fused_computation.39 | convolution fusion | flops 537264128 | bytes 3670016 | tf_op jit(solution)/shard_map/dot_general | solution.py:92
  33.2 0.5 iota_add_fusion
  33.8 0.0 copy-done.10
  33.8 0.7 constant_dynamic-slice_fusion
  36.4 1.0 copy.70
  37.4 0.0 copy-done.9
  37.4 0.7 compare_convert_fusion.1
  38.1 0.0 collective-permute-done
  38.1 5.7 %conditional.3 = (f32[256,2,256]{2,0,1:T(8,128)S(1)}, f32[256,2]{0,1:T(2,128)S(1)}) conditional(s32[]{:T(128)} %convert_element_type.78, (f32[256,2,256]{0,2,1:T(8,128)S(1)}, f32[256,2]{0,1:T(2,128)S(1)}) %tuple.76, (pred[256,256]{0,1:T(8,128)(4,1)}, bf16[256,512]{0,1:T(8,128)(2,1)}, bf16[256,2,256]{2,0,1:T(8,128)(2,1)}, ...), branch_computations={%region_6.7_spmd, %region_7.9_spmd} | conditional | flops 135004160 | bytes 4792364 | solution.py:136
  38.1 1.1 copy.58
  39.2 0.0 copy-start.4
  39.3 2.1 %convert_reduce_fusion = (f32[2,256]{1,0:T(2,128)S(1)}, bf16[2,256,256]{1,2,0:T(8,128)(2,1)}) fusion(bf16[256,2,256]{2,0,1:T(8,128)(2,1)} %get-tuple-element.68, bf16[256,512]{1,0:T(8,128)(2,1)S(1)} %copy.58, pred[256,256]{0,1:T(8,128)(4,1)} %get-tuple-element.66), kind=kOutput, calls=%fused_computation.7 | convolution fusion | flops 67763712 | bytes 722944 | tf_op jit(solution)/shard_map/cond/branch_1_fun/qhd,kd->hqk/dot_general | solution.py:118
  41.3 0.0 copy-done.4
  41.3 1.0 copy.59
  42.3 1.5 %fusion = f32[256,2,256]{2,0,1:T(8,128)S(1)} fusion(f32[256,2,256]{2,0,1:T(8,128)} %copy.59, bf16[2,256,256]{1,2,0:T(8,128)(2,1)} %get-tuple-element.190, bf16[256,512]{1,0:T(8,128)(2,1)} %copy-done.4), kind=kOutput, calls=%fused_computation.1 | convolution fusion | flops 67239936 | bytes 1441792 | tf_op jit(solution)/shard_map/cond/branch_1_fun/hqk,kd->qhd/dot_general | solution.py:127
  43.8 0.0 collective-permute-done.1
  43.8 2.7 %conditional.4 = ((f32[256,2,256]{2,0,1:T(8,128)S(1)}, f32[256,2]{0,1:T(2,128)S(1)})) conditional(s32[]{:T(128)} %convert_element_type.77, (f32[256,2,256]{2,0,1:T(8,128)S(1)}, f32[256,2]{0,1:T(2,128)S(1)}) %conditional.3, (pred[256,256]{0,1:T(8,128)(4,1)}, bf16[256,512]{0,1:T(8,128)(2,1)}, bf16[256,2,256]{2,0,1:T(8,128)(2,1)}, ...), branch_computations={%region_10.11_spmd, %region_11.13_spmd} | conditional | flops 135004160 | bytes 2695192 | solution.py:136
  43.8 1.1 copy.60
  44.9 1.3 %convert_reduce_fusion.1 = (f32[2,256]{1,0:T(2,128)S(1)}, bf16[2,256,256]{1,2,0:T(8,128)(2,1)S(1)}) fusion(bf16[256,2,256]{2,0,1:T(8,128)(2,1)} %get-tuple-element.73, bf16[256,512]{1,0:T(8,128)(2,1)S(1)} %copy.60, pred[256,256]{0,1:T(8,128)(4,1)} %get-tuple-element.71), kind=kOutput, calls=%fused_computation.18 | convolution fusion | flops 67763712 | bytes 722944 | tf_op jit(solution)/shard_map/cond/branch_1_fun/qhd,kd->hqk/dot_general | solution.py:118
  46.2 0.3 fusion.5
  46.5 0.0 collective-permute-done.2
  46.5 0.7 le.49
  47.3 1.0 conditional.5
  47.3 1.0 copy.71
  48.3 0.0 copy-done.2
  48.3 1.1 multiply_convert_fusion
  49.5 1.7 %convolution_convert_fusion = bf16[256,2048]{1,0:T(8,128)(2,1)} fusion(bf16[256,512]{0,1:T(8,128)(2,1)S(1)} %bitcast.116, bf16[512,2048]{1,0:T(8,128)(2,1)S(1)} %copy-done), kind=kOutput, calls=%fused_computation.35 | convolution fusion | flops 537395200 | bytes 3407872 | tf_op jit(solution)/shard_map/dot_general | solution.py:146
  51.2 0.0 reduce-scatter.2.cloned.1.call-update
  51.2 57.2 %reduce-scatter.2.cloned.1.call-done = bf16[32,2048]{1,0:T(8,128)(2,1)} async-done(((bf16[256,2048]{1,0:T(8,128)(2,1)}), bf16[32,2048]{1,0:T(8,128)(2,1)}) %reduce-scatter.2.cloned.1.call-update) | async-done | bytes 131088 | tf_op jit(solution)/shard_map/reduce_scatter | solution.py:145
  (19 shorter events, 0.1 us)
Async XLA Ops:
  6.5 42.9 %copy-start = (bf16[512,2048]{1,0:T(8,128)(2,1)S(1)}, bf16[512,2048]{1,0:T(8,128)(2,1)}, u32[]{:S(2)}) copy-start(bf16[512,2048]{1,0:T(8,128)(2,1)} %param.23) | copy-start | bytes 6291460
  6.5 3.3 %copy-start.1 = (bf16[256,2048]{1,0:T(8,128)(2,1)S(1)}, bf16[256,2048]{1,0:T(8,128)(2,1)}, u32[]{:S(2)}) copy-start(bf16[256,2048]{1,0:T(8,128)(2,1)} %param.16) | copy-start | bytes 3145732
  6.5 2.3 %copy-start.11 = (f32[256]{0:T(256)S(1)}, f32[256]{0:T(256)}, u32[]{:S(2)}) copy-start(f32[256]{0:T(256)} %param.22) | copy-start | bytes 3076
  6.5 2.5 %copy-start.8 = (s32[48]{0:T(128)S(1)}, s32[48]{0:T(128)}, u32[]{:S(2)}) copy-start(s32[48]{0:T(128)} %param.24) | copy-start | bytes 580
  6.5 101.8 %reduce-scatter.2.cloned.1.call-start = ((), (), s32[]{:S(2)}) async-start(), calls=%async_computation.1 | async-start | bytes 1179648 | tf_op jit(solution)/shard_map/reduce_scatter | solution.py:145
  9.0 14.2 %copy-start.12 = (bf16[2048,512]{1,0:T(8,128)(2,1)S(1)}, bf16[2048,512]{1,0:T(8,128)(2,1)}, u32[]{:S(2)}) copy-start(bf16[2048,512]{1,0:T(8,128)(2,1)} %param.17) | copy-start | bytes 6291460
  11.8 26.3 %collective-permute-start = (bf16[256,512]{0,1:T(8,128)(2,1)S(1)}, bf16[256,512]{0,1:T(8,128)(2,1)}, u32[]{:S(2)}, u32[]{:S(2)}) collective-permute-start(bf16[256,512]{0,1:T(8,128)(2,1)S(1)} %maximum_bitcast_fusion), channel_id=1, source_target_pairs={{0,8},{8,16},{16,24},{24,32},{32,40},{40,48},{48,56},{56,64},{64,7... | collective-permute-start | bytes 786440 | tf_op jit(solution)/shard_map/ppermute | solution.py:16
  13.7 30.1 %collective-permute-start.1 = (bf16[256,512]{0,1:T(8,128)(2,1)S(1)}, bf16[256,512]{0,1:T(8,128)(2,1)}, u32[]{:S(2)}, u32[]{:S(2)}) collective-permute-start(bf16[256,512]{0,1:T(8,128)(2,1)S(1)} %maximum_bitcast_fusion), channel_id=1, source_target_pairs={{0,16},{8,24},{16,32},{24,40},{32,48},{40,56},{48,64},{56,72},{64,... | collective-permute-start | bytes 786440 | tf_op jit(solution)/shard_map/ppermute | solution.py:16
  16.9 29.6 %collective-permute-start.2 = (bf16[256,512]{0,1:T(8,128)(2,1)S(1)}, bf16[256,512]{0,1:T(8,128)(2,1)}, u32[]{:S(2)}, u32[]{:S(2)}) collective-permute-start(bf16[256,512]{0,1:T(8,128)(2,1)S(1)} %maximum_bitcast_fusion), channel_id=1, source_target_pairs={{0,24},{8,32},{16,40},{24,48},{32,56},{40,64},{48,72},{56,80},{64,... | collective-permute-start | bytes 786440 | tf_op jit(solution)/shard_map/ppermute | solution.py:16
  24.7 1.9 %copy-start.3 = (f32[256,512]{1,0:T(8,128)S(1)}, f32[256,512]{1,0:T(8,128)}, u32[]{:S(2)}) copy-start(f32[256,512]{1,0:T(8,128)} %fusion.39) | copy-start | bytes 1572868
  26.5 2.5 %copy-start.6 = (s32[256]{0:T(256)S(1)}, s32[256]{0:T(256)}, u32[]{:S(2)}) copy-start(s32[256]{0:T(256)} %get-tuple-element.185) | copy-start | bytes 3076
  26.5 2.5 %copy-start.7 = (s32[256]{0:T(256)S(1)}, s32[256]{0:T(256)}, u32[]{:S(2)}) copy-start(s32[256]{0:T(256)} %get-tuple-element.186) | copy-start | bytes 3076
  29.0 1.3 %copy-start.5 = (bf16[256,2,256]{2,0,1:T(8,128)(2,1)}, bf16[256,2,256]{2,0,1:T(8,128)(2,1)S(1)}, u32[]{:S(2)}) copy-start(bf16[256,2,256]{2,0,1:T(8,128)(2,1)S(1)} %pad_maximum_fusion) | copy-start | bytes 786436
  30.5 3.3 %copy-start.10 = (s32[96,3]{0,1:T(4,128)S(1)}, s32[96,3]{0,1:T(4,128)}, u32[]{:S(2)}) copy-start(s32[96,3]{0,1:T(4,128)} %param.25) | copy-start | bytes 3460
  30.5 6.9 %copy-start.9 = (s32[48]{0:T(128)S(1)}, s32[48]{0:T(128)}, u32[]{:S(2)}) copy-start(s32[48]{0:T(128)} %param.24) | copy-start | bytes 580
  39.2 2.1 %copy-start.4 = (bf16[256,512]{1,0:T(8,128)(2,1)}, bf16[256,512]{1,0:T(8,128)(2,1)S(1)}, u32[]{:S(2)}) copy-start(bf16[256,512]{1,0:T(8,128)(2,1)S(1)} %copy.58) | copy-start | bytes 786436 | tf_op jit(solution)/shard_map/cond
  47.3 1.0 copy-start.2
Sparse Core Ops, SparseCore 0:
  51.3 57.0 reduce-scatter.1
where the time goes:
time: 116 us; the launch traced here: 115 us
  waiting for transfers between devices  57.2 us (49%)
  between operations  15.7 us (14%)
  matrix products  15.4 us (13%)
  starting transfers between devices  10.2 us (9%)
  local copies, waits for them, and re-layouts  8.35 us (7%)
  other arithmetic  8.28 us (7%)
    reduce_scatter x1, waiting for transfers between devices, shards(): lax.psum_scatter(jnp.dot(gated, out_weight, preferred_element_type=jnp.fl...  57.2 us
    ppermute x3, starting transfers between devices, passed_along(): return lax.ppermute(block, axis, route)  10.1 us
    dot_general x3, matrix products, accumulate(): jnp.einsum('qhd,kd->hqk', queries, key_block[:, :head_dim], preferred_ele...  3.68 us
    another operation x3, local copies, waits for them, and re-layouts  3.18 us
    dot_general x1, matrix products, shards(): jnp.dot(tokens, gate_weight, preferred_element_type=jnp.float32)  2.71 us
  transfers between devices with their start and end apart: 4, of which 1 were waited for; matrix products, arithmetic and copies ran while one was open for 19% of the time, Pallas kernels for 0%

commit v1 on v0

v1 whole, which is shorter than its diff:
```python
import functools

import jax
import jax.numpy as jnp
import numpy as np
from jax import lax
from jax.experimental import pallas as pl
from jax.experimental.pallas import tpu as pltpu
from jax.sharding import PartitionSpec as P

HEADS = 16
ROPE_THETA = 10000000.0
EPSILON = 1e-06

F32 = jnp.float32
BF16 = jnp.bfloat16
ANY = pl.BlockSpec(memory_space=pl.ANY)
VMEM = pl.BlockSpec(memory_space=pltpu.VMEM)
SMEM = pl.BlockSpec(memory_space=pltpu.SMEM)


def params(mib):
    return pltpu.CompilerParams(vmem_limit_bytes=mib << 20)


def cost(flops, nbytes, trans=0):
    return pl.CostEstimate(flops=flops, bytes_accessed=nbytes, transcendentals=trans)


def rope_rows(head_dim):
    rot_width = head_dim // 4
    half = rot_width // 2
    frequency = ROPE_THETA ** (-(np.arange(half, dtype=np.float64) * 2.0 / rot_width))
    rows = np.zeros((8, 128), np.float32)
    rows[0, :half] = frequency
    rows[0, half:rot_width] = frequency
    rows[1, :half] = -1.0
    rows[1, half:rot_width] = 1.0
    return rows


def doc_begin(starts, rows, base):
    at = base + lax.broadcasted_iota(jnp.int32, (rows, starts.shape[1]), 0)
    return jnp.max(jnp.where(starts <= at, starts, 0), axis=1, keepdims=True)


def normed_rotated(x, gain, cosine, sine, half):
    square = jnp.mean(x * x, axis=-1, keepdims=True)
    x = x * lax.rsqrt(square + EPSILON) * gain
    front = x[:, :128]
    lane = lax.broadcasted_iota(jnp.int32, front.shape, 1)
    partner = jnp.where(
        lane < half, pltpu.roll(front, 128 - half, 1), pltpu.roll(front, half, 1)
    )
    return front * cosine + partner * sine, x[:, 128:]


def kv_body(head_dim, kv_share, starts, rope, gain, tok_in, kw_in, vw_in, kv, trig, tok, kw, vw, sems):
    rows = tok.shape[0]
    column = pl.multiple_of((lax.axis_index("head") // kv_share) * head_dim, head_dim)
    columns = pl.ds(column, head_dim)
    copies = [
        pltpu.make_async_copy(tok_in, tok, sems.at[0]),
        pltpu.make_async_copy(kw_in.at[:, columns], kw, sems.at[1]),
        pltpu.make_async_copy(vw_in.at[:, columns], vw, sems.at[2]),
    ]
    for c in copies:
        c.start()
    base = lax.axis_index("seq") * rows
    begin = doc_begin(starts[...], rows, base)
    offset = (base + lax.broadcasted_iota(jnp.int32, (rows, 1), 0) - begin).astype(F32)
    angle = offset * rope[0:1, :]
    cosine = jnp.cos(angle)
    sine = jnp.sin(angle) * rope[1:2, :]
    trig[:, :128] = cosine
    trig[:, 128:] = sine
    copies[0].wait()
    copies[1].wait()
    key = jnp.dot(tok[...], kw[...], preferred_element_type=F32)
    front, back = normed_rotated(key, gain[...], cosine, sine, head_dim // 8)
    kv[:, :128] = front.astype(BF16)
    kv[:, 128:head_dim] = back.astype(BF16)
    copies[2].wait()
    kv[:, head_dim:] = jnp.dot(tok[...], vw[...], preferred_element_type=F32).astype(BF16)


def attend(query, key, value, keep, scale):
    scores = lax.dot_general(query, key, (((1,), (1,)), ((), ())), preferred_element_type=F32)
    weights = jnp.where(keep, jnp.exp(scores * scale), 0.0).astype(BF16)
    wide = weights.astype(F32)
    half = wide.shape[1] // 2
    return (
        jnp.dot(weights, value, preferred_element_type=F32),
        wide[:, :half] + wide[:, half:],
    )


def kept(rows, width, query_base, key_base, begin):
    at = query_base + lax.broadcasted_iota(jnp.int32, (rows, width), 0)
    key = key_base + lax.broadcasted_iota(jnp.int32, (rows, width), 1)
    return (key <= at) & (key >= begin)


def q_body(head_dim, starts, gain, trig, kv, tok_in, qw_in, gw_in, q_out, gate, num, den, tok, w, sems):
    rows = tok.shape[0]
    heads = qw_in.shape[1] // head_dim
    token_copy = pltpu.make_async_copy(tok_in, tok, sems.at[2 * heads])
    token_copy.start()
    copies = []
    for i in range(2 * heads):
        source = qw_in if i < heads else gw_in
        columns = pl.ds((i % heads) * head_dim, head_dim)
        copies.append(pltpu.make_async_copy(source.at[:, columns], w.at[i], sems.at[i]))
        copies[i].start()
    base = lax.axis_index("seq") * rows
    begin = doc_begin(starts[...], rows, base)
    keep = kept(rows, rows, base, base, begin)
    token_copy.wait()
    for i in range(heads):
        at = pl.ds(i * rows, rows)
        copies[i].wait()
        query = jnp.dot(tok[...], w[i], preferred_element_type=F32)
        front, back = normed_rotated(query, gain[...], trig[:, :128], trig[:, 128:], head_dim // 8)
        q_out[at, :128] = front.astype(BF16)
        q_out[at, 128:] = back.astype(BF16)
        weighted, sums = attend(
            q_out[at, :], kv[:, :head_dim], kv[:, head_dim:], keep, head_dim ** (-0.5)
        )
        num[at, :] = weighted
        den[at, :] = sums
    for i in range(heads):
        copies[heads + i].wait()
        logits = jnp.dot(tok[...], w[heads + i], preferred_element_type=F32)
        gate[pl.ds(i * rows, rows), :] = 1.0 / (1.0 + jnp.exp(-logits))


def out_body(head_dim, starts, readers, query, gate, num, den, near, far, own, ow, parts, gated, turned):
    heads = query.shape[0] // head_dim
    rows = query.shape[0] // heads
    block = lax.axis_index("seq")
    core = lax.rem(block, 2)
    head = lax.axis_index("head")
    base = block * rows
    begin = doc_begin(starts[...], rows, base)
    chip = block - core

    def mask(source):
        distance = block - source
        inside = (source >= 0) & (distance >= 1) & (distance <= readers.shape[0])
        listed = readers[
            jnp.clip(distance - 1, 0, readers.shape[0] - 1), jnp.maximum(source, 0)
        ]
        first = jnp.where(inside & (listed == 1), 0, 1 << 30)
        return kept(rows, rows, base, source * rows, jnp.maximum(begin, first))

    def add(block_ref, keep):
        for i in range(heads):
            at = pl.ds(i * rows, rows)
            weighted, sums = attend(
                query[at, :],
                block_ref[:, :head_dim],
                block_ref[:, head_dim:],
                keep,
                head_dim ** (-0.5),
            )
            num[at, :] += weighted
            den[at, :] += sums

    add(near, mask(chip - 2 + core))
    add(far, mask(chip - 1 - core))

    @pl.when(core == 1)
    def _():
        add(own, mask(block - 1))

    for i in range(heads):
        at = pl.ds(i * rows, rows)
        total = jnp.sum(den[at, :], axis=1, keepdims=True)
        gated[:, i * head_dim : (i + 1) * head_dim] = (num[at, :] / total * gate[at, :]).astype(BF16)
    count = 8
    piece = rows // count
    for i, step in enumerate(ORDER):
        source = lax.rem(head + jnp.where(core == 0, step, count - step), count)
        turned[i * piece : (i + 1) * piece, :] = gated[
            pl.ds(pl.multiple_of(source * piece, piece), piece), :
        ]
    parts[...] = jnp.dot(turned[...], ow[...], preferred_element_type=F32).astype(BF16)


ORDER = (2, 4, 6, 7, 1, 3, 5, 0)


def second_body(parts, got, a, b, c):
    piece = a.shape[0]
    for i, out in enumerate((a, b, c)):
        mine = parts[(4 + i) * piece : (5 + i) * piece, :].astype(F32)
        out[...] = (mine + got[i * piece : (i + 1) * piece, :].astype(F32)).astype(BF16)


def last_body(parts, a, b, c, d, out):
    piece = out.shape[0]
    total = parts[7 * piece :, :].astype(F32)
    for ref in (a, b, c, d):
        total = total + ref[...].astype(F32)
    out[...] = total.astype(BF16)


def shards(
    tokens,
    q_weight,
    gate_weight,
    k_weight,
    v_weight,
    q_gain,
    k_gain,
    out_weight,
    doc_starts,
    readers,
):
    rows, width = tokens.shape
    head_dim = q_gain.shape[0]
    heads = q_weight.shape[1] // head_dim
    kv_count = k_weight.shape[1] // head_dim
    kv_share = lax.axis_size("head") // kv_count
    seq, head = lax.axis_size("seq"), lax.axis_size("head")
    starts = doc_starts.reshape(1, -1)
    rope = jnp.asarray(rope_rows(head_dim))
    stacked = heads * rows

    def shape(r, c, dtype=BF16):
        return jax.ShapeDtypeStruct((r, c), dtype)

    own, trig = pl.pallas_call(
        functools.partial(kv_body, head_dim, kv_share),
        out_shape=(shape(rows, 2 * head_dim), shape(rows, 256, F32)),
        in_specs=[VMEM, VMEM, VMEM, ANY, ANY, ANY],
        out_specs=(VMEM, VMEM),
        scratch_shapes=[
            pltpu.VMEM((rows, width), BF16),
            pltpu.VMEM((width, head_dim), BF16),
            pltpu.VMEM((width, head_dim), BF16),
            pltpu.SemaphoreType.DMA((3,)),
        ],
        compiler_params=params(16),
        cost_estimate=cost(4 * rows * width * head_dim, 3 << 20),
        name="kv",
    )(starts, rope, k_gain.reshape(1, -1), tokens, k_weight, v_weight)

    near = lax.ppermute(own, "seq", [(i, (i + 2) % seq) for i in range(seq)])
    below = lax.ppermute(own, "seq", [(i, i ^ 1) for i in range(seq)])

    query, gate, num, den = pl.pallas_call(
        functools.partial(q_body, head_dim),
        out_shape=(
            shape(stacked, head_dim),
            shape(stacked, head_dim, F32),
            shape(stacked, head_dim, F32),
            shape(stacked, 128, F32),
        ),
        in_specs=[VMEM, VMEM, VMEM, VMEM, ANY, ANY, ANY],
        out_specs=(VMEM,) * 4,
        scratch_shapes=[
            pltpu.VMEM((rows, width), BF16),
            pltpu.VMEM((2 * heads, width, head_dim), BF16),
            pltpu.SemaphoreType.DMA((2 * heads + 1,)),
        ],
        compiler_params=params(20),
        cost_estimate=cost(4 * rows * width * heads * head_dim, 5 << 20),
        name="query",
    )(starts, q_gain.reshape(1, -1), trig, own, tokens, q_weight, gate_weight)

    far = lax.ppermute(near, "seq", [(i, i ^ 1) for i in range(seq)])

    parts = pl.pallas_call(
        functools.partial(out_body, head_dim),
        out_shape=shape(rows, width),
        in_specs=[VMEM, SMEM] + [VMEM] * 8,
        out_specs=VMEM,
        scratch_shapes=[
            pltpu.VMEM((rows, heads * head_dim), BF16),
            pltpu.VMEM((rows, heads * head_dim), BF16),
        ],
        compiler_params=params(20),
        cost_estimate=cost(2 * rows * width * heads * head_dim, 4 << 20),
        name="attend",
    )(starts, readers.T, query, gate, num, den, near, far, below, out_weight)

    def turn(block, step):
        route = []
        for s in range(seq):
            for h in range(head):
                to = (h + step) % head if s % 2 == 0 else (h - step) % head
                route.append((s * head + h, s * head + to))
        return lax.ppermute(block, ("seq", "head"), route)

    piece = rows // head
    got = turn(parts[: 3 * piece], 1)
    d = turn(parts[3 * piece : 4 * piece], -1)
    a, b, c = pl.pallas_call(
        second_body,
        out_shape=(shape(piece, width),) * 3,
        in_specs=[VMEM, VMEM],
        out_specs=(VMEM,) * 3,
        compiler_params=params(8),
        name="second",
    )(parts, got)
    b = turn(b, 3)
    c = turn(c, -3)
    a = turn(a, 1)
    return pl.pallas_call(
        last_body,
        out_shape=shape(piece, width),
        in_specs=[VMEM] * 5,
        out_specs=VMEM,
        compiler_params=params(8),
        name="last",
    )(parts, a, b, c, d)


def solution(mesh):
    placed = (
        P("seq", None),
        P(None, "head"),
        P(None, "head"),
        P(),
        P(),
        P(),
        P(),
        P("head", None),
        P(),
        P(),
    )
    return jax.shard_map(
        shards, mesh=mesh, in_specs=placed, out_specs=P(("seq", "head"), None), check_vma=False
    )
```

time: 116 us -> 74.8 us (0.64)
  the two profiles are of different devices: /device:TPU:4 before, /device:TPU:1 now
where the time goes in v1:
time: 74.8 us; the launch traced here: 73.6 us
  starting transfers between devices  36.6 us (49%)
  waiting for transfers between devices  19.9 us (27%)
  Pallas kernels  10.4 us (14%)
  local copies, waits for them, and re-layouts  6.49 us (9%)
    ppermute x5, starting transfers between devices, turn(): return lax.ppermute(block, ('seq', 'head'), route)  19.1 us
    ppermute x5, waiting for transfers between devices, turn(): return lax.ppermute(block, ('seq', 'head'), route)  10.9 us
    ppermute x1, starting transfers between devices, shards(): below = lax.ppermute(own, 'seq', [(i, i ^ 1) for i in range(seq)])  10.4 us
    ppermute x1, waiting for transfers between devices, shards(): near = lax.ppermute(own, 'seq', [(i, (i + 2) % seq) for i in range(seq)])  9 us
    unnamed x26, local copies, waits for them, and re-layouts  6.46 us
    pallas_call x1, Pallas kernels, shards(): pl.pallas_call(functools.partial(q_body, head_dim), out_shape=(shape(stac...  4.25 us
    ppermute x1, starting transfers between devices, shards(): near = lax.ppermute(own, 'seq', [(i, (i + 2) % seq) for i in range(seq)])  3.94 us
    ppermute x1, starting transfers between devices, shards(): far = lax.ppermute(near, 'seq', [(i, i ^ 1) for i in range(seq)])  3.15 us
  transfers between devices with their start and end apart: 8, of which 4 were waited for; matrix products, arithmetic and copies ran while one was open for 0% of the time, Pallas kernels for 6%

profile of v1, /device:TPU:1, one launch (start us, length us, event | category | flops | bytes accessed | tf_op | source)
XLA Modules:
  0.0 73.6 jit_solution(4983306155086445653)
XLA Ops:
  0.0 0.0 copy-start
  0.0 1.2 %copy-done = bf16[256,2048]{1,0:T(8,128)(2,1)S(1)} copy-done((bf16[256,2048]{1,0:T(8,128)(2,1)S(1)}, bf16[256,2048]{1,0:T(8,128)(2,1)}, u32[]{:S(2)}) %copy-start) | copy-done | bytes 1048600
  1.2 0.0 copy-start.5
  1.2 1.6 %copy-done.5 = bf16[2048,512]{1,0:T(8,128)(2,1)S(1)} copy-done((bf16[2048,512]{1,0:T(8,128)(2,1)S(1)}, bf16[2048,512]{1,0:T(8,128)(2,1)}, u32[]{:S(2)}) %copy-start.5) | copy-done | bytes 2097176
  2.8 0.0 copy-start.6
  2.8 1.6 %copy-done.6 = bf16[2048,512]{1,0:T(8,128)(2,1)S(1)} copy-done((bf16[2048,512]{1,0:T(8,128)(2,1)S(1)}, bf16[2048,512]{1,0:T(8,128)(2,1)}, u32[]{:S(2)}) %copy-start.6) | copy-done | bytes 2097176
  4.4 0.0 copy-start.7
  4.4 0.7 copy-done.7
  5.1 0.0 copy-start.9
  5.1 0.7 copy-done.9
  5.8 0.0 copy-start.12
  5.8 0.7 copy-done.12
  6.4 0.0 copy-start.1
  6.4 0.0 copy-start.2
  6.4 0.0 copy-start.3
  6.4 0.0 copy-start.8
  6.4 0.0 copy-start.11
  6.5 2.5 %kv.1 = (bf16[256,512]{1,0:T(8,128)(2,1)S(1)}, f32[256,256]{1,0:T(8,128)S(1)}) custom-call(s32[1,48]{1,0:T(1,128)S(1)} %bitcast.4, f32[8,128]{1,0:T(8,128)S(1)} %copy-done.9, f32[1,256]{1,0:T(1,128)S(1)} %bitcast.9, bf16[256,2048]{1,0:T(8,128)(2,1)S(1)} %copy-done, bf16[2048,512]{1,0:T(8,128)(2,1)S(1)} %copy-done.5, bf16[2048,512]{1,0:T(8,128)(2,1)S(1)} %copy-done.6), custom_call_target="tpu_custom_call" | custom-call | flops 536870912 | bytes 3145728 | tf_op jit(solution)/shard_map/kv/pallas_call | solution.py:233
  8.9 3.9 %collective-permute-start = (bf16[256,512]{1,0:T(8,128)(2,1)S(1)}, bf16[256,512]{1,0:T(8,128)(2,1)S(1)}, u32[]{:S(2)}, u32[]{:S(2)}) collective-permute-start(bf16[256,512]{1,0:T(8,128)(2,1)S(1)} %get-tuple-element.15.kv), channel_id=1, source_target_pairs={{0,16},{8,24},{16,32},{24,40},{32,48},{40,56},{48,64},{56,72},{64,... | collective-permute-start | bytes 786440 | tf_op jit(solution)/shard_map/ppermute | solution.py:249
  12.9 10.4 %collective-permute-start.2 = (bf16[256,512]{1,0:T(8,128)(2,1)S(1)}, bf16[256,512]{1,0:T(8,128)(2,1)S(1)}, u32[]{:S(2)}, u32[]{:S(2)}) collective-permute-start(bf16[256,512]{1,0:T(8,128)(2,1)S(1)} %get-tuple-element.15.kv), channel_id=1, source_target_pairs={{0,8},{8,0},{16,24},{24,16},{32,40},{40,32},{48,56},{56,48},{64,72... | collective-permute-start | bytes 786440 | tf_op jit(solution)/shard_map/ppermute | solution.py:250
  23.3 9.0 %collective-permute-done.near = bf16[256,512]{1,0:T(8,128)(2,1)S(1)} collective-permute-done((bf16[256,512]{1,0:T(8,128)(2,1)S(1)}, bf16[256,512]{1,0:T(8,128)(2,1)S(1)}, u32[]{:S(2)}, u32[]{:S(2)}) %collective-permute-start) | collective-permute-done | bytes 262176 | tf_op jit(solution)/shard_map/ppermute | solution.py:249
  32.3 3.1 %collective-permute-start.1 = (bf16[256,512]{1,0:T(8,128)(2,1)S(1)}, bf16[256,512]{1,0:T(8,128)(2,1)S(1)}, u32[]{:S(2)}, u32[]{:S(2)}) collective-permute-start(bf16[256,512]{1,0:T(8,128)(2,1)S(1)} %collective-permute-done.near), channel_id=1, source_target_pairs={{0,8},{8,0},{16,24},{24,16},{32,40},{40,32},{48,56},{56,48},{64,72... | collective-permute-start | bytes 786440 | tf_op jit(solution)/shard_map/ppermute | solution.py:272
  35.4 0.0 copy-done.1
  35.4 0.0 copy-done.2
  35.4 0.0 copy-done.3
  35.4 0.0 copy-done.8
  35.4 0.0 copy-done.11
  35.5 0.0 copy-start.4
  35.5 0.0 copy-start.10
  35.5 4.3 %query.1 = (bf16[512,256]{1,0:T(8,128)(2,1)S(1)}, f32[512,256]{1,0:T(8,128)S(1)}, f32[512,256]{1,0:T(8,128)S(1)}, f32[512,128]{1,0:T(8,128)S(1)}) custom-call(s32[1,48]{1,0:T(1,128)S(1)} %bitcast.5, f32[1,256]{1,0:T(1,128)S(1)} %bitcast.8, f32[256,256]{1,0:T(8,128)S(1)} %get-tuple-element.14.trig, bf16[256,512]{1,0:T(8,128)(2,1)S(1)} %get-tuple-element.15.kv, ...), custom_call_target="tpu_custom_call" | custom-call | flops 1073741824 | bytes 5242880 | tf_op jit(solution)/shard_map/query/pallas_call | solution.py:252
  39.7 0.0 collective-permute-done.2.own
  39.8 0.0 collective-permute-done.1.far
  39.8 0.0 copy-done.4
  39.8 0.0 copy-done.10
  39.8 2.8 %attend.1.parts = bf16[256,2048]{1,0:T(8,128)(2,1)S(1)} custom-call(s32[1,48]{1,0:T(1,128)S(1)} %bitcast.6, s32[3,96]{1,0:T(4,128)S(1)} %bitcast.7, bf16[512,256]{1,0:T(8,128)(2,1)S(1)} %get-tuple-element.16.query, f32[512,256]{1,0:T(8,128)S(1)} %get-tuple-element.17.gate, f32[512,256]{1,0:T(8,128)S(1)} %get-tuple-element.18.num, ...), custom_call_target="tpu_custom_call" | custom-call | flops 536870912 | bytes 4194304 | tf_op jit(solution)/shard_map/attend/pallas_call | solution.py:274
  42.7 5.1 %collective-permute-start.3 = (bf16[96,2048]{1,0:T(8,128)(2,1)S(1)}, bf16[96,2048]{1,0:T(8,128)(2,1)S(1)}, u32[]{:S(2)}, u32[]{:S(2)}) collective-permute-start(bf16[96,2048]{1,0:T(8,128)(2,1)S(1)} %slice.8), channel_id=1, source_target_pairs={{0,1},{1,2},{2,3},{3,4},{4,5},{5,6},{6,7},{7,0},{8,15},{9,8},{10,9... | collective-permute-start | bytes 1179656 | tf_op jit(solution)/shard_map/ppermute | solution.py:294
  47.8 1.9 %collective-permute-start.7 = (bf16[32,2048]{1,0:T(8,128)(2,1)S(1)}, bf16[32,2048]{1,0:T(8,128)(2,1)S(1)}, u32[]{:S(2)}, u32[]{:S(2)}) collective-permute-start(bf16[32,2048]{1,0:T(8,128)(2,1)S(1)} %slice.9), channel_id=1, source_target_pairs={{0,7},{1,0},{2,1},{3,2},{4,3},{5,4},{6,5},{7,6},{8,9},{9,10},{10,1... | collective-permute-start | bytes 393224 | tf_op jit(solution)/shard_map/ppermute | solution.py:294
  49.7 4.2 %collective-permute-done.3.got = bf16[96,2048]{1,0:T(8,128)(2,1)S(1)} collective-permute-done((bf16[96,2048]{1,0:T(8,128)(2,1)S(1)}, bf16[96,2048]{1,0:T(8,128)(2,1)S(1)}, u32[]{:S(2)}, u32[]{:S(2)}) %collective-permute-start.3) | collective-permute-done | bytes 393248 | tf_op jit(solution)/shard_map/ppermute | solution.py:294
  53.9 0.1 second.1
  54.0 5.0 %collective-permute-start.4 = (bf16[32,2048]{1,0:T(8,128)(2,1)S(1)}, bf16[32,2048]{1,0:T(8,128)(2,1)S(1)}, u32[]{:S(2)}, u32[]{:S(2)}) collective-permute-start(bf16[32,2048]{1,0:T(8,128)(2,1)S(1)} %get-tuple-element.20), channel_id=1, source_target_pairs={{0,1},{1,2},{2,3},{3,4},{4,5},{5,6},{6,7},{7,0},{8,15},{9,8},{10,9... | collective-permute-start | bytes 393224 | tf_op jit(solution)/shard_map/ppermute | solution.py:294
  59.0 3.6 %collective-permute-start.5 = (bf16[32,2048]{1,0:T(8,128)(2,1)S(1)}, bf16[32,2048]{1,0:T(8,128)(2,1)S(1)}, u32[]{:S(2)}, u32[]{:S(2)}) collective-permute-start(bf16[32,2048]{1,0:T(8,128)(2,1)S(1)} %get-tuple-element.21), channel_id=1, source_target_pairs={{0,3},{1,4},{2,5},{3,6},{4,7},{5,0},{6,1},{7,2},{8,13},{9,14},{10,... | collective-permute-start | bytes 393224 | tf_op jit(solution)/shard_map/ppermute | solution.py:294
  62.7 3.4 %collective-permute-start.6 = (bf16[32,2048]{1,0:T(8,128)(2,1)S(1)}, bf16[32,2048]{1,0:T(8,128)(2,1)S(1)}, u32[]{:S(2)}, u32[]{:S(2)}) collective-permute-start(bf16[32,2048]{1,0:T(8,128)(2,1)S(1)} %get-tuple-element.22), channel_id=1, source_target_pairs={{0,5},{1,6},{2,7},{3,0},{4,1},{5,2},{6,3},{7,4},{8,11},{9,12},{10,... | collective-permute-start | bytes 393224 | tf_op jit(solution)/shard_map/ppermute | solution.py:294
  66.1 0.0 collective-permute-done.7.d
  66.1 0.0 collective-permute-done.4.a
  66.1 2.7 %collective-permute-done.5.b = bf16[32,2048]{1,0:T(8,128)(2,1)S(1)} collective-permute-done((bf16[32,2048]{1,0:T(8,128)(2,1)S(1)}, bf16[32,2048]{1,0:T(8,128)(2,1)S(1)}, u32[]{:S(2)}, u32[]{:S(2)}) %collective-permute-start.5) | collective-permute-done | bytes 131104 | tf_op jit(solution)/shard_map/ppermute | solution.py:294
  68.8 4.0 %collective-permute-done.6.c = bf16[32,2048]{1,0:T(8,128)(2,1)S(1)} collective-permute-done((bf16[32,2048]{1,0:T(8,128)(2,1)S(1)}, bf16[32,2048]{1,0:T(8,128)(2,1)S(1)}, u32[]{:S(2)}, u32[]{:S(2)}) %collective-permute-start.6) | collective-permute-done | bytes 131104 | tf_op jit(solution)/shard_map/ppermute | solution.py:294
  72.9 0.7 %last.1 = bf16[32,2048]{1,0:T(8,128)(2,1)} custom-call(bf16[256,2048]{1,0:T(8,128)(2,1)S(1)} %attend.1.parts, bf16[32,2048]{1,0:T(8,128)(2,1)S(1)} %collective-permute-done.4.a, bf16[32,2048]{1,0:T(8,128)(2,1)S(1)} %collective-permute-done.5.b, bf16[32,2048]{1,0:T(8,128)(2,1)S(1)} %collective-permute-done.6.c, bf16[32,2048]{1,0:T(8,128)(2,1)S(1)} %collective-permute-done.7.d), custom_call_target="tpu_custom_call" | custom-call | tf_op jit(solution)/shard_map/last/pallas_call | solution.py:310
  (2 shorter events, 0.0 us)
Async XLA Ops:
  0.0 1.2 %copy-start = (bf16[256,2048]{1,0:T(8,128)(2,1)S(1)}, bf16[256,2048]{1,0:T(8,128)(2,1)}, u32[]{:S(2)}) copy-start(bf16[256,2048]{1,0:T(8,128)(2,1)} %tok_in.3) | copy-start | bytes 3145732
  1.2 1.6 %copy-start.5 = (bf16[2048,512]{1,0:T(8,128)(2,1)S(1)}, bf16[2048,512]{1,0:T(8,128)(2,1)}, u32[]{:S(2)}) copy-start(bf16[2048,512]{1,0:T(8,128)(2,1)} %kw_in.1) | copy-start | bytes 6291460
  2.8 1.6 %copy-start.6 = (bf16[2048,512]{1,0:T(8,128)(2,1)S(1)}, bf16[2048,512]{1,0:T(8,128)(2,1)}, u32[]{:S(2)}) copy-start(bf16[2048,512]{1,0:T(8,128)(2,1)} %vw_in.1) | copy-start | bytes 6291460
  4.4 0.7 copy-start.7
  5.1 0.7 copy-start.9
  5.8 0.7 copy-start.12
  6.4 29.0 %copy-start.1 = (bf16[256,2048]{1,0:T(8,128)(2,1)S(1)}, bf16[256,2048]{1,0:T(8,128)(2,1)}, u32[]{:S(2)}) copy-start(bf16[256,2048]{1,0:T(8,128)(2,1)} %tok_in.3) | copy-start | bytes 3145732
  6.4 29.0 %copy-start.2 = (bf16[2048,512]{1,0:T(8,128)(2,1)S(1)}, bf16[2048,512]{1,0:T(8,128)(2,1)}, u32[]{:S(2)}) copy-start(bf16[2048,512]{1,0:T(8,128)(2,1)} %qw_in.1) | copy-start | bytes 6291460
  6.4 29.0 %copy-start.3 = (bf16[2048,512]{1,0:T(8,128)(2,1)S(1)}, bf16[2048,512]{1,0:T(8,128)(2,1)}, u32[]{:S(2)}) copy-start(bf16[2048,512]{1,0:T(8,128)(2,1)} %gw_in.1) | copy-start | bytes 6291460
  6.4 29.0 %copy-start.8 = (s32[48]{0:T(128)S(1)}, s32[48]{0:T(128)}, u32[]{:S(2)}) copy-start(s32[48]{0:T(128)} %param.19) | copy-start | bytes 580
  6.4 29.0 %copy-start.11 = (f32[256]{0:T(256)S(1)}, f32[256]{0:T(256)}, u32[]{:S(2)}) copy-start(f32[256]{0:T(256)} %param.16) | copy-start | bytes 3076
  8.9 23.3 %collective-permute-start = (bf16[256,512]{1,0:T(8,128)(2,1)S(1)}, bf16[256,512]{1,0:T(8,128)(2,1)S(1)}, u32[]{:S(2)}, u32[]{:S(2)}) collective-permute-start(bf16[256,512]{1,0:T(8,128)(2,1)S(1)} %get-tuple-element.15.kv), channel_id=1, source_target_pairs={{0,16},{8,24},{16,32},{24,40},{32,48},{40,56},{48,64},{56,72},{64,... | collective-permute-start | bytes 786440 | tf_op jit(solution)/shard_map/ppermute | solution.py:249
  12.9 26.9 %collective-permute-start.2 = (bf16[256,512]{1,0:T(8,128)(2,1)S(1)}, bf16[256,512]{1,0:T(8,128)(2,1)S(1)}, u32[]{:S(2)}, u32[]{:S(2)}) collective-permute-start(bf16[256,512]{1,0:T(8,128)(2,1)S(1)} %get-tuple-element.15.kv), channel_id=1, source_target_pairs={{0,8},{8,0},{16,24},{24,16},{32,40},{40,32},{48,56},{56,48},{64,72... | collective-permute-start | bytes 786440 | tf_op jit(solution)/shard_map/ppermute | solution.py:250
  32.3 7.5 %collective-permute-start.1 = (bf16[256,512]{1,0:T(8,128)(2,1)S(1)}, bf16[256,512]{1,0:T(8,128)(2,1)S(1)}, u32[]{:S(2)}, u32[]{:S(2)}) collective-permute-start(bf16[256,512]{1,0:T(8,128)(2,1)S(1)} %collective-permute-done.near), channel_id=1, source_target_pairs={{0,8},{8,0},{16,24},{24,16},{32,40},{40,32},{48,56},{56,48},{64,72... | collective-permute-start | bytes 786440 | tf_op jit(solution)/shard_map/ppermute | solution.py:272
  35.5 4.3 %copy-start.4 = (bf16[512,2048]{1,0:T(8,128)(2,1)S(1)}, bf16[512,2048]{1,0:T(8,128)(2,1)}, u32[]{:S(2)}) copy-start(bf16[512,2048]{1,0:T(8,128)(2,1)} %ow.1) | copy-start | bytes 6291460
  35.5 4.3 %copy-start.10 = (s32[96,3]{0,1:T(4,128)S(1)}, s32[96,3]{0,1:T(4,128)}, u32[]{:S(2)}) copy-start(s32[96,3]{0,1:T(4,128)} %param.20) | copy-start | bytes 3460
  42.7 11.2 %collective-permute-start.3 = (bf16[96,2048]{1,0:T(8,128)(2,1)S(1)}, bf16[96,2048]{1,0:T(8,128)(2,1)S(1)}, u32[]{:S(2)}, u32[]{:S(2)}) collective-permute-start(bf16[96,2048]{1,0:T(8,128)(2,1)S(1)} %slice.8), channel_id=1, source_target_pairs={{0,1},{1,2},{2,3},{3,4},{4,5},{5,6},{6,7},{7,0},{8,15},{9,8},{10,9... | collective-permute-start | bytes 1179656 | tf_op jit(solution)/shard_map/ppermute | solution.py:294
  47.8 18.3 %collective-permute-start.7 = (bf16[32,2048]{1,0:T(8,128)(2,1)S(1)}, bf16[32,2048]{1,0:T(8,128)(2,1)S(1)}, u32[]{:S(2)}, u32[]{:S(2)}) collective-permute-start(bf16[32,2048]{1,0:T(8,128)(2,1)S(1)} %slice.9), channel_id=1, source_target_pairs={{0,7},{1,0},{2,1},{3,2},{4,3},{5,4},{6,5},{7,6},{8,9},{9,10},{10,1... | collective-permute-start | bytes 393224 | tf_op jit(solution)/shard_map/ppermute | solution.py:294
  54.0 12.1 %collective-permute-start.4 = (bf16[32,2048]{1,0:T(8,128)(2,1)S(1)}, bf16[32,2048]{1,0:T(8,128)(2,1)S(1)}, u32[]{:S(2)}, u32[]{:S(2)}) collective-permute-start(bf16[32,2048]{1,0:T(8,128)(2,1)S(1)} %get-tuple-element.20), channel_id=1, source_target_pairs={{0,1},{1,2},{2,3},{3,4},{4,5},{5,6},{6,7},{7,0},{8,15},{9,8},{10,9... | collective-permute-start | bytes 393224 | tf_op jit(solution)/shard_map/ppermute | solution.py:294
  59.0 9.8 %collective-permute-start.5 = (bf16[32,2048]{1,0:T(8,128)(2,1)S(1)}, bf16[32,2048]{1,0:T(8,128)(2,1)S(1)}, u32[]{:S(2)}, u32[]{:S(2)}) collective-permute-start(bf16[32,2048]{1,0:T(8,128)(2,1)S(1)} %get-tuple-element.21), channel_id=1, source_target_pairs={{0,3},{1,4},{2,5},{3,6},{4,7},{5,0},{6,1},{7,2},{8,13},{9,14},{10,... | collective-permute-start | bytes 393224 | tf_op jit(solution)/shard_map/ppermute | solution.py:294
  62.7 10.2 %collective-permute-start.6 = (bf16[32,2048]{1,0:T(8,128)(2,1)S(1)}, bf16[32,2048]{1,0:T(8,128)(2,1)S(1)}, u32[]{:S(2)}, u32[]{:S(2)}) collective-permute-start(bf16[32,2048]{1,0:T(8,128)(2,1)S(1)} %get-tuple-element.22), channel_id=1, source_target_pairs={{0,5},{1,6},{2,7},{3,0},{4,1},{5,2},{6,3},{7,4},{8,11},{9,12},{10,... | collective-permute-start | bytes 393224 | tf_op jit(solution)/shard_map/ppermute | solution.py:294

commit v2 on v1

v2 whole, which is shorter than its diff:
```python
import functools
import math

import jax
import jax.numpy as jnp
from jax import lax
from jax.experimental import pallas as pl
from jax.experimental.pallas import tpu as pltpu
from jax.sharding import PartitionSpec as P

HEADS = 16
ROPE_THETA = 10000000.0
EPSILON = 1e-06

F32 = jnp.float32
BF16 = jnp.bfloat16
HBM = pl.BlockSpec(memory_space=pltpu.HBM)
VMEM = pl.BlockSpec(memory_space=pltpu.VMEM)
SMEM = pl.BlockSpec(memory_space=pltpu.SMEM)


def params(mib):
    return pltpu.CompilerParams(vmem_limit_bytes=int(mib * (1 << 20)))


def cost(flops, nbytes, trans=0):
    return pl.CostEstimate(flops=flops, bytes_accessed=nbytes, transcendentals=trans)


def rope_angles(offset, head_dim):
    rot_width = head_dim // 4
    half = rot_width // 2
    lane = lax.broadcasted_iota(jnp.int32, (1, 128), 1)
    exponent = lax.rem(lane, half).astype(F32) * (-math.log(ROPE_THETA) * 2.0 / rot_width)
    frequency = jnp.where(lane < rot_width, jnp.exp(exponent), 0.0)
    angle = offset * frequency
    return jnp.cos(angle), jnp.sin(angle) * jnp.where(lane < half, -1.0, 1.0)


def doc_begin(starts, rows, base):
    at = base + lax.broadcasted_iota(jnp.int32, (rows, starts.shape[1]), 0)
    return jnp.max(jnp.where(starts <= at, starts, 0), axis=1, keepdims=True)


def normed_rotated(x, gain, cosine, sine, half):
    square = jnp.mean(x * x, axis=-1, keepdims=True)
    x = x * lax.rsqrt(square + EPSILON) * gain
    front = x[:, :128]
    lane = lax.broadcasted_iota(jnp.int32, front.shape, 1)
    partner = jnp.where(
        lane < half, pltpu.roll(front, 128 - half, 1), pltpu.roll(front, half, 1)
    )
    return front * cosine + partner * sine, x[:, 128:]


def kv_body(head_dim, kv_share, starts_in, gain_in, tok_in, kw_in, vw_in, kv, trig, starts, gain, tok, kw, vw, sems):
    rows = tok.shape[0]
    column = pl.multiple_of((lax.axis_index("head") // kv_share) * head_dim, head_dim)
    columns = pl.ds(column, head_dim)
    copies = [
        pltpu.make_async_copy(source, target, sems.at[i])
        for i, (source, target) in enumerate(
            (
                (starts_in, starts),
                (gain_in, gain),
                (tok_in, tok),
                (kw_in.at[:, columns], kw),
                (vw_in.at[:, columns], vw),
            )
        )
    ]
    for c in copies:
        c.start()
    base = lax.axis_index("seq") * rows
    copies[0].wait()
    begin = doc_begin(starts[...], rows, base)
    offset = (base + lax.broadcasted_iota(jnp.int32, (rows, 1), 0) - begin).astype(F32)
    cosine, sine = rope_angles(offset, head_dim)
    trig[:, :128] = cosine
    trig[:, 128:] = sine
    for c in copies[1:]:
        c.wait()
    key = jnp.dot(tok[...], kw[...], preferred_element_type=F32)
    kv[:, head_dim:] = jnp.dot(tok[...], vw[...], preferred_element_type=F32).astype(BF16)
    front, back = normed_rotated(key, gain[...], trig[:, :128], trig[:, 128:], head_dim // 8)
    kv[:, :128] = front.astype(BF16)
    kv[:, 128:head_dim] = back.astype(BF16)


def attend(query, key, value, keep, scale):
    scores = lax.dot_general(query, key, (((1,), (1,)), ((), ())), preferred_element_type=F32)
    weights = jnp.where(keep, jnp.exp(scores * scale), 0.0).astype(BF16)
    wide = weights.astype(F32)
    half = wide.shape[1] // 2
    return (
        jnp.dot(weights, value, preferred_element_type=F32),
        wide[:, :half] + wide[:, half:],
    )


def kept(rows, width, query_base, key_base, begin):
    at = query_base + lax.broadcasted_iota(jnp.int32, (rows, width), 0)
    key = key_base + lax.broadcasted_iota(jnp.int32, (rows, width), 1)
    return (key <= at) & (key >= begin)


def q_body(head_dim, starts_in, gain_in, trig, kv, tok_in, qw_in, gw_in, q_out, gate, num, den, starts, gain, tok, w, sems):
    rows = tok.shape[0]
    heads = qw_in.shape[1] // head_dim
    pairs = [(starts_in, starts), (gain_in, gain), (tok_in, tok)]
    small = len(pairs)
    for i in range(heads):
        columns = pl.ds(i * head_dim, head_dim)
        pairs.append((qw_in.at[:, columns], w.at[2 * i]))
        pairs.append((gw_in.at[:, columns], w.at[2 * i + 1]))
    copies = [
        pltpu.make_async_copy(source, target, sems.at[i])
        for i, (source, target) in enumerate(pairs)
    ]
    for c in copies:
        c.start()
    base = lax.axis_index("seq") * rows
    copies[0].wait()
    begin = doc_begin(starts[...], rows, base)
    keep = kept(rows, rows, base, base, begin)
    for c in copies[1:small]:
        c.wait()
    for i in range(heads):
        at = pl.ds(i * rows, rows)
        copies[small + 2 * i].wait()
        query = jnp.dot(tok[...], w[2 * i], preferred_element_type=F32)
        front, back = normed_rotated(query, gain[...], trig[:, :128], trig[:, 128:], head_dim // 8)
        q_out[at, :128] = front.astype(BF16)
        q_out[at, 128:] = back.astype(BF16)
        copies[small + 2 * i + 1].wait()
        logits = jnp.dot(tok[...], w[2 * i + 1], preferred_element_type=F32)
        gate[at, :] = 1.0 / (1.0 + jnp.exp(-logits))
        weighted, sums = attend(
            q_out[at, :], kv[:, :head_dim], kv[:, head_dim:], keep, head_dim ** (-0.5)
        )
        num[at, :] = weighted
        den[at, :] = sums


def out_body(head_dim, starts, readers, query, gate, num, den, near, far, own, ow, part_a, part_b, part_c, part_d, gated, turned):
    heads = query.shape[0] // head_dim
    rows = query.shape[0] // heads
    block = lax.axis_index("seq")
    core = lax.rem(block, 2)
    head = lax.axis_index("head")
    base = block * rows
    begin = doc_begin(starts[...], rows, base)
    chip = block - core

    def mask(source):
        distance = block - source
        inside = (source >= 0) & (distance >= 1) & (distance <= readers.shape[0])
        listed = readers[
            jnp.clip(distance - 1, 0, readers.shape[0] - 1), jnp.maximum(source, 0)
        ]
        first = jnp.where(inside & (listed == 1), 0, 1 << 30)
        return kept(rows, rows, base, source * rows, jnp.maximum(begin, first))

    def add(block_ref, keep):
        for i in range(heads):
            at = pl.ds(i * rows, rows)
            weighted, sums = attend(
                query[at, :],
                block_ref[:, :head_dim],
                block_ref[:, head_dim:],
                keep,
                head_dim ** (-0.5),
            )
            num[at, :] += weighted
            den[at, :] += sums

    add(near, mask(chip - 2 + core))
    add(far, mask(chip - 1 - core))

    @pl.when(core == 1)
    def _():
        add(own, mask(block - 1))

    for i in range(heads):
        at = pl.ds(i * rows, rows)
        total = jnp.sum(den[at, :], axis=1, keepdims=True)
        gated[:, i * head_dim : (i + 1) * head_dim] = (num[at, :] / total * gate[at, :]).astype(BF16)
    count = 8
    piece = rows // count
    for i, step in enumerate(ORDER):
        source = lax.rem(head + jnp.where(core == 0, step, count - step), count)
        turned[i * piece : (i + 1) * piece, :] = gated[
            pl.ds(pl.multiple_of(source * piece, piece), piece), :
        ]
    result = jnp.dot(turned[...], ow[...], preferred_element_type=F32).astype(BF16)
    at = 0
    for ref in (part_a, part_b, part_c, part_d):
        ref[...] = result[at : at + ref.shape[0], :]
        at += ref.shape[0]


ORDER = (1, 3, 7, 5, 4, 2, 6, 0)


def second_body(rest, got_a, got_b, got_c, forward, backward):
    piece = forward.shape[0]
    total = rest[:piece, :].astype(F32) + got_a[piece:, :].astype(F32) + got_c[...].astype(F32)
    forward[...] = total.astype(BF16)
    total = rest[piece : 2 * piece, :].astype(F32) + got_b[piece:, :].astype(F32)
    backward[...] = total.astype(BF16)


def last_body(rest, got_a, got_b, forward, backward, out):
    piece = out.shape[0]
    total = rest[2 * piece :, :].astype(F32)
    for ref in (got_a, got_b, forward, backward):
        total = total + ref[:piece, :].astype(F32)
    out[...] = total.astype(BF16)


def shards(
    tokens,
    q_weight,
    gate_weight,
    k_weight,
    v_weight,
    q_gain,
    k_gain,
    out_weight,
    doc_starts,
    readers,
):
    rows, width = tokens.shape
    head_dim = q_gain.shape[0]
    heads = q_weight.shape[1] // head_dim
    kv_count = k_weight.shape[1] // head_dim
    kv_share = lax.axis_size("head") // kv_count
    seq, head = lax.axis_size("seq"), lax.axis_size("head")
    starts = doc_starts.reshape(1, -1)
    stacked = heads * rows

    def shape(r, c, dtype=BF16):
        return jax.ShapeDtypeStruct((r, c), dtype)

    def held(r, c, dtype=BF16):
        return pltpu.VMEM((r, c), dtype)

    def far_away(*arrays):
        return tuple(pltpu.with_memory_space_constraint(x, pltpu.HBM) for x in arrays)

    own, trig = pl.pallas_call(
        functools.partial(kv_body, head_dim, kv_share),
        out_shape=(held(rows, 2 * head_dim), held(rows, 256, F32)),
        in_specs=[HBM] * 5,
        out_specs=(VMEM, VMEM),
        scratch_shapes=[
            pltpu.VMEM(starts.shape, jnp.int32),
            pltpu.VMEM((1, head_dim), F32),
            pltpu.VMEM((rows, width), BF16),
            pltpu.VMEM((width, head_dim), BF16),
            pltpu.VMEM((width, head_dim), BF16),
            pltpu.SemaphoreType.DMA((5,)),
        ],
        compiler_params=params(16),
        cost_estimate=cost(4 * rows * width * head_dim, 3 << 20),
        name="kv",
    )(*far_away(starts, k_gain.reshape(1, -1), tokens, k_weight, v_weight))

    near = lax.ppermute(own, "seq", [(i, i + 2) for i in range(seq - 2)])
    below = lax.ppermute(own, "seq", [(i, i ^ 1) for i in range(seq)])

    query, gate, num, den = pl.pallas_call(
        functools.partial(q_body, head_dim),
        out_shape=(
            held(stacked, head_dim),
            held(stacked, head_dim, F32),
            held(stacked, head_dim, F32),
            held(stacked, 128, F32),
        ),
        in_specs=[HBM] * 2 + [VMEM] * 2 + [HBM] * 3,
        out_specs=(VMEM,) * 4,
        scratch_shapes=[
            pltpu.VMEM(starts.shape, jnp.int32),
            pltpu.VMEM((1, head_dim), F32),
            pltpu.VMEM((rows, width), BF16),
            pltpu.VMEM((2 * heads, width, head_dim), BF16),
            pltpu.SemaphoreType.DMA((3 + 2 * heads,)),
        ],
        compiler_params=params(24),
        cost_estimate=cost(4 * rows * width * heads * head_dim, 5 << 20),
        name="query",
    )(*far_away(starts, q_gain.reshape(1, -1)), trig, own, *far_away(tokens, q_weight, gate_weight))

    near, query = lax.optimization_barrier((near, query))
    far = lax.ppermute(near, "seq", [(i, i ^ 1) for i in range(seq)])

    piece = rows // head
    part_a, part_b, part_c, rest = pl.pallas_call(
        functools.partial(out_body, head_dim),
        out_shape=tuple(shape(n * piece, width) for n in (2, 2, 1, 3)),
        in_specs=[VMEM, SMEM] + [VMEM] * 8,
        out_specs=(VMEM,) * 4,
        scratch_shapes=[
            pltpu.VMEM((rows, heads * head_dim), BF16),
            pltpu.VMEM((rows, heads * head_dim), BF16),
        ],
        compiler_params=params(20),
        cost_estimate=cost(2 * rows * width * heads * head_dim, 4 << 20),
        name="attend",
    )(starts, readers.T, query, gate, num, den, near, far, below, out_weight)

    def turn(block, step):
        route = []
        for s in range(seq):
            for h in range(head):
                to = (h + step) % head if s % 2 == 0 else (h - step) % head
                route.append((s * head + h, s * head + to))
        return lax.ppermute(block, ("seq", "head"), route)

    got_c = turn(part_c, 2)
    got_a = turn(part_a, 1)
    got_b = turn(part_b, -1)
    forward, backward = pl.pallas_call(
        second_body,
        out_shape=(shape(piece, width),) * 2,
        in_specs=[VMEM] * 4,
        out_specs=(VMEM,) * 2,
        compiler_params=params(8),
        name="second",
    )(rest, got_a, got_b, got_c)
    forward = turn(forward, 2)
    backward = turn(backward, -2)
    return pl.pallas_call(
        last_body,
        out_shape=shape(piece, width),
        in_specs=[VMEM] * 5,
        out_specs=VMEM,
        compiler_params=params(8),
        name="last",
    )(rest, got_a, got_b, forward, backward)


def solution(mesh):
    placed = (
        P("seq", None),
        P(None, "head"),
        P(None, "head"),
        P(),
        P(),
        P(),
        P(),
        P("head", None),
        P(),
        P(),
    )
    return jax.shard_map(
        shards, mesh=mesh, in_specs=placed, out_specs=P(("seq", "head"), None), check_vma=False
    )
```

time: 74.8 us -> 57.1 us (0.76); the launches traced: 73.6 us -> 56.8 us
  starting transfers between devices: 36.6 us -> 29.2 us
  local copies, waits for them, and re-layouts: 6.49 us -> 0.02 us
  waiting for transfers between devices: 19.9 us -> 15.9 us
  Pallas kernels: 10.4 us -> 11.5 us
    ppermute x1, waiting for transfers between devices: 9 us -> 0.01 us  [shards(): near = lax.ppermute(own, 'seq', [(i, i + 2) for i in range(seq - 2)])]
    unnamed x26 -> x6, local copies, waits for them, and re-layouts: 6.46 us -> 0.02 us
    ppermute x5, starting transfers between devices: 19.1 us -> 13.6 us  [turn(): return lax.ppermute(block, ('seq', 'head'), route)]
    ppermute x5, waiting for transfers between devices: 10.9 us -> 14.4 us  [turn(): return lax.ppermute(block, ('seq', 'head'), route)]
    ppermute x1, waiting for transfers between devices: 0.01 us -> 1.49 us  [shards(): far = lax.ppermute(near, 'seq', [(i, i ^ 1) for i in range(seq)])]
    ppermute x1, starting transfers between devices: 3.15 us -> 1.92 us  [shards(): far = lax.ppermute(near, 'seq', [(i, i ^ 1) for i in range(seq)])]
  transfers between devices with their start and end apart: 8 -> 8, of which waited for: 4 -> 4; matrix products, arithmetic and copies ran while one was open for 0% -> 0% of each run, Pallas kernels for 6% -> 9%
where the time goes in v2:
time: 57.1 us; the launch traced here: 56.8 us
  starting transfers between devices  29.2 us (51%)
  waiting for transfers between devices  15.9 us (28%)
  Pallas kernels  11.5 us (20%)
    ppermute x5, waiting for transfers between devices, turn(): return lax.ppermute(block, ('seq', 'head'), route)  14.4 us
    ppermute x5, starting transfers between devices, turn(): return lax.ppermute(block, ('seq', 'head'), route)  13.6 us
    ppermute x1, starting transfers between devices, shards(): below = lax.ppermute(own, 'seq', [(i, i ^ 1) for i in range(seq)])  9.74 us
    pallas_call x1, Pallas kernels, shards(): pl.pallas_call(functools.partial(q_body, head_dim), out_shape=(held(stack...  5.01 us
    ppermute x1, starting transfers between devices, shards(): near = lax.ppermute(own, 'seq', [(i, i + 2) for i in range(seq - 2)])  3.95 us
    pallas_call x1, Pallas kernels, shards(): pl.pallas_call(functools.partial(out_body, head_dim), out_shape=tuple((sh...  2.84 us
    pallas_call x1, Pallas kernels, shards(): pl.pallas_call(functools.partial(kv_body, head_dim, kv_share), out_shape=...  2.8 us
    ppermute x1, starting transfers between devices, shards(): far = lax.ppermute(near, 'seq', [(i, i ^ 1) for i in range(seq)])  1.92 us
  transfers between devices with their start and end apart: 8, of which 4 were waited for; matrix products, arithmetic and copies ran while one was open for 0% of the time, Pallas kernels for 9%

profile of v2, /device:TPU:1, one launch (start us, length us, event | category | flops | bytes accessed | tf_op | source)
XLA Modules:
  0.0 56.8 jit_solution(14029585437221699831)
XLA Ops:
  0.0 2.8 %kv.1 = (bf16[256,512]{1,0:T(8,128)(2,1)S(1)}, f32[256,256]{1,0:T(8,128)S(1)}) custom-call(s32[1,48]{1,0:T(1,128)} %bitcast.4, f32[1,256]{1,0:T(1,128)} %bitcast.8, bf16[256,2048]{1,0:T(8,128)(2,1)} %tok_in.3, bf16[2048,512]{1,0:T(8,128)(2,1)} %kw_in.1, bf16[2048,512]{1,0:T(8,128)(2,1)} %vw_in.1), custom_call_target="tpu_custom_call" | custom-call | flops 536870912 | bytes 3145728 | tf_op jit(solution)/shard_map/kv/pallas_call | solution.py:251
  2.8 4.0 %collective-permute-start = (bf16[256,512]{1,0:T(8,128)(2,1)S(1)}, bf16[256,512]{1,0:T(8,128)(2,1)S(1)}, u32[]{:S(2)}, u32[]{:S(2)}) collective-permute-start(bf16[256,512]{1,0:T(8,128)(2,1)S(1)} %get-tuple-element.19.kv), channel_id=1, source_target_pairs={{0,16},{8,24},{16,32},{24,40},{32,48},{40,56},{48,64},{56,72},{64,... | collective-permute-start | bytes 786440 | tf_op jit(solution)/shard_map/ppermute | solution.py:269
  6.8 9.7 %collective-permute-start.2 = (bf16[256,512]{1,0:T(8,128)(2,1)S(1)}, bf16[256,512]{1,0:T(8,128)(2,1)S(1)}, u32[]{:S(2)}, u32[]{:S(2)}) collective-permute-start(bf16[256,512]{1,0:T(8,128)(2,1)S(1)} %get-tuple-element.19.kv), channel_id=1, source_target_pairs={{0,8},{8,0},{16,24},{24,16},{32,40},{40,32},{48,56},{56,48},{64,72... | collective-permute-start | bytes 786440 | tf_op jit(solution)/shard_map/ppermute | solution.py:270
  16.5 0.0 copy-start
  16.5 0.0 copy-start.1
  16.5 0.0 copy-start.2
  16.6 5.0 %query.1 = (bf16[512,256]{1,0:T(8,128)(2,1)S(1)}, f32[512,256]{1,0:T(8,128)S(1)}, f32[512,256]{1,0:T(8,128)S(1)}, f32[512,128]{1,0:T(8,128)S(1)}) custom-call(s32[1,48]{1,0:T(1,128)} %bitcast.5, f32[1,256]{1,0:T(1,128)} %bitcast.9, f32[256,256]{1,0:T(8,128)S(1)} %get-tuple-element.20.trig, bf16[256,512]{1,0:T(8,128)(2,1)S(1)} %get-tuple-element.19.kv, ...), custom_call_target="tpu_custom_call" | custom-call | flops 1073741824 | bytes 5242880 | tf_op jit(solution)/shard_map/query/pallas_call | solution.py:272
  21.6 0.0 collective-permute-done.near
  21.6 1.9 %collective-permute-start.1 = (bf16[256,512]{1,0:T(8,128)(2,1)S(1)}, bf16[256,512]{1,0:T(8,128)(2,1)S(1)}, u32[]{:S(2)}, u32[]{:S(2)}) collective-permute-start(bf16[256,512]{1,0:T(8,128)(2,1)S(1)} %collective-permute-done.near), channel_id=1, source_target_pairs={{0,8},{8,0},{16,24},{24,16},{32,40},{40,32},{48,56},{56,48},{64,72... | collective-permute-start | bytes 786440 | tf_op jit(solution)/shard_map/ppermute | solution.py:295
  23.5 0.0 collective-permute-done.2.own
  23.5 1.5 %collective-permute-done.1.far = bf16[256,512]{1,0:T(8,128)(2,1)S(1)} collective-permute-done((bf16[256,512]{1,0:T(8,128)(2,1)S(1)}, bf16[256,512]{1,0:T(8,128)(2,1)S(1)}, u32[]{:S(2)}, u32[]{:S(2)}) %collective-permute-start.1) | collective-permute-done | bytes 262176 | tf_op jit(solution)/shard_map/ppermute | solution.py:295
  25.0 0.0 copy-done
  25.0 0.0 copy-done.1
  25.0 0.0 copy-done.2
  25.0 2.8 %attend.1 = (bf16[64,2048]{1,0:T(8,128)(2,1)S(1)}, bf16[64,2048]{1,0:T(8,128)(2,1)S(1)}, bf16[32,2048]{1,0:T(8,128)(2,1)S(1)}, bf16[96,2048]{1,0:T(8,128)(2,1)S(1)}) custom-call(s32[1,48]{1,0:T(1,128)S(1)} %bitcast.6, s32[3,96]{1,0:T(4,128)S(1)} %bitcast.7, bf16[512,256]{1,0:T(8,128)(2,1)S(1)} %get-tuple-element.22.query, ...), custom_call_target="tpu_custom_call" | custom-call | flops 536870912 | bytes 4194304 | tf_op jit(solution)/shard_map/attend/pallas_call | solution.py:298
  27.9 1.9 %collective-permute-start.3 = (bf16[64,2048]{1,0:T(8,128)(2,1)S(1)}, bf16[64,2048]{1,0:T(8,128)(2,1)S(1)}, u32[]{:S(2)}, u32[]{:S(2)}) collective-permute-start(bf16[64,2048]{1,0:T(8,128)(2,1)S(1)} %get-tuple-element.28), channel_id=1, source_target_pairs={{0,1},{1,2},{2,3},{3,4},{4,5},{5,6},{6,7},{7,0},{8,15},{9,8},{10,9... | collective-permute-start | bytes 786440 | tf_op jit(solution)/shard_map/ppermute | solution.py:318
  29.8 3.4 %collective-permute-start.4 = (bf16[64,2048]{1,0:T(8,128)(2,1)S(1)}, bf16[64,2048]{1,0:T(8,128)(2,1)S(1)}, u32[]{:S(2)}, u32[]{:S(2)}) collective-permute-start(bf16[64,2048]{1,0:T(8,128)(2,1)S(1)} %get-tuple-element.29), channel_id=1, source_target_pairs={{0,7},{1,0},{2,1},{3,2},{4,3},{5,4},{6,5},{7,6},{8,9},{9,10},{10,1... | collective-permute-start | bytes 786440 | tf_op jit(solution)/shard_map/ppermute | solution.py:318
  33.2 1.9 %collective-permute-start.5 = (bf16[32,2048]{1,0:T(8,128)(2,1)S(1)}, bf16[32,2048]{1,0:T(8,128)(2,1)S(1)}, u32[]{:S(2)}, u32[]{:S(2)}) collective-permute-start(bf16[32,2048]{1,0:T(8,128)(2,1)S(1)} %get-tuple-element.30), channel_id=1, source_target_pairs={{0,2},{1,3},{2,4},{3,5},{4,6},{5,7},{6,0},{7,1},{8,14},{9,15},{10,... | collective-permute-start | bytes 393224 | tf_op jit(solution)/shard_map/ppermute | solution.py:318
  35.1 5.9 %collective-permute-done.5.got_c = bf16[32,2048]{1,0:T(8,128)(2,1)S(1)} collective-permute-done((bf16[32,2048]{1,0:T(8,128)(2,1)S(1)}, bf16[32,2048]{1,0:T(8,128)(2,1)S(1)}, u32[]{:S(2)}, u32[]{:S(2)}) %collective-permute-start.5) | collective-permute-done | bytes 131104 | tf_op jit(solution)/shard_map/ppermute | solution.py:318
  41.0 0.0 collective-permute-done.3.got_a
  41.0 0.0 collective-permute-done.4.got_b
  41.0 0.1 second.1
  41.1 4.5 %collective-permute-start.6 = (bf16[32,2048]{1,0:T(8,128)(2,1)S(1)}, bf16[32,2048]{1,0:T(8,128)(2,1)S(1)}, u32[]{:S(2)}, u32[]{:S(2)}) collective-permute-start(bf16[32,2048]{1,0:T(8,128)(2,1)S(1)} %get-tuple-element.31), channel_id=1, source_target_pairs={{0,2},{1,3},{2,4},{3,5},{4,6},{5,7},{6,0},{7,1},{8,14},{9,15},{10,... | collective-permute-start | bytes 393224 | tf_op jit(solution)/shard_map/ppermute | solution.py:318
  45.6 1.9 %collective-permute-start.7 = (bf16[32,2048]{1,0:T(8,128)(2,1)S(1)}, bf16[32,2048]{1,0:T(8,128)(2,1)S(1)}, u32[]{:S(2)}, u32[]{:S(2)}) collective-permute-start(bf16[32,2048]{1,0:T(8,128)(2,1)S(1)} %get-tuple-element.32), channel_id=1, source_target_pairs={{0,6},{1,7},{2,0},{3,1},{4,2},{5,3},{6,4},{7,5},{8,10},{9,11},{10,... | collective-permute-start | bytes 393224 | tf_op jit(solution)/shard_map/ppermute | solution.py:318
  47.5 1.4 %collective-permute-done.6.forward = bf16[32,2048]{1,0:T(8,128)(2,1)S(1)} collective-permute-done((bf16[32,2048]{1,0:T(8,128)(2,1)S(1)}, bf16[32,2048]{1,0:T(8,128)(2,1)S(1)}, u32[]{:S(2)}, u32[]{:S(2)}) %collective-permute-start.6) | collective-permute-done | bytes 131104 | tf_op jit(solution)/shard_map/ppermute | solution.py:318
  48.9 7.1 %collective-permute-done.7.backward = bf16[32,2048]{1,0:T(8,128)(2,1)S(1)} collective-permute-done((bf16[32,2048]{1,0:T(8,128)(2,1)S(1)}, bf16[32,2048]{1,0:T(8,128)(2,1)S(1)}, u32[]{:S(2)}, u32[]{:S(2)}) %collective-permute-start.7) | collective-permute-done | bytes 131104 | tf_op jit(solution)/shard_map/ppermute | solution.py:318
  56.0 0.7 %last.1 = bf16[32,2048]{1,0:T(8,128)(2,1)} custom-call(bf16[96,2048]{1,0:T(8,128)(2,1)S(1)} %get-tuple-element.27.rest, bf16[64,2048]{1,0:T(8,128)(2,1)S(1)} %collective-permute-done.3.got_a, bf16[64,2048]{1,0:T(8,128)(2,1)S(1)} %collective-permute-done.4.got_b, bf16[32,2048]{1,0:T(8,128)(2,1)S(1)} %collective-permute-done.6.forward, ...), custom_call_target="tpu_custom_call" | custom-call | tf_op jit(solution)/shard_map/last/pallas_call | solution.py:333
Async XLA Ops:
  2.8 18.8 %collective-permute-start = (bf16[256,512]{1,0:T(8,128)(2,1)S(1)}, bf16[256,512]{1,0:T(8,128)(2,1)S(1)}, u32[]{:S(2)}, u32[]{:S(2)}) collective-permute-start(bf16[256,512]{1,0:T(8,128)(2,1)S(1)} %get-tuple-element.19.kv), channel_id=1, source_target_pairs={{0,16},{8,24},{16,32},{24,40},{32,48},{40,56},{48,64},{56,72},{64,... | collective-permute-start | bytes 786440 | tf_op jit(solution)/shard_map/ppermute | solution.py:269
  6.8 16.7 %collective-permute-start.2 = (bf16[256,512]{1,0:T(8,128)(2,1)S(1)}, bf16[256,512]{1,0:T(8,128)(2,1)S(1)}, u32[]{:S(2)}, u32[]{:S(2)}) collective-permute-start(bf16[256,512]{1,0:T(8,128)(2,1)S(1)} %get-tuple-element.19.kv), channel_id=1, source_target_pairs={{0,8},{8,0},{16,24},{24,16},{32,40},{40,32},{48,56},{56,48},{64,72... | collective-permute-start | bytes 786440 | tf_op jit(solution)/shard_map/ppermute | solution.py:270
  16.5 8.5 %copy-start = (bf16[512,2048]{1,0:T(8,128)(2,1)S(1)}, bf16[512,2048]{1,0:T(8,128)(2,1)}, u32[]{:S(2)}) copy-start(bf16[512,2048]{1,0:T(8,128)(2,1)} %ow.1) | copy-start | bytes 6291460
  16.5 8.5 %copy-start.1 = (s32[48]{0:T(128)S(1)}, s32[48]{0:T(128)}, u32[]{:S(2)}) copy-start(s32[48]{0:T(128)} %param.18) | copy-start | bytes 580
  16.5 8.5 %copy-start.2 = (s32[96,3]{0,1:T(4,128)S(1)}, s32[96,3]{0,1:T(4,128)}, u32[]{:S(2)}) copy-start(s32[96,3]{0,1:T(4,128)} %param.19) | copy-start | bytes 3460
  21.6 3.4 %collective-permute-start.1 = (bf16[256,512]{1,0:T(8,128)(2,1)S(1)}, bf16[256,512]{1,0:T(8,128)(2,1)S(1)}, u32[]{:S(2)}, u32[]{:S(2)}) collective-permute-start(bf16[256,512]{1,0:T(8,128)(2,1)S(1)} %collective-permute-done.near), channel_id=1, source_target_pairs={{0,8},{8,0},{16,24},{24,16},{32,40},{40,32},{48,56},{56,48},{64,72... | collective-permute-start | bytes 786440 | tf_op jit(solution)/shard_map/ppermute | solution.py:295
  27.9 13.1 %collective-permute-start.3 = (bf16[64,2048]{1,0:T(8,128)(2,1)S(1)}, bf16[64,2048]{1,0:T(8,128)(2,1)S(1)}, u32[]{:S(2)}, u32[]{:S(2)}) collective-permute-start(bf16[64,2048]{1,0:T(8,128)(2,1)S(1)} %get-tuple-element.28), channel_id=1, source_target_pairs={{0,1},{1,2},{2,3},{3,4},{4,5},{5,6},{6,7},{7,0},{8,15},{9,8},{10,9... | collective-permute-start | bytes 786440 | tf_op jit(solution)/shard_map/ppermute | solution.py:318
  29.8 11.2 %collective-permute-start.4 = (bf16[64,2048]{1,0:T(8,128)(2,1)S(1)}, bf16[64,2048]{1,0:T(8,128)(2,1)S(1)}, u32[]{:S(2)}, u32[]{:S(2)}) collective-permute-start(bf16[64,2048]{1,0:T(8,128)(2,1)S(1)} %get-tuple-element.29), channel_id=1, source_target_pairs={{0,7},{1,0},{2,1},{3,2},{4,3},{5,4},{6,5},{7,6},{8,9},{9,10},{10,1... | collective-permute-start | bytes 786440 | tf_op jit(solution)/shard_map/ppermute | solution.py:318
  33.2 7.8 %collective-permute-start.5 = (bf16[32,2048]{1,0:T(8,128)(2,1)S(1)}, bf16[32,2048]{1,0:T(8,128)(2,1)S(1)}, u32[]{:S(2)}, u32[]{:S(2)}) collective-permute-start(bf16[32,2048]{1,0:T(8,128)(2,1)S(1)} %get-tuple-element.30), channel_id=1, source_target_pairs={{0,2},{1,3},{2,4},{3,5},{4,6},{5,7},{6,0},{7,1},{8,14},{9,15},{10,... | collective-permute-start | bytes 393224 | tf_op jit(solution)/shard_map/ppermute | solution.py:318
  41.1 7.8 %collective-permute-start.6 = (bf16[32,2048]{1,0:T(8,128)(2,1)S(1)}, bf16[32,2048]{1,0:T(8,128)(2,1)S(1)}, u32[]{:S(2)}, u32[]{:S(2)}) collective-permute-start(bf16[32,2048]{1,0:T(8,128)(2,1)S(1)} %get-tuple-element.31), channel_id=1, source_target_pairs={{0,2},{1,3},{2,4},{3,5},{4,6},{5,7},{6,0},{7,1},{8,14},{9,15},{10,... | collective-permute-start | bytes 393224 | tf_op jit(solution)/shard_map/ppermute | solution.py:318
  45.6 10.4 %collective-permute-start.7 = (bf16[32,2048]{1,0:T(8,128)(2,1)S(1)}, bf16[32,2048]{1,0:T(8,128)(2,1)S(1)}, u32[]{:S(2)}, u32[]{:S(2)}) collective-permute-start(bf16[32,2048]{1,0:T(8,128)(2,1)S(1)} %get-tuple-element.32), channel_id=1, source_target_pairs={{0,6},{1,7},{2,0},{3,1},{4,2},{5,3},{6,4},{7,5},{8,10},{9,11},{10,... | collective-permute-start | bytes 393224 | tf_op jit(solution)/shard_map/ppermute | solution.py:318

commit v3 on v2

--- a/solution.py
+++ b/solution.py
@@ -8,7 +8,7 @@
 from jax.experimental.pallas import tpu as pltpu
 from jax.sharding import PartitionSpec as P
 
-HEADS = 16
+
 ROPE_THETA = 10000000.0
 EPSILON = 1e-06
 
@@ -53,7 +53,7 @@
     return front * cosine + partner * sine, x[:, 128:]
 
 
-def kv_body(head_dim, kv_share, starts_in, gain_in, tok_in, kw_in, vw_in, kv, trig, starts, gain, tok, kw, vw, sems):
+def kv_body(head_dim, kv_share, starts_in, gain_in, tok_in, kw_in, vw_in, qw_in, gw_in, kv, trig, tok, qw, gw, starts, gain, kw, vw, sems):
     rows = tok.shape[0]
     column = pl.multiple_of((lax.axis_index("head") // kv_share) * head_dim, head_dim)
     columns = pl.ds(column, head_dim)
@@ -66,6 +66,8 @@
                 (tok_in, tok),
                 (kw_in.at[:, columns], kw),
                 (vw_in.at[:, columns], vw),
+                (qw_in, qw),
+                (gw_in, gw),
             )
         )
     ]
@@ -78,13 +80,15 @@
     cosine, sine = rope_angles(offset, head_dim)
     trig[:, :128] = cosine
     trig[:, 128:] = sine
-    for c in copies[1:]:
+    for c in copies[1:5]:
         c.wait()
     key = jnp.dot(tok[...], kw[...], preferred_element_type=F32)
     kv[:, head_dim:] = jnp.dot(tok[...], vw[...], preferred_element_type=F32).astype(BF16)
     front, back = normed_rotated(key, gain[...], trig[:, :128], trig[:, 128:], head_dim // 8)
     kv[:, :128] = front.astype(BF16)
     kv[:, 128:head_dim] = back.astype(BF16)
+    for c in copies[5:]:
+        c.wait()
 
 
 def attend(query, key, value, keep, scale):
@@ -104,36 +108,20 @@
     return (key <= at) & (key >= begin)
 
 
-def q_body(head_dim, starts_in, gain_in, trig, kv, tok_in, qw_in, gw_in, q_out, gate, num, den, starts, gain, tok, w, sems):
+def q_body(head_dim, starts, gain, trig, kv, tok, qw, gw, q_out, gate, num, den):
     rows = tok.shape[0]
-    heads = qw_in.shape[1] // head_dim
-    pairs = [(starts_in, starts), (gain_in, gain), (tok_in, tok)]
-    small = len(pairs)
-    for i in range(heads):
-        columns = pl.ds(i * head_dim, head_dim)
-        pairs.append((qw_in.at[:, columns], w.at[2 * i]))
-        pairs.append((gw_in.at[:, columns], w.at[2 * i + 1]))
-    copies = [
-        pltpu.make_async_copy(source, target, sems.at[i])
-        for i, (source, target) in enumerate(pairs)
-    ]
-    for c in copies:
-        c.start()
+    heads = qw.shape[1] // head_dim
     base = lax.axis_index("seq") * rows
-    copies[0].wait()
     begin = doc_begin(starts[...], rows, base)
     keep = kept(rows, rows, base, base, begin)
-    for c in copies[1:small]:
-        c.wait()
     for i in range(heads):
         at = pl.ds(i * rows, rows)
-        copies[small + 2 * i].wait()
-        query = jnp.dot(tok[...], w[2 * i], preferred_element_type=F32)
+        columns = slice(i * head_dim, (i + 1) * head_dim)
+        query = jnp.dot(tok[...], qw[:, columns], preferred_element_type=F32)
         front, back = normed_rotated(query, gain[...], trig[:, :128], trig[:, 128:], head_dim // 8)
         q_out[at, :128] = front.astype(BF16)
         q_out[at, 128:] = back.astype(BF16)
-        copies[small + 2 * i + 1].wait()
-        logits = jnp.dot(tok[...], w[2 * i + 1], preferred_element_type=F32)
+        logits = jnp.dot(tok[...], gw[:, columns], preferred_element_type=F32)
         gate[at, :] = 1.0 / (1.0 + jnp.exp(-logits))
         weighted, sums = attend(
             q_out[at, :], kv[:, :head_dim], kv[:, head_dim:], keep, head_dim ** (-0.5)
@@ -142,45 +130,49 @@
         den[at, :] = sums
 
 
-def out_body(head_dim, starts, readers, query, gate, num, den, near, far, own, ow, part_a, part_b, part_c, part_d, gated, turned):
-    heads = query.shape[0] // head_dim
-    rows = query.shape[0] // heads
+def source_mask(starts, readers, rows, source):
+    block = lax.axis_index("seq")
+    span = readers.shape[0]
+    distance = block - source
+    inside = (source >= 0) & (distance >= 1) & (distance <= span)
+    listed = readers[jnp.clip(distance - 1, 0, span - 1), jnp.maximum(source, 0)]
+    first = jnp.where(inside & (listed == 1), 0, 1 << 30)
+    begin = doc_begin(starts[...], rows, block * rows)
+    return kept(rows, rows, block * rows, source * rows, jnp.maximum(begin, first))
+
+
+def attend_block(head_dim, query, block, keep, num_in, den_in, num, den):
+    rows = keep.shape[0]
+    for i in range(query.shape[0] // rows):
+        at = pl.ds(i * rows, rows)
+        weighted, sums = attend(
+            query[at, :], block[:, :head_dim], block[:, head_dim:], keep, head_dim ** (-0.5)
+        )
+        num[at, :] = num_in[at, :] + weighted
+        den[at, :] = den_in[at, :] + sums
+
+
+def near_body(head_dim, starts, readers, query, num_in, den_in, near, own, num, den):
+    rows = near.shape[0]
+    block = lax.axis_index("seq")
+    core = lax.rem(block, 2)
+    keep = source_mask(starts, readers, rows, block - 2)
+    attend_block(head_dim, query, near, keep, num_in, den_in, num, den)
+
+    @pl.when(core == 1)
+    def _():
+        keep = source_mask(starts, readers, rows, block - 1)
+        attend_block(head_dim, query, own, keep, num, den, num, den)
+
+
+def out_body(head_dim, starts, readers, query, gate, num_in, den_in, far, ow, part_a, part_b, part_c, part_d, num, den, gated, turned):
+    rows = far.shape[0]
+    heads = query.shape[0] // rows
     block = lax.axis_index("seq")
     core = lax.rem(block, 2)
     head = lax.axis_index("head")
-    base = block * rows
-    begin = doc_begin(starts[...], rows, base)
-    chip = block - core
-
-    def mask(source):
-        distance = block - source
-        inside = (source >= 0) & (distance >= 1) & (distance <= readers.shape[0])
-        listed = readers[
-            jnp.clip(distance - 1, 0, readers.shape[0] - 1), jnp.maximum(source, 0)
-        ]
-        first = jnp.where(inside & (listed == 1), 0, 1 << 30)
-        return kept(rows, rows, base, source * rows, jnp.maximum(begin, first))
-
-    def add(block_ref, keep):
-        for i in range(heads):
-            at = pl.ds(i * rows, rows)
-            weighted, sums = attend(
-                query[at, :],
-                block_ref[:, :head_dim],
-                block_ref[:, head_dim:],
-                keep,
-                head_dim ** (-0.5),
-            )
-            num[at, :] += weighted
-            den[at, :] += sums
-
-    add(near, mask(chip - 2 + core))
-    add(far, mask(chip - 1 - core))
-
-    @pl.when(core == 1)
-    def _():
-        add(own, mask(block - 1))
-
+    keep = source_mask(starts, readers, rows, block - 1 - 2 * core)
+    attend_block(head_dim, query, far, keep, num_in, den_in, num, den)
     for i in range(heads):
         at = pl.ds(i * rows, rows)
         total = jnp.sum(den[at, :], axis=1, keepdims=True)
@@ -202,12 +194,16 @@
 ORDER = (1, 3, 7, 5, 4, 2, 6, 0)
 
 
-def second_body(rest, got_a, got_b, got_c, forward, backward):
-    piece = forward.shape[0]
+def forward_body(rest, got_a, got_c, out):
+    piece = out.shape[0]
     total = rest[:piece, :].astype(F32) + got_a[piece:, :].astype(F32) + got_c[...].astype(F32)
-    forward[...] = total.astype(BF16)
+    out[...] = total.astype(BF16)
+
+
+def backward_body(rest, got_b, out):
+    piece = out.shape[0]
     total = rest[piece : 2 * piece, :].astype(F32) + got_b[piece:, :].astype(F32)
-    backward[...] = total.astype(BF16)
+    out[...] = total.astype(BF16)
 
 
 def last_body(rest, got_a, got_b, forward, backward, out):
@@ -248,23 +244,32 @@
     def far_away(*arrays):
         return tuple(pltpu.with_memory_space_constraint(x, pltpu.HBM) for x in arrays)
 
-    own, trig = pl.pallas_call(
+    own, trig, near_tokens, near_q, near_gate = pl.pallas_call(
         functools.partial(kv_body, head_dim, kv_share),
-        out_shape=(held(rows, 2 * head_dim), held(rows, 256, F32)),
-        in_specs=[HBM] * 5,
-        out_specs=(VMEM, VMEM),
+        out_shape=(
+            held(rows, 2 * head_dim),
+            held(rows, 256, F32),
+            held(rows, width),
+            held(*q_weight.shape),
+            held(*gate_weight.shape),
+        ),
+        in_specs=[HBM] * 7,
+        out_specs=(VMEM,) * 5,
         scratch_shapes=[
             pltpu.VMEM(starts.shape, jnp.int32),
             pltpu.VMEM((1, head_dim), F32),
-            pltpu.VMEM((rows, width), BF16),
             pltpu.VMEM((width, head_dim), BF16),
             pltpu.VMEM((width, head_dim), BF16),
-            pltpu.SemaphoreType.DMA((5,)),
+            pltpu.SemaphoreType.DMA((7,)),
         ],
         compiler_params=params(16),
-        cost_estimate=cost(4 * rows * width * head_dim, 3 << 20),
+        cost_estimate=cost(4 * rows * width * head_dim, 7 << 20),
         name="kv",
-    )(*far_away(starts, k_gain.reshape(1, -1), tokens, k_weight, v_weight))
+    )(
+        *far_away(
+            starts, k_gain.reshape(1, -1), tokens, k_weight, v_weight, q_weight, gate_weight
+        )
+    )
 
     near = lax.ppermute(own, "seq", [(i, i + 2) for i in range(seq - 2)])
     below = lax.ppermute(own, "seq", [(i, i ^ 1) for i in range(seq)])
@@ -277,37 +282,43 @@
             held(stacked, head_dim, F32),
             held(stacked, 128, F32),
         ),
-        in_specs=[HBM] * 2 + [VMEM] * 2 + [HBM] * 3,
+        in_specs=[VMEM] * 7,
         out_specs=(VMEM,) * 4,
-        scratch_shapes=[
-            pltpu.VMEM(starts.shape, jnp.int32),
-            pltpu.VMEM((1, head_dim), F32),
-            pltpu.VMEM((rows, width), BF16),
-            pltpu.VMEM((2 * heads, width, head_dim), BF16),
-            pltpu.SemaphoreType.DMA((3 + 2 * heads,)),
-        ],
         compiler_params=params(24),
         cost_estimate=cost(4 * rows * width * heads * head_dim, 5 << 20),
         name="query",
-    )(*far_away(starts, q_gain.reshape(1, -1)), trig, own, *far_away(tokens, q_weight, gate_weight))
+    )(starts, q_gain.reshape(1, -1), trig, own, near_tokens, near_q, near_gate)
 
     near, query = lax.optimization_barrier((near, query))
     far = lax.ppermute(near, "seq", [(i, i ^ 1) for i in range(seq)])
+
+    table = readers.T
+    num, den = pl.pallas_call(
+        functools.partial(near_body, head_dim),
+        out_shape=(held(stacked, head_dim, F32), held(stacked, 128, F32)),
+        in_specs=[VMEM, SMEM] + [VMEM] * 5,
+        out_specs=(VMEM,) * 2,
+        compiler_params=params(16),
+        cost_estimate=cost(4 * stacked * rows * head_dim, 3 << 20),
+        name="near",
+    )(starts, table, query, num, den, near, below)
 
     piece = rows // head
     part_a, part_b, part_c, rest = pl.pallas_call(
         functools.partial(out_body, head_dim),
-        out_shape=tuple(shape(n * piece, width) for n in (2, 2, 1, 3)),
-        in_specs=[VMEM, SMEM] + [VMEM] * 8,
+        out_shape=tuple(held(n * piece, width) for n in (2, 2, 1, 3)),
+        in_specs=[VMEM, SMEM] + [VMEM] * 6,
         out_specs=(VMEM,) * 4,
         scratch_shapes=[
+            pltpu.VMEM((stacked, head_dim), F32),
+            pltpu.VMEM((stacked, 128), F32),
             pltpu.VMEM((rows, heads * head_dim), BF16),
             pltpu.VMEM((rows, heads * head_dim), BF16),
         ],
-        compiler_params=params(20),
+        compiler_params=params(24),
         cost_estimate=cost(2 * rows * width * heads * head_dim, 4 << 20),
         name="attend",
-    )(starts, readers.T, query, gate, num, den, near, far, below, out_weight)
+    )(starts, table, query, gate, num, den, far, out_weight)
 
     def turn(block, step):
         route = []
@@ -317,19 +328,21 @@
                 route.append((s * head + h, s * head + to))
         return lax.ppermute(block, ("seq", "head"), route)
 
+    def summed(body, *blocks):
+        return pl.pallas_call(
+            body,
+            out_shape=held(piece, width),
+            in_specs=[VMEM] * len(blocks),
+            out_specs=VMEM,
+            compiler_params=params(8),
+            cost_estimate=cost(4 * piece * width, 8 * piece * width),
+        )(*blocks)
+
+    got_a = turn(part_a, 1)
     got_c = turn(part_c, 2)
-    got_a = turn(part_a, 1)
     got_b = turn(part_b, -1)
-    forward, backward = pl.pallas_call(
-        second_body,
-        out_shape=(shape(piece, width),) * 2,
-        in_specs=[VMEM] * 4,
-        out_specs=(VMEM,) * 2,
-        compiler_params=params(8),
-        name="second",
-    )(rest, got_a, got_b, got_c)
-    forward = turn(forward, 2)
-    backward = turn(backward, -2)
+    forward = turn(summed(forward_body, rest, got_a, got_c), 2)
+    backward = turn(summed(backward_body, rest, got_b), -2)
     return pl.pallas_call(
         last_body,
         out_shape=shape(piece, width),

time: 57.1 us -> 54.5 us (0.954)
  the two profiles are of different devices: /device:TPU:1 before, /device:TPU:528 now
where the time goes in v3:
time: 54.5 us; the launch traced here: 54.2 us
  starting transfers between devices  28.4 us (52%)
  waiting for transfers between devices  16.4 us (30%)
  Pallas kernels  9.18 us (17%)
    ppermute x5, starting transfers between devices, turn(): return lax.ppermute(block, ('seq', 'head'), route)  21.2 us
    ppermute x5, waiting for transfers between devices, turn(): return lax.ppermute(block, ('seq', 'head'), route)  10.3 us
    ppermute x1, waiting for transfers between devices, shards(): near = lax.ppermute(own, 'seq', [(i, i + 2) for i in range(seq - 2)])  5.86 us
    ppermute x1, starting transfers between devices, shards(): near = lax.ppermute(own, 'seq', [(i, i + 2) for i in range(seq - 2)])  3.4 us
    pallas_call x1, Pallas kernels, shards(): pl.pallas_call(functools.partial(kv_body, head_dim, kv_share), out_shape=...  3.29 us
    pallas_call x1, Pallas kernels, shards(): pl.pallas_call(functools.partial(q_body, head_dim), out_shape=(held(stack...  2.01 us
    ppermute x1, starting transfers between devices, shards(): below = lax.ppermute(own, 'seq', [(i, i ^ 1) for i in range(seq)])  1.92 us
    ppermute x1, starting transfers between devices, shards(): far = lax.ppermute(near, 'seq', [(i, i ^ 1) for i in range(seq)])  1.91 us
  transfers between devices with their start and end apart: 8, of which 5 were waited for; matrix products, arithmetic and copies ran while one was open for 0% of the time, Pallas kernels for 6%

profile of v3, /device:TPU:528, one launch (start us, length us, event | category | flops | bytes accessed | tf_op | source)
XLA Modules:
  0.0 54.2 jit_solution(16307352655973652098)
XLA Ops:
  0.0 0.0 copy-start.2
  0.0 0.0 copy-start.3
  0.0 3.3 %kv.1 = (bf16[256,512]{1,0:T(8,128)(2,1)S(1)}, f32[256,256]{1,0:T(8,128)S(1)}, bf16[256,2048]{1,0:T(8,128)(2,1)S(1)}, bf16[2048,512]{1,0:T(8,128)(2,1)S(1)}, bf16[2048,512]{1,0:T(8,128)(2,1)S(1)}) custom-call(s32[1,48]{1,0:T(1,128)} %bitcast.6, f32[1,256]{1,0:T(1,128)} %bitcast.11, bf16[256,2048]{1,0:T(8,128)(2,1)} %tok_in.1, bf16[2048,512]{1,0:T(8,128)(2,1)} %kw_in.1, ...), custom_call_target="tpu_custom_call" | custom-call | flops 536870912 | bytes 7340032 | tf_op jit(solution)/shard_map/kv/pallas_call | solution.py:247
  3.3 3.4 %collective-permute-start = (bf16[256,512]{1,0:T(8,128)(2,1)S(1)}, bf16[256,512]{1,0:T(8,128)(2,1)S(1)}, u32[]{:S(2)}, u32[]{:S(2)}) collective-permute-start(bf16[256,512]{1,0:T(8,128)(2,1)S(1)} %get-tuple-element.22.kv), channel_id=1, source_target_pairs={{0,16},{8,24},{16,32},{24,40},{32,48},{40,56},{48,64},{56,72},{64,... | collective-permute-start | bytes 786440 | tf_op jit(solution)/shard_map/ppermute | solution.py:274
  6.7 1.9 %collective-permute-start.1 = (bf16[256,512]{1,0:T(8,128)(2,1)S(1)}, bf16[256,512]{1,0:T(8,128)(2,1)S(1)}, u32[]{:S(2)}, u32[]{:S(2)}) collective-permute-start(bf16[256,512]{1,0:T(8,128)(2,1)S(1)} %get-tuple-element.22.kv), channel_id=1, source_target_pairs={{0,8},{8,0},{16,24},{24,16},{32,40},{40,32},{48,56},{56,48},{64,72... | collective-permute-start | bytes 786440 | tf_op jit(solution)/shard_map/ppermute | solution.py:275
  8.6 0.0 copy-done.2
  8.6 0.0 copy-done.3
  8.7 0.0 copy-start.1
  8.7 0.0 copy-start
  8.7 2.0 %query.1 = (bf16[512,256]{1,0:T(8,128)(2,1)S(1)}, f32[512,256]{1,0:T(8,128)S(1)}, f32[512,256]{1,0:T(8,128)S(1)}, f32[512,128]{1,0:T(8,128)S(1)}) custom-call(s32[1,48]{1,0:T(1,128)S(1)} %bitcast.7, f32[1,256]{1,0:T(1,128)S(1)} %bitcast.10, f32[256,256]{1,0:T(8,128)S(1)} %get-tuple-element.23.trig, bf16[256,512]{1,0:T(8,128)(2,1)S(1)} %get-tuple-element.22.kv, ...), custom_call_target="tpu_custom_call" | custom-call | flops 1073741824 | bytes 5242880 | tf_op jit(solution)/shard_map/query/pallas_call | solution.py:277
  10.7 5.9 %collective-permute-done.near = bf16[256,512]{1,0:T(8,128)(2,1)S(1)} collective-permute-done((bf16[256,512]{1,0:T(8,128)(2,1)S(1)}, bf16[256,512]{1,0:T(8,128)(2,1)S(1)}, u32[]{:S(2)}, u32[]{:S(2)}) %collective-permute-start) | collective-permute-done | bytes 262176 | tf_op jit(solution)/shard_map/ppermute | solution.py:274
  16.6 1.9 %collective-permute-start.2 = (bf16[256,512]{1,0:T(8,128)(2,1)S(1)}, bf16[256,512]{1,0:T(8,128)(2,1)S(1)}, u32[]{:S(2)}, u32[]{:S(2)}) collective-permute-start(bf16[256,512]{1,0:T(8,128)(2,1)S(1)} %collective-permute-done.near), channel_id=1, source_target_pairs={{0,8},{8,0},{16,24},{24,16},{32,40},{40,32},{48,56},{56,48},{64,72... | collective-permute-start | bytes 786440 | tf_op jit(solution)/shard_map/ppermute | solution.py:293
  18.5 0.0 collective-permute-done.1.own
  18.5 0.0 copy-done.1
  18.5 1.2 %near.1 = (f32[512,256]{1,0:T(8,128)S(1)}, f32[512,128]{1,0:T(8,128)S(1)}) custom-call(s32[1,48]{1,0:T(1,128)S(1)} %bitcast.8, s32[3,96]{1,0:T(4,128)S(1)} %bitcast.4, bf16[512,256]{1,0:T(8,128)(2,1)S(1)} %get-tuple-element.28.query, f32[512,256]{1,0:T(8,128)S(1)} %get-tuple-element.30.num_in, f32[512,128]{1,0:T(8,128)S(1)} %get-tuple-element.31.den_in, ...), custom_call_target="tpu_custom_call" | custom-call | flops 134217728 | bytes 3145728 | tf_op jit(solution)/shard_map/near/pallas_call | solution.py:296
  19.7 0.3 collective-permute-done.2.far
  20.0 0.0 copy-done
  20.0 1.9 %attend.1 = (bf16[64,2048]{1,0:T(8,128)(2,1)S(1)}, bf16[64,2048]{1,0:T(8,128)(2,1)S(1)}, bf16[32,2048]{1,0:T(8,128)(2,1)S(1)}, bf16[96,2048]{1,0:T(8,128)(2,1)S(1)}) custom-call(s32[1,48]{1,0:T(1,128)S(1)} %bitcast.9, s32[3,96]{1,0:T(4,128)S(1)} %bitcast.5, bf16[512,256]{1,0:T(8,128)(2,1)S(1)} %get-tuple-element.28.query, ...), custom_call_target="tpu_custom_call" | custom-call | flops 536870912 | bytes 4194304 | tf_op jit(solution)/shard_map/attend/pallas_call | solution.py:307
  21.9 3.5 %collective-permute-start.3 = (bf16[64,2048]{1,0:T(8,128)(2,1)S(1)}, bf16[64,2048]{1,0:T(8,128)(2,1)S(1)}, u32[]{:S(2)}, u32[]{:S(2)}) collective-permute-start(bf16[64,2048]{1,0:T(8,128)(2,1)S(1)} %get-tuple-element.36), channel_id=1, source_target_pairs={{0,1},{1,2},{2,3},{3,4},{4,5},{5,6},{6,7},{7,0},{8,15},{9,8},{10,9... | collective-permute-start | bytes 786440 | tf_op jit(solution)/shard_map/ppermute | solution.py:329
  25.4 2.4 %collective-permute-start.4 = (bf16[64,2048]{1,0:T(8,128)(2,1)S(1)}, bf16[64,2048]{1,0:T(8,128)(2,1)S(1)}, u32[]{:S(2)}, u32[]{:S(2)}) collective-permute-start(bf16[64,2048]{1,0:T(8,128)(2,1)S(1)} %get-tuple-element.37), channel_id=1, source_target_pairs={{0,7},{1,0},{2,1},{3,2},{4,3},{5,4},{6,5},{7,6},{8,9},{9,10},{10,1... | collective-permute-start | bytes 786440 | tf_op jit(solution)/shard_map/ppermute | solution.py:329
  27.7 6.9 %collective-permute-start.5 = (bf16[32,2048]{1,0:T(8,128)(2,1)S(1)}, bf16[32,2048]{1,0:T(8,128)(2,1)S(1)}, u32[]{:S(2)}, u32[]{:S(2)}) collective-permute-start(bf16[32,2048]{1,0:T(8,128)(2,1)S(1)} %get-tuple-element.38), channel_id=1, source_target_pairs={{0,2},{1,3},{2,4},{3,5},{4,6},{5,7},{6,0},{7,1},{8,14},{9,15},{10,... | collective-permute-start | bytes 393224 | tf_op jit(solution)/shard_map/ppermute | solution.py:329
  34.6 2.6 %collective-permute-done.5.got_c = bf16[32,2048]{1,0:T(8,128)(2,1)S(1)} collective-permute-done((bf16[32,2048]{1,0:T(8,128)(2,1)S(1)}, bf16[32,2048]{1,0:T(8,128)(2,1)S(1)}, u32[]{:S(2)}, u32[]{:S(2)}) %collective-permute-start.5) | collective-permute-done | bytes 131104 | tf_op jit(solution)/shard_map/ppermute | solution.py:329
  37.3 0.0 collective-permute-done.3.got_a
  37.3 0.1 shard_map.100
  37.3 6.5 %collective-permute-start.6 = (bf16[32,2048]{1,0:T(8,128)(2,1)S(1)}, bf16[32,2048]{1,0:T(8,128)(2,1)S(1)}, u32[]{:S(2)}, u32[]{:S(2)}) collective-permute-start(bf16[32,2048]{1,0:T(8,128)(2,1)S(1)} %shard_map.100), channel_id=1, source_target_pairs={{0,2},{1,3},{2,4},{3,5},{4,6},{5,7},{6,0},{7,1},{8,14},{9,15},{10,... | collective-permute-start | bytes 393224 | tf_op jit(solution)/shard_map/ppermute | solution.py:329
  43.8 0.0 collective-permute-done.4.got_b
  43.9 1.9 %collective-permute-start.7 = (bf16[32,2048]{1,0:T(8,128)(2,1)S(1)}, bf16[32,2048]{1,0:T(8,128)(2,1)S(1)}, u32[]{:S(2)}, u32[]{:S(2)}) collective-permute-start(bf16[32,2048]{1,0:T(8,128)(2,1)S(1)} %shard_map.101), channel_id=1, source_target_pairs={{0,6},{1,7},{2,0},{3,1},{4,2},{5,3},{6,4},{7,5},{8,10},{9,11},{10,... | collective-permute-start | bytes 393224 | tf_op jit(solution)/shard_map/ppermute | solution.py:329
  45.8 2.8 %collective-permute-done.6.forward = bf16[32,2048]{1,0:T(8,128)(2,1)S(1)} collective-permute-done((bf16[32,2048]{1,0:T(8,128)(2,1)S(1)}, bf16[32,2048]{1,0:T(8,128)(2,1)S(1)}, u32[]{:S(2)}, u32[]{:S(2)}) %collective-permute-start.6) | collective-permute-done | bytes 131104 | tf_op jit(solution)/shard_map/ppermute | solution.py:329
  48.6 4.8 %collective-permute-done.7.backward = bf16[32,2048]{1,0:T(8,128)(2,1)S(1)} collective-permute-done((bf16[32,2048]{1,0:T(8,128)(2,1)S(1)}, bf16[32,2048]{1,0:T(8,128)(2,1)S(1)}, u32[]{:S(2)}, u32[]{:S(2)}) %collective-permute-start.7) | collective-permute-done | bytes 131104 | tf_op jit(solution)/shard_map/ppermute | solution.py:329
  53.5 0.7 %last.1 = bf16[32,2048]{1,0:T(8,128)(2,1)} custom-call(bf16[96,2048]{1,0:T(8,128)(2,1)S(1)} %get-tuple-element.35.rest, bf16[64,2048]{1,0:T(8,128)(2,1)S(1)} %collective-permute-done.3.got_a, bf16[64,2048]{1,0:T(8,128)(2,1)S(1)} %collective-permute-done.4.got_b, bf16[32,2048]{1,0:T(8,128)(2,1)S(1)} %collective-permute-done.6.forward, ...), custom_call_target="tpu_custom_call" | custom-call | tf_op jit(solution)/shard_map/last/pallas_call | solution.py:346
  (1 shorter events, 0.0 us)
Async XLA Ops:
  0.0 8.6 %copy-start.2 = (s32[48]{0:T(128)S(1)}, s32[48]{0:T(128)}, u32[]{:S(2)}) copy-start(s32[48]{0:T(128)} %param.18) | copy-start | bytes 580
  0.0 8.6 %copy-start.3 = (f32[256]{0:T(256)S(1)}, f32[256]{0:T(256)}, u32[]{:S(2)}) copy-start(f32[256]{0:T(256)} %param.15) | copy-start | bytes 3076
  3.3 13.3 %collective-permute-start = (bf16[256,512]{1,0:T(8,128)(2,1)S(1)}, bf16[256,512]{1,0:T(8,128)(2,1)S(1)}, u32[]{:S(2)}, u32[]{:S(2)}) collective-permute-start(bf16[256,512]{1,0:T(8,128)(2,1)S(1)} %get-tuple-element.22.kv), channel_id=1, source_target_pairs={{0,16},{8,24},{16,32},{24,40},{32,48},{40,56},{48,64},{56,72},{64,... | collective-permute-start | bytes 786440 | tf_op jit(solution)/shard_map/ppermute | solution.py:274
  6.7 11.8 %collective-permute-start.1 = (bf16[256,512]{1,0:T(8,128)(2,1)S(1)}, bf16[256,512]{1,0:T(8,128)(2,1)S(1)}, u32[]{:S(2)}, u32[]{:S(2)}) collective-permute-start(bf16[256,512]{1,0:T(8,128)(2,1)S(1)} %get-tuple-element.22.kv), channel_id=1, source_target_pairs={{0,8},{8,0},{16,24},{24,16},{32,40},{40,32},{48,56},{56,48},{64,72... | collective-permute-start | bytes 786440 | tf_op jit(solution)/shard_map/ppermute | solution.py:275
  8.7 9.8 %copy-start.1 = (s32[96,3]{0,1:T(4,128)S(1)}, s32[96,3]{0,1:T(4,128)}, u32[]{:S(2)}) copy-start(s32[96,3]{0,1:T(4,128)} %param.19) | copy-start | bytes 3460
  8.7 11.3 %copy-start = (bf16[512,2048]{1,0:T(8,128)(2,1)S(1)}, bf16[512,2048]{1,0:T(8,128)(2,1)}, u32[]{:S(2)}) copy-start(bf16[512,2048]{1,0:T(8,128)(2,1)} %ow.1) | copy-start | bytes 6291460
  16.6 3.4 %collective-permute-start.2 = (bf16[256,512]{1,0:T(8,128)(2,1)S(1)}, bf16[256,512]{1,0:T(8,128)(2,1)S(1)}, u32[]{:S(2)}, u32[]{:S(2)}) collective-permute-start(bf16[256,512]{1,0:T(8,128)(2,1)S(1)} %collective-permute-done.near), channel_id=1, source_target_pairs={{0,8},{8,0},{16,24},{24,16},{32,40},{40,32},{48,56},{56,48},{64,72... | collective-permute-start | bytes 786440 | tf_op jit(solution)/shard_map/ppermute | solution.py:293
  21.9 15.4 %collective-permute-start.3 = (bf16[64,2048]{1,0:T(8,128)(2,1)S(1)}, bf16[64,2048]{1,0:T(8,128)(2,1)S(1)}, u32[]{:S(2)}, u32[]{:S(2)}) collective-permute-start(bf16[64,2048]{1,0:T(8,128)(2,1)S(1)} %get-tuple-element.36), channel_id=1, source_target_pairs={{0,1},{1,2},{2,3},{3,4},{4,5},{5,6},{6,7},{7,0},{8,15},{9,8},{10,9... | collective-permute-start | bytes 786440 | tf_op jit(solution)/shard_map/ppermute | solution.py:329
  25.4 18.5 %collective-permute-start.4 = (bf16[64,2048]{1,0:T(8,128)(2,1)S(1)}, bf16[64,2048]{1,0:T(8,128)(2,1)S(1)}, u32[]{:S(2)}, u32[]{:S(2)}) collective-permute-start(bf16[64,2048]{1,0:T(8,128)(2,1)S(1)} %get-tuple-element.37), channel_id=1, source_target_pairs={{0,7},{1,0},{2,1},{3,2},{4,3},{5,4},{6,5},{7,6},{8,9},{9,10},{10,1... | collective-permute-start | bytes 786440 | tf_op jit(solution)/shard_map/ppermute | solution.py:329
  27.7 9.6 %collective-permute-start.5 = (bf16[32,2048]{1,0:T(8,128)(2,1)S(1)}, bf16[32,2048]{1,0:T(8,128)(2,1)S(1)}, u32[]{:S(2)}, u32[]{:S(2)}) collective-permute-start(bf16[32,2048]{1,0:T(8,128)(2,1)S(1)} %get-tuple-element.38), channel_id=1, source_target_pairs={{0,2},{1,3},{2,4},{3,5},{4,6},{5,7},{6,0},{7,1},{8,14},{9,15},{10,... | collective-permute-start | bytes 393224 | tf_op jit(solution)/shard_map/ppermute | solution.py:329
  37.3 11.3 %collective-permute-start.6 = (bf16[32,2048]{1,0:T(8,128)(2,1)S(1)}, bf16[32,2048]{1,0:T(8,128)(2,1)S(1)}, u32[]{:S(2)}, u32[]{:S(2)}) collective-permute-start(bf16[32,2048]{1,0:T(8,128)(2,1)S(1)} %shard_map.100), channel_id=1, source_target_pairs={{0,2},{1,3},{2,4},{3,5},{4,6},{5,7},{6,0},{7,1},{8,14},{9,15},{10,... | collective-permute-start | bytes 393224 | tf_op jit(solution)/shard_map/ppermute | solution.py:329
  43.9 9.6 %collective-permute-start.7 = (bf16[32,2048]{1,0:T(8,128)(2,1)S(1)}, bf16[32,2048]{1,0:T(8,128)(2,1)S(1)}, u32[]{:S(2)}, u32[]{:S(2)}) collective-permute-start(bf16[32,2048]{1,0:T(8,128)(2,1)S(1)} %shard_map.101), channel_id=1, source_target_pairs={{0,6},{1,7},{2,0},{3,1},{4,2},{5,3},{6,4},{7,5},{8,10},{9,11},{10,... | collective-permute-start | bytes 393224 | tf_op jit(solution)/shard_map/ppermute | solution.py:329

commit v4 on v3

--- a/solution.py
+++ b/solution.py
@@ -57,21 +57,21 @@
     rows = tok.shape[0]
     column = pl.multiple_of((lax.axis_index("head") // kv_share) * head_dim, head_dim)
     columns = pl.ds(column, head_dim)
-    copies = [
-        pltpu.make_async_copy(source, target, sems.at[i])
-        for i, (source, target) in enumerate(
-            (
-                (starts_in, starts),
-                (gain_in, gain),
-                (tok_in, tok),
-                (kw_in.at[:, columns], kw),
-                (vw_in.at[:, columns], vw),
-                (qw_in, qw),
-                (gw_in, gw),
-            )
-        )
-    ]
-    for c in copies:
+    half = tok.shape[1] // 2
+    low, high = pl.ds(0, half), pl.ds(half, half)
+    pairs = (
+        (starts_in, starts),
+        (gain_in, gain),
+        (tok_in.at[:, low], tok.at[:, low]),
+        (kw_in.at[low, columns], kw.at[low, :]),
+        (tok_in.at[:, high], tok.at[:, high]),
+        (kw_in.at[high, columns], kw.at[high, :]),
+        (vw_in.at[:, columns], vw),
+        (qw_in, qw),
+        (gw_in, gw),
+    )
+    copies = [pltpu.make_async_copy(a, b, sems.at[i]) for i, (a, b) in enumerate(pairs)]
+    for c in copies[:7]:
         c.start()
     base = lax.axis_index("seq") * rows
     copies[0].wait()
@@ -80,14 +80,20 @@
     cosine, sine = rope_angles(offset, head_dim)
     trig[:, :128] = cosine
     trig[:, 128:] = sine
-    for c in copies[1:5]:
+    for c in copies[1:4]:
         c.wait()
-    key = jnp.dot(tok[...], kw[...], preferred_element_type=F32)
+    key = jnp.dot(tok[:, :half], kw[:half, :], preferred_element_type=F32)
+    for c in copies[4:6]:
+        c.wait()
+    for c in copies[7:]:
+        c.start()
+    key = key + jnp.dot(tok[:, half:], kw[half:, :], preferred_element_type=F32)
+    copies[6].wait()
     kv[:, head_dim:] = jnp.dot(tok[...], vw[...], preferred_element_type=F32).astype(BF16)
     front, back = normed_rotated(key, gain[...], trig[:, :128], trig[:, 128:], head_dim // 8)
     kv[:, :128] = front.astype(BF16)
     kv[:, 128:head_dim] = back.astype(BF16)
-    for c in copies[5:]:
+    for c in copies[7:]:
         c.wait()
 
 
@@ -180,7 +186,7 @@
     count = 8
     piece = rows // count
     for i, step in enumerate(ORDER):
-        source = lax.rem(head + jnp.where(core == 0, step, count - step), count)
+        source = lax.rem(head + jnp.where(lax.rem(head + core, 2) == 0, step, count - step), count)
         turned[i * piece : (i + 1) * piece, :] = gated[
             pl.ds(pl.multiple_of(source * piece, piece), piece), :
         ]
@@ -191,25 +197,25 @@
         at += ref.shape[0]
 
 
-ORDER = (1, 3, 7, 5, 4, 2, 6, 0)
-
-
-def forward_body(rest, got_a, got_c, out):
+ORDER = (1, 3, 7, 5, 4, 6, 2, 0)
+
+
+def first_body(rest, got_a, got_c, out):
     piece = out.shape[0]
     total = rest[:piece, :].astype(F32) + got_a[piece:, :].astype(F32) + got_c[...].astype(F32)
     out[...] = total.astype(BF16)
 
 
-def backward_body(rest, got_b, out):
+def second_body(rest, got_b, out):
     piece = out.shape[0]
     total = rest[piece : 2 * piece, :].astype(F32) + got_b[piece:, :].astype(F32)
     out[...] = total.astype(BF16)
 
 
-def last_body(rest, got_a, got_b, forward, backward, out):
+def last_body(rest, got_a, got_b, first, second, out):
     piece = out.shape[0]
     total = rest[2 * piece :, :].astype(F32)
-    for ref in (got_a, got_b, forward, backward):
+    for ref in (got_a, got_b, first, second):
         total = total + ref[:piece, :].astype(F32)
     out[...] = total.astype(BF16)
 
@@ -260,7 +266,7 @@
             pltpu.VMEM((1, head_dim), F32),
             pltpu.VMEM((width, head_dim), BF16),
             pltpu.VMEM((width, head_dim), BF16),
-            pltpu.SemaphoreType.DMA((7,)),
+            pltpu.SemaphoreType.DMA((9,)),
         ],
         compiler_params=params(16),
         cost_estimate=cost(4 * rows * width * head_dim, 7 << 20),
@@ -324,7 +330,7 @@
         route = []
         for s in range(seq):
             for h in range(head):
-                to = (h + step) % head if s % 2 == 0 else (h - step) % head
+                to = (h + step) % head if (s + h) % 2 == 0 else (h - step) % head
                 route.append((s * head + h, s * head + to))
         return lax.ppermute(block, ("seq", "head"), route)
 
@@ -339,10 +345,10 @@
         )(*blocks)
 
     got_a = turn(part_a, 1)
-    got_c = turn(part_c, 2)
+    got_c = turn(part_c, -2)
     got_b = turn(part_b, -1)
-    forward = turn(summed(forward_body, rest, got_a, got_c), 2)
-    backward = turn(summed(backward_body, rest, got_b), -2)
+    first = turn(summed(first_body, rest, got_a, got_c), -2)
+    second = turn(summed(second_body, rest, got_b), 2)
     return pl.pallas_call(
         last_body,
         out_shape=shape(piece, width),
@@ -350,7 +356,7 @@
         out_specs=VMEM,
         compiler_params=params(8),
         name="last",
-    )(rest, got_a, got_b, forward, backward)
+    )(rest, got_a, got_b, first, second)
 
 
 def solution(mesh):

time: 54.5 us -> 54.9 us (level)
  the two profiles are of different devices: /device:TPU:528 before, /device:TPU:512 now
where the time goes in v4:
time: 54.9 us; the launch traced here: 54.6 us
  starting transfers between devices  27.3 us (50%)
  waiting for transfers between devices  17.3 us (32%)
  Pallas kernels  9.84 us (18%)
    ppermute x5, starting transfers between devices, turn(): return lax.ppermute(block, ('seq', 'head'), route)  20.1 us
    ppermute x5, waiting for transfers between devices, turn(): return lax.ppermute(block, ('seq', 'head'), route)  11.1 us
    ppermute x1, waiting for transfers between devices, shards(): near = lax.ppermute(own, 'seq', [(i, i + 2) for i in range(seq - 2)])  5.86 us
    pallas_call x1, Pallas kernels, shards(): pl.pallas_call(functools.partial(kv_body, head_dim, kv_share), out_shape=...  3.95 us
    ppermute x1, starting transfers between devices, shards(): near = lax.ppermute(own, 'seq', [(i, i + 2) for i in range(seq - 2)])  3.4 us
    pallas_call x1, Pallas kernels, shards(): pl.pallas_call(functools.partial(q_body, head_dim), out_shape=(held(stack...  2.02 us
    ppermute x1, starting transfers between devices, shards(): below = lax.ppermute(own, 'seq', [(i, i ^ 1) for i in range(seq)])  1.92 us
    ppermute x1, starting transfers between devices, shards(): far = lax.ppermute(near, 'seq', [(i, i ^ 1) for i in range(seq)])  1.91 us
  transfers between devices with their start and end apart: 8, of which 5 were waited for; matrix products, arithmetic and copies ran while one was open for 0% of the time, Pallas kernels for 6%

profile of v4, /device:TPU:512, one launch (start us, length us, event | category | flops | bytes accessed | tf_op | source)
XLA Modules:
  0.0 54.6 jit_solution(7382722731710094)
XLA Ops:
  0.0 0.0 copy-start.2
  0.0 0.0 copy-start.3
  0.0 4.0 %kv.1 = (bf16[256,512]{1,0:T(8,128)(2,1)S(1)}, f32[256,256]{1,0:T(8,128)S(1)}, bf16[256,2048]{1,0:T(8,128)(2,1)S(1)}, bf16[2048,512]{1,0:T(8,128)(2,1)S(1)}, bf16[2048,512]{1,0:T(8,128)(2,1)S(1)}) custom-call(s32[1,48]{1,0:T(1,128)} %bitcast.6, f32[1,256]{1,0:T(1,128)} %bitcast.11, bf16[256,2048]{1,0:T(8,128)(2,1)} %tok_in.1, bf16[2048,512]{1,0:T(8,128)(2,1)} %kw_in.1, ...), custom_call_target="tpu_custom_call" | custom-call | flops 536870912 | bytes 7340032 | tf_op jit(solution)/shard_map/kv/pallas_call | solution.py:253
  4.0 3.4 %collective-permute-start = (bf16[256,512]{1,0:T(8,128)(2,1)S(1)}, bf16[256,512]{1,0:T(8,128)(2,1)S(1)}, u32[]{:S(2)}, u32[]{:S(2)}) collective-permute-start(bf16[256,512]{1,0:T(8,128)(2,1)S(1)} %get-tuple-element.22.kv), channel_id=1, source_target_pairs={{0,16},{8,24},{16,32},{24,40},{32,48},{40,56},{48,64},{56,72},{64,... | collective-permute-start | bytes 786440 | tf_op jit(solution)/shard_map/ppermute | solution.py:280
  7.4 1.9 %collective-permute-start.1 = (bf16[256,512]{1,0:T(8,128)(2,1)S(1)}, bf16[256,512]{1,0:T(8,128)(2,1)S(1)}, u32[]{:S(2)}, u32[]{:S(2)}) collective-permute-start(bf16[256,512]{1,0:T(8,128)(2,1)S(1)} %get-tuple-element.22.kv), channel_id=1, source_target_pairs={{0,8},{8,0},{16,24},{24,16},{32,40},{40,32},{48,56},{56,48},{64,72... | collective-permute-start | bytes 786440 | tf_op jit(solution)/shard_map/ppermute | solution.py:281
  9.3 0.0 copy-done.2
  9.3 0.0 copy-done.3
  9.3 0.0 copy-start.1
  9.3 0.0 copy-start
  9.3 2.0 %query.1 = (bf16[512,256]{1,0:T(8,128)(2,1)S(1)}, f32[512,256]{1,0:T(8,128)S(1)}, f32[512,256]{1,0:T(8,128)S(1)}, f32[512,128]{1,0:T(8,128)S(1)}) custom-call(s32[1,48]{1,0:T(1,128)S(1)} %bitcast.7, f32[1,256]{1,0:T(1,128)S(1)} %bitcast.10, f32[256,256]{1,0:T(8,128)S(1)} %get-tuple-element.23.trig, bf16[256,512]{1,0:T(8,128)(2,1)S(1)} %get-tuple-element.22.kv, ...), custom_call_target="tpu_custom_call" | custom-call | flops 1073741824 | bytes 5242880 | tf_op jit(solution)/shard_map/query/pallas_call | solution.py:283
  11.4 5.9 %collective-permute-done.near = bf16[256,512]{1,0:T(8,128)(2,1)S(1)} collective-permute-done((bf16[256,512]{1,0:T(8,128)(2,1)S(1)}, bf16[256,512]{1,0:T(8,128)(2,1)S(1)}, u32[]{:S(2)}, u32[]{:S(2)}) %collective-permute-start) | collective-permute-done | bytes 262176 | tf_op jit(solution)/shard_map/ppermute | solution.py:280
  17.2 1.9 %collective-permute-start.2 = (bf16[256,512]{1,0:T(8,128)(2,1)S(1)}, bf16[256,512]{1,0:T(8,128)(2,1)S(1)}, u32[]{:S(2)}, u32[]{:S(2)}) collective-permute-start(bf16[256,512]{1,0:T(8,128)(2,1)S(1)} %collective-permute-done.near), channel_id=1, source_target_pairs={{0,8},{8,0},{16,24},{24,16},{32,40},{40,32},{48,56},{56,48},{64,72... | collective-permute-start | bytes 786440 | tf_op jit(solution)/shard_map/ppermute | solution.py:299
  19.1 0.0 collective-permute-done.1.own
  19.2 0.0 copy-done.1
  19.2 1.2 %near.1 = (f32[512,256]{1,0:T(8,128)S(1)}, f32[512,128]{1,0:T(8,128)S(1)}) custom-call(s32[1,48]{1,0:T(1,128)S(1)} %bitcast.8, s32[3,96]{1,0:T(4,128)S(1)} %bitcast.4, bf16[512,256]{1,0:T(8,128)(2,1)S(1)} %get-tuple-element.28.query, f32[512,256]{1,0:T(8,128)S(1)} %get-tuple-element.30.num_in, f32[512,128]{1,0:T(8,128)S(1)} %get-tuple-element.31.den_in, ...), custom_call_target="tpu_custom_call" | custom-call | flops 134217728 | bytes 3145728 | tf_op jit(solution)/shard_map/near/pallas_call | solution.py:302
  20.3 0.3 collective-permute-done.2.far
  20.6 0.0 copy-done
  20.6 1.9 %attend.1 = (bf16[64,2048]{1,0:T(8,128)(2,1)S(1)}, bf16[64,2048]{1,0:T(8,128)(2,1)S(1)}, bf16[32,2048]{1,0:T(8,128)(2,1)S(1)}, bf16[96,2048]{1,0:T(8,128)(2,1)S(1)}) custom-call(s32[1,48]{1,0:T(1,128)S(1)} %bitcast.9, s32[3,96]{1,0:T(4,128)S(1)} %bitcast.5, bf16[512,256]{1,0:T(8,128)(2,1)S(1)} %get-tuple-element.28.query, ...), custom_call_target="tpu_custom_call" | custom-call | flops 536870912 | bytes 4194304 | tf_op jit(solution)/shard_map/attend/pallas_call | solution.py:313
  22.5 3.5 %collective-permute-start.3 = (bf16[64,2048]{1,0:T(8,128)(2,1)S(1)}, bf16[64,2048]{1,0:T(8,128)(2,1)S(1)}, u32[]{:S(2)}, u32[]{:S(2)}) collective-permute-start(bf16[64,2048]{1,0:T(8,128)(2,1)S(1)} %get-tuple-element.36), channel_id=1, source_target_pairs={{0,1},{1,0},{2,3},{3,2},{4,5},{5,4},{6,7},{7,6},{8,15},{9,10},{10,... | collective-permute-start | bytes 786440 | tf_op jit(solution)/shard_map/ppermute | solution.py:335
  26.0 5.1 %collective-permute-start.4 = (bf16[64,2048]{1,0:T(8,128)(2,1)S(1)}, bf16[64,2048]{1,0:T(8,128)(2,1)S(1)}, u32[]{:S(2)}, u32[]{:S(2)}) collective-permute-start(bf16[64,2048]{1,0:T(8,128)(2,1)S(1)} %get-tuple-element.37), channel_id=1, source_target_pairs={{0,7},{1,2},{2,1},{3,4},{4,3},{5,6},{6,5},{7,0},{8,9},{9,8},{10,11... | collective-permute-start | bytes 786440 | tf_op jit(solution)/shard_map/ppermute | solution.py:335
  31.2 4.0 %collective-permute-start.5 = (bf16[32,2048]{1,0:T(8,128)(2,1)S(1)}, bf16[32,2048]{1,0:T(8,128)(2,1)S(1)}, u32[]{:S(2)}, u32[]{:S(2)}) collective-permute-start(bf16[32,2048]{1,0:T(8,128)(2,1)S(1)} %get-tuple-element.38), channel_id=1, source_target_pairs={{0,6},{1,3},{2,0},{3,5},{4,2},{5,7},{6,4},{7,1},{8,10},{9,15},{10,... | collective-permute-start | bytes 393224 | tf_op jit(solution)/shard_map/ppermute | solution.py:335
  35.2 4.1 %collective-permute-done.5.got_c = bf16[32,2048]{1,0:T(8,128)(2,1)S(1)} collective-permute-done((bf16[32,2048]{1,0:T(8,128)(2,1)S(1)}, bf16[32,2048]{1,0:T(8,128)(2,1)S(1)}, u32[]{:S(2)}, u32[]{:S(2)}) %collective-permute-start.5) | collective-permute-done | bytes 131104 | tf_op jit(solution)/shard_map/ppermute | solution.py:335
  39.3 0.0 collective-permute-done.3.got_a
  39.3 0.1 shard_map.100
  39.4 5.5 %collective-permute-start.6 = (bf16[32,2048]{1,0:T(8,128)(2,1)S(1)}, bf16[32,2048]{1,0:T(8,128)(2,1)S(1)}, u32[]{:S(2)}, u32[]{:S(2)}) collective-permute-start(bf16[32,2048]{1,0:T(8,128)(2,1)S(1)} %shard_map.100), channel_id=1, source_target_pairs={{0,6},{1,3},{2,0},{3,5},{4,2},{5,7},{6,4},{7,1},{8,10},{9,15},{10,... | collective-permute-start | bytes 393224 | tf_op jit(solution)/shard_map/ppermute | solution.py:335
  44.9 0.0 collective-permute-done.4.got_b
  44.9 1.9 %collective-permute-start.7 = (bf16[32,2048]{1,0:T(8,128)(2,1)S(1)}, bf16[32,2048]{1,0:T(8,128)(2,1)S(1)}, u32[]{:S(2)}, u32[]{:S(2)}) collective-permute-start(bf16[32,2048]{1,0:T(8,128)(2,1)S(1)} %shard_map.101), channel_id=1, source_target_pairs={{0,2},{1,7},{2,4},{3,1},{4,6},{5,3},{6,0},{7,5},{8,14},{9,11},{10,... | collective-permute-start | bytes 393224 | tf_op jit(solution)/shard_map/ppermute | solution.py:335
  46.8 1.4 %collective-permute-done.6.first = bf16[32,2048]{1,0:T(8,128)(2,1)S(1)} collective-permute-done((bf16[32,2048]{1,0:T(8,128)(2,1)S(1)}, bf16[32,2048]{1,0:T(8,128)(2,1)S(1)}, u32[]{:S(2)}, u32[]{:S(2)}) %collective-permute-start.6) | collective-permute-done | bytes 131104 | tf_op jit(solution)/shard_map/ppermute | solution.py:335
  48.2 5.7 %collective-permute-done.7.second = bf16[32,2048]{1,0:T(8,128)(2,1)S(1)} collective-permute-done((bf16[32,2048]{1,0:T(8,128)(2,1)S(1)}, bf16[32,2048]{1,0:T(8,128)(2,1)S(1)}, u32[]{:S(2)}, u32[]{:S(2)}) %collective-permute-start.7) | collective-permute-done | bytes 131104 | tf_op jit(solution)/shard_map/ppermute | solution.py:335
  53.9 0.7 %last.1 = bf16[32,2048]{1,0:T(8,128)(2,1)} custom-call(bf16[96,2048]{1,0:T(8,128)(2,1)S(1)} %get-tuple-element.35.rest, bf16[64,2048]{1,0:T(8,128)(2,1)S(1)} %collective-permute-done.3.got_a, bf16[64,2048]{1,0:T(8,128)(2,1)S(1)} %collective-permute-done.4.got_b, bf16[32,2048]{1,0:T(8,128)(2,1)S(1)} %collective-permute-done.6.first, ...), custom_call_target="tpu_custom_call" | custom-call | tf_op jit(solution)/shard_map/last/pallas_call | solution.py:352
  (1 shorter events, 0.0 us)
Async XLA Ops:
  0.0 9.3 %copy-start.2 = (s32[48]{0:T(128)S(1)}, s32[48]{0:T(128)}, u32[]{:S(2)}) copy-start(s32[48]{0:T(128)} %param.18) | copy-start | bytes 580
  0.0 9.3 %copy-start.3 = (f32[256]{0:T(256)S(1)}, f32[256]{0:T(256)}, u32[]{:S(2)}) copy-start(f32[256]{0:T(256)} %param.15) | copy-start | bytes 3076
  4.0 13.3 %collective-permute-start = (bf16[256,512]{1,0:T(8,128)(2,1)S(1)}, bf16[256,512]{1,0:T(8,128)(2,1)S(1)}, u32[]{:S(2)}, u32[]{:S(2)}) collective-permute-start(bf16[256,512]{1,0:T(8,128)(2,1)S(1)} %get-tuple-element.22.kv), channel_id=1, source_target_pairs={{0,16},{8,24},{16,32},{24,40},{32,48},{40,56},{48,64},{56,72},{64,... | collective-permute-start | bytes 786440 | tf_op jit(solution)/shard_map/ppermute | solution.py:280
  7.4 11.8 %collective-permute-start.1 = (bf16[256,512]{1,0:T(8,128)(2,1)S(1)}, bf16[256,512]{1,0:T(8,128)(2,1)S(1)}, u32[]{:S(2)}, u32[]{:S(2)}) collective-permute-start(bf16[256,512]{1,0:T(8,128)(2,1)S(1)} %get-tuple-element.22.kv), channel_id=1, source_target_pairs={{0,8},{8,0},{16,24},{24,16},{32,40},{40,32},{48,56},{56,48},{64,72... | collective-permute-start | bytes 786440 | tf_op jit(solution)/shard_map/ppermute | solution.py:281
  9.3 9.8 %copy-start.1 = (s32[96,3]{0,1:T(4,128)S(1)}, s32[96,3]{0,1:T(4,128)}, u32[]{:S(2)}) copy-start(s32[96,3]{0,1:T(4,128)} %param.19) | copy-start | bytes 3460
  9.3 11.3 %copy-start = (bf16[512,2048]{1,0:T(8,128)(2,1)S(1)}, bf16[512,2048]{1,0:T(8,128)(2,1)}, u32[]{:S(2)}) copy-start(bf16[512,2048]{1,0:T(8,128)(2,1)} %ow.1) | copy-start | bytes 6291460
  17.2 3.4 %collective-permute-start.2 = (bf16[256,512]{1,0:T(8,128)(2,1)S(1)}, bf16[256,512]{1,0:T(8,128)(2,1)S(1)}, u32[]{:S(2)}, u32[]{:S(2)}) collective-permute-start(bf16[256,512]{1,0:T(8,128)(2,1)S(1)} %collective-permute-done.near), channel_id=1, source_target_pairs={{0,8},{8,0},{16,24},{24,16},{32,40},{40,32},{48,56},{56,48},{64,72... | collective-permute-start | bytes 786440 | tf_op jit(solution)/shard_map/ppermute | solution.py:299
  22.5 16.8 %collective-permute-start.3 = (bf16[64,2048]{1,0:T(8,128)(2,1)S(1)}, bf16[64,2048]{1,0:T(8,128)(2,1)S(1)}, u32[]{:S(2)}, u32[]{:S(2)}) collective-permute-start(bf16[64,2048]{1,0:T(8,128)(2,1)S(1)} %get-tuple-element.36), channel_id=1, source_target_pairs={{0,1},{1,0},{2,3},{3,2},{4,5},{5,4},{6,7},{7,6},{8,15},{9,10},{10,... | collective-permute-start | bytes 786440 | tf_op jit(solution)/shard_map/ppermute | solution.py:335
  26.0 18.8 %collective-permute-start.4 = (bf16[64,2048]{1,0:T(8,128)(2,1)S(1)}, bf16[64,2048]{1,0:T(8,128)(2,1)S(1)}, u32[]{:S(2)}, u32[]{:S(2)}) collective-permute-start(bf16[64,2048]{1,0:T(8,128)(2,1)S(1)} %get-tuple-element.37), channel_id=1, source_target_pairs={{0,7},{1,2},{2,1},{3,4},{4,3},{5,6},{6,5},{7,0},{8,9},{9,8},{10,11... | collective-permute-start | bytes 786440 | tf_op jit(solution)/shard_map/ppermute | solution.py:335
  31.2 8.1 %collective-permute-start.5 = (bf16[32,2048]{1,0:T(8,128)(2,1)S(1)}, bf16[32,2048]{1,0:T(8,128)(2,1)S(1)}, u32[]{:S(2)}, u32[]{:S(2)}) collective-permute-start(bf16[32,2048]{1,0:T(8,128)(2,1)S(1)} %get-tuple-element.38), channel_id=1, source_target_pairs={{0,6},{1,3},{2,0},{3,5},{4,2},{5,7},{6,4},{7,1},{8,10},{9,15},{10,... | collective-permute-start | bytes 393224 | tf_op jit(solution)/shard_map/ppermute | solution.py:335
  39.4 8.9 %collective-permute-start.6 = (bf16[32,2048]{1,0:T(8,128)(2,1)S(1)}, bf16[32,2048]{1,0:T(8,128)(2,1)S(1)}, u32[]{:S(2)}, u32[]{:S(2)}) collective-permute-start(bf16[32,2048]{1,0:T(8,128)(2,1)S(1)} %shard_map.100), channel_id=1, source_target_pairs={{0,6},{1,3},{2,0},{3,5},{4,2},{5,7},{6,4},{7,1},{8,10},{9,15},{10,... | collective-permute-start | bytes 393224 | tf_op jit(solution)/shard_map/ppermute | solution.py:335
  44.9 9.0 %collective-permute-start.7 = (bf16[32,2048]{1,0:T(8,128)(2,1)S(1)}, bf16[32,2048]{1,0:T(8,128)(2,1)S(1)}, u32[]{:S(2)}, u32[]{:S(2)}) collective-permute-start(bf16[32,2048]{1,0:T(8,128)(2,1)S(1)} %shard_map.101), channel_id=1, source_target_pairs={{0,2},{1,7},{2,4},{3,1},{4,6},{5,3},{6,0},{7,5},{8,14},{9,11},{10,... | collective-permute-start | bytes 393224 | tf_op jit(solution)/shard_map/ppermute | solution.py:335

commit v5 on v4

--- a/solution.py
+++ b/solution.py
@@ -37,8 +37,11 @@
     return jnp.cos(angle), jnp.sin(angle) * jnp.where(lane < half, -1.0, 1.0)
 
 
-def doc_begin(starts, rows, base):
-    at = base + lax.broadcasted_iota(jnp.int32, (rows, starts.shape[1]), 0)
+def rows_from(base, rows):
+    return base + lax.broadcasted_iota(jnp.int32, (rows, 1), 0)
+
+
+def doc_begin(starts, at):
     return jnp.max(jnp.where(starts <= at, starts, 0), axis=1, keepdims=True)
 
 
@@ -53,7 +56,7 @@
     return front * cosine + partner * sine, x[:, 128:]
 
 
-def kv_body(head_dim, kv_share, starts_in, gain_in, tok_in, kw_in, vw_in, qw_in, gw_in, kv, trig, tok, qw, gw, starts, gain, kw, vw, sems):
+def kv_body(head_dim, kv_share, starts_in, gain_in, tok_in, kw_in, vw_in, qw_in, kv, trig, tok, qw, starts, gain, kw, vw, sems):
     rows = tok.shape[0]
     column = pl.multiple_of((lax.axis_index("head") // kv_share) * head_dim, head_dim)
     columns = pl.ds(column, head_dim)
@@ -68,15 +71,14 @@
         (kw_in.at[high, columns], kw.at[high, :]),
         (vw_in.at[:, columns], vw),
         (qw_in, qw),
-        (gw_in, gw),
     )
     copies = [pltpu.make_async_copy(a, b, sems.at[i]) for i, (a, b) in enumerate(pairs)]
-    for c in copies[:7]:
+    for c in copies:
         c.start()
     base = lax.axis_index("seq") * rows
     copies[0].wait()
-    begin = doc_begin(starts[...], rows, base)
-    offset = (base + lax.broadcasted_iota(jnp.int32, (rows, 1), 0) - begin).astype(F32)
+    at = rows_from(base, rows)
+    offset = (at - doc_begin(starts[...], at)).astype(F32)
     cosine, sine = rope_angles(offset, head_dim)
     trig[:, :128] = cosine
     trig[:, 128:] = sine
@@ -85,21 +87,24 @@
     key = jnp.dot(tok[:, :half], kw[:half, :], preferred_element_type=F32)
     for c in copies[4:6]:
         c.wait()
-    for c in copies[7:]:
-        c.start()
     key = key + jnp.dot(tok[:, half:], kw[half:, :], preferred_element_type=F32)
     copies[6].wait()
     kv[:, head_dim:] = jnp.dot(tok[...], vw[...], preferred_element_type=F32).astype(BF16)
     front, back = normed_rotated(key, gain[...], trig[:, :128], trig[:, 128:], head_dim // 8)
     kv[:, :128] = front.astype(BF16)
     kv[:, 128:head_dim] = back.astype(BF16)
-    for c in copies[7:]:
-        c.wait()
+    copies[7].wait()
 
 
 def attend(query, key, value, keep, scale):
     scores = lax.dot_general(query, key, (((1,), (1,)), ((), ())), preferred_element_type=F32)
-    weights = jnp.where(keep, jnp.exp(scores * scale), 0.0).astype(BF16)
+    rows = keep.shape[0]
+    weights = jnp.concatenate(
+        [
+            jnp.where(keep, jnp.exp(scores[i : i + rows] * scale), 0.0)
+            for i in range(0, query.shape[0], rows)
+        ]
+    ).astype(BF16)
     wide = weights.astype(F32)
     half = wide.shape[1] // 2
     return (
@@ -108,18 +113,16 @@
     )
 
 
-def kept(rows, width, query_base, key_base, begin):
-    at = query_base + lax.broadcasted_iota(jnp.int32, (rows, width), 0)
-    key = key_base + lax.broadcasted_iota(jnp.int32, (rows, width), 1)
+def kept(at, width, key_base, begin):
+    key = key_base + lax.broadcasted_iota(jnp.int32, (at.shape[0], width), 1)
     return (key <= at) & (key >= begin)
 
 
-def q_body(head_dim, starts, gain, trig, kv, tok, qw, gw, q_out, gate, num, den):
+def q_body(head_dim, starts, gain, trig, kv, tok, qw, gw_in, q_out, gate, num, den, gw, sem):
     rows = tok.shape[0]
     heads = qw.shape[1] // head_dim
-    base = lax.axis_index("seq") * rows
-    begin = doc_begin(starts[...], rows, base)
-    keep = kept(rows, rows, base, base, begin)
+    copy = pltpu.make_async_copy(gw_in, gw, sem)
+    copy.start()
     for i in range(heads):
         at = pl.ds(i * rows, rows)
         columns = slice(i * head_dim, (i + 1) * head_dim)
@@ -127,74 +130,90 @@
         front, back = normed_rotated(query, gain[...], trig[:, :128], trig[:, 128:], head_dim // 8)
         q_out[at, :128] = front.astype(BF16)
         q_out[at, 128:] = back.astype(BF16)
+    base = lax.axis_index("seq") * rows
+    at = rows_from(base, rows)
+    keep = kept(at, rows, base, doc_begin(starts[...], at))
+    copy.wait()
+    for i in range(heads):
+        columns = slice(i * head_dim, (i + 1) * head_dim)
         logits = jnp.dot(tok[...], gw[:, columns], preferred_element_type=F32)
-        gate[at, :] = 1.0 / (1.0 + jnp.exp(-logits))
-        weighted, sums = attend(
-            q_out[at, :], kv[:, :head_dim], kv[:, head_dim:], keep, head_dim ** (-0.5)
-        )
-        num[at, :] = weighted
-        den[at, :] = sums
-
-
-def source_mask(starts, readers, rows, source):
-    block = lax.axis_index("seq")
+        gate[pl.ds(i * rows, rows), :] = 1.0 / (1.0 + jnp.exp(-logits))
+    weighted, sums = attend(
+        q_out[...], kv[:, :head_dim], kv[:, head_dim:], keep, head_dim ** (-0.5)
+    )
+    num[...] = weighted
+    den[...] = sums
+
+
+def source_mask(starts, readers, at, width, source):
     span = readers.shape[0]
-    distance = block - source
+    distance = lax.axis_index("seq") - source
     inside = (source >= 0) & (distance >= 1) & (distance <= span)
     listed = readers[jnp.clip(distance - 1, 0, span - 1), jnp.maximum(source, 0)]
     first = jnp.where(inside & (listed == 1), 0, 1 << 30)
-    begin = doc_begin(starts[...], rows, block * rows)
-    return kept(rows, rows, block * rows, source * rows, jnp.maximum(begin, first))
-
-
-def attend_block(head_dim, query, block, keep, num_in, den_in, num, den):
-    rows = keep.shape[0]
-    for i in range(query.shape[0] // rows):
-        at = pl.ds(i * rows, rows)
-        weighted, sums = attend(
-            query[at, :], block[:, :head_dim], block[:, head_dim:], keep, head_dim ** (-0.5)
-        )
-        num[at, :] = num_in[at, :] + weighted
-        den[at, :] = den_in[at, :] + sums
+    begin = doc_begin(starts[...], at)
+    return kept(at, width, source * width, jnp.maximum(begin, first))
 
 
 def near_body(head_dim, starts, readers, query, num_in, den_in, near, own, num, den):
     rows = near.shape[0]
     block = lax.axis_index("seq")
-    core = lax.rem(block, 2)
-    keep = source_mask(starts, readers, rows, block - 2)
-    attend_block(head_dim, query, near, keep, num_in, den_in, num, den)
-
-    @pl.when(core == 1)
+    at = rows_from(block * rows, rows)
+
+    def add(keys, source, num_in, den_in):
+        keep = source_mask(starts, readers, at, rows, source)
+        weighted, sums = attend(
+            query[...], keys[:, :head_dim], keys[:, head_dim:], keep, head_dim ** (-0.5)
+        )
+        num[...] = num_in[...] + weighted
+        den[...] = den_in[...] + sums
+
+    add(near, block - 2, num_in, den_in)
+
+    @pl.when(lax.rem(block, 2) == 1)
     def _():
-        keep = source_mask(starts, readers, rows, block - 1)
-        attend_block(head_dim, query, own, keep, num, den, num, den)
-
-
-def out_body(head_dim, starts, readers, query, gate, num_in, den_in, far, ow, part_a, part_b, part_c, part_d, num, den, gated, turned):
+        add(own, block - 1, num, den)
+
+
+def out_body(head_dim, steps, starts, readers, query, gate, num, den, far, ow, *parts):
     rows = far.shape[0]
     heads = query.shape[0] // rows
     block = lax.axis_index("seq")
     core = lax.rem(block, 2)
     head = lax.axis_index("head")
-    keep = source_mask(starts, readers, rows, block - 1 - 2 * core)
-    attend_block(head_dim, query, far, keep, num_in, den_in, num, den)
-    for i in range(heads):
-        at = pl.ds(i * rows, rows)
-        total = jnp.sum(den[at, :], axis=1, keepdims=True)
-        gated[:, i * head_dim : (i + 1) * head_dim] = (num[at, :] / total * gate[at, :]).astype(BF16)
-    count = 8
+    count = len(ORDER)
     piece = rows // count
-    for i, step in enumerate(ORDER):
-        source = lax.rem(head + jnp.where(lax.rem(head + core, 2) == 0, step, count - step), count)
-        turned[i * piece : (i + 1) * piece, :] = gated[
-            pl.ds(pl.multiple_of(source * piece, piece), piece), :
-        ]
-    result = jnp.dot(turned[...], ow[...], preferred_element_type=F32).astype(BF16)
-    at = 0
-    for ref in (part_a, part_b, part_c, part_d):
-        ref[...] = result[at : at + ref.shape[0], :]
-        at += ref.shape[0]
+    even = lax.rem(head + core, 2) == 0
+    firsts = [
+        pl.multiple_of(lax.rem(head + jnp.where(even, step, count - step), count) * piece, piece)
+        for step in steps
+    ]
+
+    def gathered(ref):
+        return jnp.concatenate(
+            [ref[pl.ds(i * rows + first, piece), :] for i in range(heads) for first in firsts]
+        )
+
+    at = jnp.concatenate([rows_from(block * rows + first, piece) for first in firsts])
+    keep = source_mask(starts, readers, at, rows, block - 1 - 2 * core)
+    weighted, sums = attend(
+        gathered(query), far[:, :head_dim], far[:, head_dim:], keep, head_dim ** (-0.5)
+    )
+    total = jnp.sum(gathered(den) + sums, axis=1, keepdims=True)
+    gated = ((gathered(num) + weighted) / total * gathered(gate)).astype(BF16)
+    n = len(steps) * piece
+    result = sum(
+        jnp.dot(
+            gated[i * n : (i + 1) * n],
+            ow[i * head_dim : (i + 1) * head_dim, :],
+            preferred_element_type=F32,
+        )
+        for i in range(heads)
+    ).astype(BF16)
+    first = 0
+    for ref in parts:
+        ref[...] = result[first : first + ref.shape[0], :]
+        first += ref.shape[0]
 
 
 ORDER = (1, 3, 7, 5, 4, 6, 2, 0)
@@ -250,30 +269,29 @@
     def far_away(*arrays):
         return tuple(pltpu.with_memory_space_constraint(x, pltpu.HBM) for x in arrays)
 
-    own, trig, near_tokens, near_q, near_gate = pl.pallas_call(
+    own, trig, near_tokens, near_q = pl.pallas_call(
         functools.partial(kv_body, head_dim, kv_share),
         out_shape=(
             held(rows, 2 * head_dim),
             held(rows, 256, F32),
             held(rows, width),
             held(*q_weight.shape),
-            held(*gate_weight.shape),
         ),
-        in_specs=[HBM] * 7,
-        out_specs=(VMEM,) * 5,
+        in_specs=[HBM] * 6,
+        out_specs=(VMEM,) * 4,
         scratch_shapes=[
             pltpu.VMEM(starts.shape, jnp.int32),
             pltpu.VMEM((1, head_dim), F32),
             pltpu.VMEM((width, head_dim), BF16),
             pltpu.VMEM((width, head_dim), BF16),
-            pltpu.SemaphoreType.DMA((9,)),
+            pltpu.SemaphoreType.DMA((8,)),
         ],
         compiler_params=params(16),
-        cost_estimate=cost(4 * rows * width * head_dim, 7 << 20),
+        cost_estimate=cost(4 * rows * width * head_dim, 5 << 20),
         name="kv",
     )(
         *far_away(
-            starts, k_gain.reshape(1, -1), tokens, k_weight, v_weight, q_weight, gate_weight
+            starts, k_gain.reshape(1, -1), tokens, k_weight, v_weight, q_weight
         )
     )
 
@@ -288,12 +306,13 @@
             held(stacked, head_dim, F32),
             held(stacked, 128, F32),
         ),
-        in_specs=[VMEM] * 7,
+        in_specs=[VMEM] * 6 + [HBM],
         out_specs=(VMEM,) * 4,
+        scratch_shapes=[pltpu.VMEM(gate_weight.shape, BF16), pltpu.SemaphoreType.DMA],
         compiler_params=params(24),
         cost_estimate=cost(4 * rows * width * heads * head_dim, 5 << 20),
         name="query",
-    )(starts, q_gain.reshape(1, -1), trig, own, near_tokens, near_q, near_gate)
+    )(starts, q_gain.reshape(1, -1), trig, own, near_tokens, near_q, *far_away(gate_weight))
 
     near, query = lax.optimization_barrier((near, query))
     far = lax.ppermute(near, "seq", [(i, i ^ 1) for i in range(seq)])
@@ -310,21 +329,16 @@
     )(starts, table, query, num, den, near, below)
 
     piece = rows // head
-    part_a, part_b, part_c, rest = pl.pallas_call(
-        functools.partial(out_body, head_dim),
-        out_shape=tuple(held(n * piece, width) for n in (2, 2, 1, 3)),
-        in_specs=[VMEM, SMEM] + [VMEM] * 6,
-        out_specs=(VMEM,) * 4,
-        scratch_shapes=[
-            pltpu.VMEM((stacked, head_dim), F32),
-            pltpu.VMEM((stacked, 128), F32),
-            pltpu.VMEM((rows, heads * head_dim), BF16),
-            pltpu.VMEM((rows, heads * head_dim), BF16),
-        ],
-        compiler_params=params(24),
-        cost_estimate=cost(2 * rows * width * heads * head_dim, 4 << 20),
-        name="attend",
-    )(starts, table, query, gate, num, den, far, out_weight)
+
+    def made(steps, *sizes):
+        return pl.pallas_call(
+            functools.partial(out_body, head_dim, steps),
+            out_shape=tuple(held(n * piece, width) for n in sizes),
+            in_specs=[VMEM, SMEM] + [VMEM] * 6,
+            out_specs=(VMEM,) * len(sizes),
+            compiler_params=params(24),
+            cost_estimate=cost(2 * len(steps) * piece * width * heads * head_dim, 4 << 20),
+        )(starts, table, query, gate, num, den, far, out_weight)
 
     def turn(block, step):
         route = []
@@ -344,7 +358,9 @@
             cost_estimate=cost(4 * piece * width, 8 * piece * width),
         )(*blocks)
 
+    (part_a,) = made(ORDER[:2], 2)
     got_a = turn(part_a, 1)
+    part_b, part_c, rest = made(ORDER[2:], 2, 1, 3)
     got_c = turn(part_c, -2)
     got_b = turn(part_b, -1)
     first = turn(summed(first_body, rest, got_a, got_c), -2)

time: 54.9 us -> 52.7 us (0.960)
  the two profiles are of different devices: /device:TPU:512 before, /device:TPU:1 now
where the time goes in v5:
time: 52.7 us; the launch traced here: 52.4 us
  starting transfers between devices  28.8 us (55%)
  waiting for transfers between devices  11.9 us (23%)
  Pallas kernels  11.5 us (22%)
    ppermute x5, starting transfers between devices, turn(): return lax.ppermute(block, ('seq', 'head'), route)  13.1 us
    ppermute x5, waiting for transfers between devices, turn(): return lax.ppermute(block, ('seq', 'head'), route)  11.9 us
    ppermute x1, starting transfers between devices, shards(): below = lax.ppermute(own, 'seq', [(i, i ^ 1) for i in range(seq)])  9.74 us
    ppermute x1, starting transfers between devices, shards(): near = lax.ppermute(own, 'seq', [(i, i + 2) for i in range(seq - 2)])  3.95 us
    pallas_call x2, Pallas kernels, made(): pl.pallas_call(functools.partial(out_body, head_dim, steps), out_shape=tu...  3.09 us
    pallas_call x1, Pallas kernels, shards(): pl.pallas_call(functools.partial(kv_body, head_dim, kv_share), out_shape=...  3.03 us
    pallas_call x1, Pallas kernels, shards(): pl.pallas_call(functools.partial(q_body, head_dim), out_shape=(held(stack...  3 us
    ppermute x1, starting transfers between devices, shards(): far = lax.ppermute(near, 'seq', [(i, i ^ 1) for i in range(seq)])  1.92 us
  transfers between devices with their start and end apart: 8, of which 2 were waited for; matrix products, arithmetic and copies ran while one was open for 0% of the time, Pallas kernels for 12%

profile of v5, /device:TPU:1, one launch (start us, length us, event | category | flops | bytes accessed | tf_op | source)
XLA Modules:
  0.0 52.4 jit_solution(11779178501047771951)
XLA Ops:
  0.0 0.0 copy-start.2
  0.0 0.0 copy-start.3
  0.0 3.0 %kv.1 = (bf16[256,512]{1,0:T(8,128)(2,1)S(1)}, f32[256,256]{1,0:T(8,128)S(1)}, bf16[256,2048]{1,0:T(8,128)(2,1)S(1)}, bf16[2048,512]{1,0:T(8,128)(2,1)S(1)}) custom-call(s32[1,48]{1,0:T(1,128)} %bitcast.7, f32[1,256]{1,0:T(1,128)} %bitcast.13, bf16[256,2048]{1,0:T(8,128)(2,1)} %tok_in.1, bf16[2048,512]{1,0:T(8,128)(2,1)} %kw_in.1, bf16[2048,512]{1,0:T(8,128)(2,1)} %vw_in.1, ...), custom_call_target="tpu_custom_call" | custom-call | flops 536870912 | bytes 5242880 | tf_op jit(solution)/shard_map/kv/pallas_call | solution.py:272
  3.0 4.0 %collective-permute-start = (bf16[256,512]{1,0:T(8,128)(2,1)S(1)}, bf16[256,512]{1,0:T(8,128)(2,1)S(1)}, u32[]{:S(2)}, u32[]{:S(2)}) collective-permute-start(bf16[256,512]{1,0:T(8,128)(2,1)S(1)} %get-tuple-element.20.kv), channel_id=1, source_target_pairs={{0,16},{8,24},{16,32},{24,40},{32,48},{40,56},{48,64},{56,72},{64,... | collective-permute-start | bytes 786440 | tf_op jit(solution)/shard_map/ppermute | solution.py:298
  7.0 9.7 %collective-permute-start.1 = (bf16[256,512]{1,0:T(8,128)(2,1)S(1)}, bf16[256,512]{1,0:T(8,128)(2,1)S(1)}, u32[]{:S(2)}, u32[]{:S(2)}) collective-permute-start(bf16[256,512]{1,0:T(8,128)(2,1)S(1)} %get-tuple-element.20.kv), channel_id=1, source_target_pairs={{0,8},{8,0},{16,24},{24,16},{32,40},{40,32},{48,56},{56,48},{64,72... | collective-permute-start | bytes 786440 | tf_op jit(solution)/shard_map/ppermute | solution.py:299
  16.8 0.0 copy-done.2
  16.8 0.0 copy-done.3
  16.8 0.0 copy-start.1
  16.8 0.0 copy-start
  16.8 3.0 %query.1 = (bf16[512,256]{1,0:T(8,128)(2,1)S(1)}, f32[512,256]{1,0:T(8,128)S(1)}, f32[512,256]{1,0:T(8,128)S(1)}, f32[512,128]{1,0:T(8,128)S(1)}) custom-call(s32[1,48]{1,0:T(1,128)S(1)} %bitcast.8, f32[1,256]{1,0:T(1,128)S(1)} %bitcast.12, f32[256,256]{1,0:T(8,128)S(1)} %get-tuple-element.21.trig, bf16[256,512]{1,0:T(8,128)(2,1)S(1)} %get-tuple-element.20.kv, ...), custom_call_target="tpu_custom_call" | custom-call | flops 1073741824 | bytes 5242880 | tf_op jit(solution)/shard_map/query/pallas_call | solution.py:301
  19.8 0.0 collective-permute-done.near
  19.8 1.9 %collective-permute-start.2 = (bf16[256,512]{1,0:T(8,128)(2,1)S(1)}, bf16[256,512]{1,0:T(8,128)(2,1)S(1)}, u32[]{:S(2)}, u32[]{:S(2)}) collective-permute-start(bf16[256,512]{1,0:T(8,128)(2,1)S(1)} %collective-permute-done.near), channel_id=1, source_target_pairs={{0,8},{8,0},{16,24},{24,16},{32,40},{40,32},{48,56},{56,48},{64,72... | collective-permute-start | bytes 786440 | tf_op jit(solution)/shard_map/ppermute | solution.py:318
  21.7 0.0 collective-permute-done.1.own
  21.8 0.0 copy-done.1
  21.8 1.6 %near.1 = (f32[512,256]{1,0:T(8,128)S(1)}, f32[512,128]{1,0:T(8,128)S(1)}) custom-call(s32[1,48]{1,0:T(1,128)S(1)} %bitcast.9, s32[3,96]{1,0:T(4,128)S(1)} %bitcast.4, bf16[512,256]{1,0:T(8,128)(2,1)S(1)} %get-tuple-element.25.query, f32[512,256]{1,0:T(8,128)S(1)} %get-tuple-element.27.num_in, f32[512,128]{1,0:T(8,128)S(1)} %get-tuple-element.28.den_in, ...), custom_call_target="tpu_custom_call" | custom-call | flops 134217728 | bytes 3145728 | tf_op jit(solution)/shard_map/near/pallas_call | solution.py:321
  23.4 0.0 collective-permute-done.2.far
  23.4 0.0 copy-done
  23.4 1.7 %shard_map.100 = (bf16[64,2048]{1,0:T(8,128)(2,1)S(1)}, bf16[32,2048]{1,0:T(8,128)(2,1)S(1)}, bf16[96,2048]{1,0:T(8,128)(2,1)S(1)}) custom-call(s32[1,48]{1,0:T(1,128)S(1)} %bitcast.10, s32[3,96]{1,0:T(4,128)S(1)} %bitcast.5, bf16[512,256]{1,0:T(8,128)(2,1)S(1)} %get-tuple-element.25.query, f32[512,256]{1,0:T(8,128)S(1)} %get-tuple-element.26.gate, ...), custom_call_target="tpu_custom_call" | custom-call | flops 402653184 | bytes 4194304 | tf_op jit(solution)/shard_map/pallas_call | solution.py:334
  25.0 1.9 %collective-permute-start.4 = (bf16[64,2048]{1,0:T(8,128)(2,1)S(1)}, bf16[64,2048]{1,0:T(8,128)(2,1)S(1)}, u32[]{:S(2)}, u32[]{:S(2)}) collective-permute-start(bf16[64,2048]{1,0:T(8,128)(2,1)S(1)} %get-tuple-element.33), channel_id=1, source_target_pairs={{0,7},{1,2},{2,1},{3,4},{4,3},{5,6},{6,5},{7,0},{8,9},{9,8},{10,11... | collective-permute-start | bytes 786440 | tf_op jit(solution)/shard_map/ppermute | solution.py:349
  27.0 1.4 %shard_map.101 = bf16[64,2048]{1,0:T(8,128)(2,1)S(1)} custom-call(s32[1,48]{1,0:T(1,128)S(1)} %bitcast.11, s32[3,96]{1,0:T(4,128)S(1)} %bitcast.6, bf16[512,256]{1,0:T(8,128)(2,1)S(1)} %get-tuple-element.25.query, f32[512,256]{1,0:T(8,128)S(1)} %get-tuple-element.26.gate, f32[512,256]{1,0:T(8,128)S(1)} %get-tuple-element.30.num, ...), custom_call_target="tpu_custom_call" | custom-call | flops 134217728 | bytes 4194304 | tf_op jit(solution)/shard_map/pallas_call | solution.py:334
  28.4 1.9 %collective-permute-start.3 = (bf16[64,2048]{1,0:T(8,128)(2,1)S(1)}, bf16[64,2048]{1,0:T(8,128)(2,1)S(1)}, u32[]{:S(2)}, u32[]{:S(2)}) collective-permute-start(bf16[64,2048]{1,0:T(8,128)(2,1)S(1)} %shard_map.101), channel_id=1, source_target_pairs={{0,1},{1,0},{2,3},{3,2},{4,5},{5,4},{6,7},{7,6},{8,15},{9,10},{10,... | collective-permute-start | bytes 786440 | tf_op jit(solution)/shard_map/ppermute | solution.py:349
  30.3 4.5 %collective-permute-start.5 = (bf16[32,2048]{1,0:T(8,128)(2,1)S(1)}, bf16[32,2048]{1,0:T(8,128)(2,1)S(1)}, u32[]{:S(2)}, u32[]{:S(2)}) collective-permute-start(bf16[32,2048]{1,0:T(8,128)(2,1)S(1)} %get-tuple-element.34), channel_id=1, source_target_pairs={{0,6},{1,3},{2,0},{3,5},{4,2},{5,7},{6,4},{7,1},{8,10},{9,15},{10,... | collective-permute-start | bytes 393224 | tf_op jit(solution)/shard_map/ppermute | solution.py:349
  34.9 0.0 collective-permute-done.4.got_b
  34.9 2.9 %collective-permute-start.7 = (bf16[32,2048]{1,0:T(8,128)(2,1)S(1)}, bf16[32,2048]{1,0:T(8,128)(2,1)S(1)}, u32[]{:S(2)}, u32[]{:S(2)}) collective-permute-start(bf16[32,2048]{1,0:T(8,128)(2,1)S(1)} %shard_map.103), channel_id=1, source_target_pairs={{0,2},{1,7},{2,4},{3,1},{4,6},{5,3},{6,0},{7,5},{8,14},{9,11},{10,... | collective-permute-start | bytes 393224 | tf_op jit(solution)/shard_map/ppermute | solution.py:349
  37.8 4.6 %collective-permute-done.5.got_c = bf16[32,2048]{1,0:T(8,128)(2,1)S(1)} collective-permute-done((bf16[32,2048]{1,0:T(8,128)(2,1)S(1)}, bf16[32,2048]{1,0:T(8,128)(2,1)S(1)}, u32[]{:S(2)}, u32[]{:S(2)}) %collective-permute-start.5) | collective-permute-done | bytes 131104 | tf_op jit(solution)/shard_map/ppermute | solution.py:349
  42.4 0.0 collective-permute-done.3.got_a
  42.4 0.1 shard_map.102
  42.4 1.9 %collective-permute-start.6 = (bf16[32,2048]{1,0:T(8,128)(2,1)S(1)}, bf16[32,2048]{1,0:T(8,128)(2,1)S(1)}, u32[]{:S(2)}, u32[]{:S(2)}) collective-permute-start(bf16[32,2048]{1,0:T(8,128)(2,1)S(1)} %shard_map.102), channel_id=1, source_target_pairs={{0,6},{1,3},{2,0},{3,5},{4,2},{5,7},{6,4},{7,1},{8,10},{9,15},{10,... | collective-permute-start | bytes 393224 | tf_op jit(solution)/shard_map/ppermute | solution.py:349
  44.3 0.0 collective-permute-done.7.second
  44.4 7.3 %collective-permute-done.6.first = bf16[32,2048]{1,0:T(8,128)(2,1)S(1)} collective-permute-done((bf16[32,2048]{1,0:T(8,128)(2,1)S(1)}, bf16[32,2048]{1,0:T(8,128)(2,1)S(1)}, u32[]{:S(2)}, u32[]{:S(2)}) %collective-permute-start.6) | collective-permute-done | bytes 131104 | tf_op jit(solution)/shard_map/ppermute | solution.py:349
  51.6 0.7 %last.1 = bf16[32,2048]{1,0:T(8,128)(2,1)} custom-call(bf16[96,2048]{1,0:T(8,128)(2,1)S(1)} %get-tuple-element.32.rest, bf16[64,2048]{1,0:T(8,128)(2,1)S(1)} %collective-permute-done.3.got_a, bf16[64,2048]{1,0:T(8,128)(2,1)S(1)} %collective-permute-done.4.got_b, bf16[32,2048]{1,0:T(8,128)(2,1)S(1)} %collective-permute-done.6.first, ...), custom_call_target="tpu_custom_call" | custom-call | tf_op jit(solution)/shard_map/last/pallas_call | solution.py:368
  (1 shorter events, 0.0 us)
Async XLA Ops:
  0.0 16.8 %copy-start.2 = (s32[48]{0:T(128)S(1)}, s32[48]{0:T(128)}, u32[]{:S(2)}) copy-start(s32[48]{0:T(128)} %param.18) | copy-start | bytes 580
  0.0 16.8 %copy-start.3 = (f32[256]{0:T(256)S(1)}, f32[256]{0:T(256)}, u32[]{:S(2)}) copy-start(f32[256]{0:T(256)} %param.15) | copy-start | bytes 3076
  3.0 16.8 %collective-permute-start = (bf16[256,512]{1,0:T(8,128)(2,1)S(1)}, bf16[256,512]{1,0:T(8,128)(2,1)S(1)}, u32[]{:S(2)}, u32[]{:S(2)}) collective-permute-start(bf16[256,512]{1,0:T(8,128)(2,1)S(1)} %get-tuple-element.20.kv), channel_id=1, source_target_pairs={{0,16},{8,24},{16,32},{24,40},{32,48},{40,56},{48,64},{56,72},{64,... | collective-permute-start | bytes 786440 | tf_op jit(solution)/shard_map/ppermute | solution.py:298
  7.0 14.7 %collective-permute-start.1 = (bf16[256,512]{1,0:T(8,128)(2,1)S(1)}, bf16[256,512]{1,0:T(8,128)(2,1)S(1)}, u32[]{:S(2)}, u32[]{:S(2)}) collective-permute-start(bf16[256,512]{1,0:T(8,128)(2,1)S(1)} %get-tuple-element.20.kv), channel_id=1, source_target_pairs={{0,8},{8,0},{16,24},{24,16},{32,40},{40,32},{48,56},{56,48},{64,72... | collective-permute-start | bytes 786440 | tf_op jit(solution)/shard_map/ppermute | solution.py:299
  16.8 5.0 %copy-start.1 = (s32[96,3]{0,1:T(4,128)S(1)}, s32[96,3]{0,1:T(4,128)}, u32[]{:S(2)}) copy-start(s32[96,3]{0,1:T(4,128)} %param.19) | copy-start | bytes 3460
  16.8 6.6 %copy-start = (bf16[512,2048]{1,0:T(8,128)(2,1)S(1)}, bf16[512,2048]{1,0:T(8,128)(2,1)}, u32[]{:S(2)}) copy-start(bf16[512,2048]{1,0:T(8,128)(2,1)} %ow.3) | copy-start | bytes 6291460
  19.8 3.5 %collective-permute-start.2 = (bf16[256,512]{1,0:T(8,128)(2,1)S(1)}, bf16[256,512]{1,0:T(8,128)(2,1)S(1)}, u32[]{:S(2)}, u32[]{:S(2)}) collective-permute-start(bf16[256,512]{1,0:T(8,128)(2,1)S(1)} %collective-permute-done.near), channel_id=1, source_target_pairs={{0,8},{8,0},{16,24},{24,16},{32,40},{40,32},{48,56},{56,48},{64,72... | collective-permute-start | bytes 786440 | tf_op jit(solution)/shard_map/ppermute | solution.py:318
  25.0 9.8 %collective-permute-start.4 = (bf16[64,2048]{1,0:T(8,128)(2,1)S(1)}, bf16[64,2048]{1,0:T(8,128)(2,1)S(1)}, u32[]{:S(2)}, u32[]{:S(2)}) collective-permute-start(bf16[64,2048]{1,0:T(8,128)(2,1)S(1)} %get-tuple-element.33), channel_id=1, source_target_pairs={{0,7},{1,2},{2,1},{3,4},{4,3},{5,6},{6,5},{7,0},{8,9},{9,8},{10,11... | collective-permute-start | bytes 786440 | tf_op jit(solution)/shard_map/ppermute | solution.py:349
  28.4 14.0 %collective-permute-start.3 = (bf16[64,2048]{1,0:T(8,128)(2,1)S(1)}, bf16[64,2048]{1,0:T(8,128)(2,1)S(1)}, u32[]{:S(2)}, u32[]{:S(2)}) collective-permute-start(bf16[64,2048]{1,0:T(8,128)(2,1)S(1)} %shard_map.101), channel_id=1, source_target_pairs={{0,1},{1,0},{2,3},{3,2},{4,5},{5,4},{6,7},{7,6},{8,15},{9,10},{10,... | collective-permute-start | bytes 786440 | tf_op jit(solution)/shard_map/ppermute | solution.py:349
  30.3 12.0 %collective-permute-start.5 = (bf16[32,2048]{1,0:T(8,128)(2,1)S(1)}, bf16[32,2048]{1,0:T(8,128)(2,1)S(1)}, u32[]{:S(2)}, u32[]{:S(2)}) collective-permute-start(bf16[32,2048]{1,0:T(8,128)(2,1)S(1)} %get-tuple-element.34), channel_id=1, source_target_pairs={{0,6},{1,3},{2,0},{3,5},{4,2},{5,7},{6,4},{7,1},{8,10},{9,15},{10,... | collective-permute-start | bytes 393224 | tf_op jit(solution)/shard_map/ppermute | solution.py:349
  34.9 9.4 %collective-permute-start.7 = (bf16[32,2048]{1,0:T(8,128)(2,1)S(1)}, bf16[32,2048]{1,0:T(8,128)(2,1)S(1)}, u32[]{:S(2)}, u32[]{:S(2)}) collective-permute-start(bf16[32,2048]{1,0:T(8,128)(2,1)S(1)} %shard_map.103), channel_id=1, source_target_pairs={{0,2},{1,7},{2,4},{3,1},{4,6},{5,3},{6,0},{7,5},{8,14},{9,11},{10,... | collective-permute-start | bytes 393224 | tf_op jit(solution)/shard_map/ppermute | solution.py:349
  42.4 9.2 %collective-permute-start.6 = (bf16[32,2048]{1,0:T(8,128)(2,1)S(1)}, bf16[32,2048]{1,0:T(8,128)(2,1)S(1)}, u32[]{:S(2)}, u32[]{:S(2)}) collective-permute-start(bf16[32,2048]{1,0:T(8,128)(2,1)S(1)} %shard_map.102), channel_id=1, source_target_pairs={{0,6},{1,3},{2,0},{3,5},{4,2},{5,7},{6,4},{7,1},{8,10},{9,15},{10,... | collective-permute-start | bytes 393224 | tf_op jit(solution)/shard_map/ppermute | solution.py:349

commit v6 on v5

--- a/solution.py
+++ b/solution.py
@@ -219,15 +219,16 @@
 ORDER = (1, 3, 7, 5, 4, 6, 2, 0)
 
 
-def first_body(rest, got_a, got_c, out):
+def first_body(rest, got_a, out):
     piece = out.shape[0]
-    total = rest[:piece, :].astype(F32) + got_a[piece:, :].astype(F32) + got_c[...].astype(F32)
+    total = rest[:piece, :].astype(F32) + got_a[piece:, :].astype(F32)
     out[...] = total.astype(BF16)
 
 
-def second_body(rest, got_b, out):
+def second_body(rest, got_b, got_c, out):
     piece = out.shape[0]
-    total = rest[piece : 2 * piece, :].astype(F32) + got_b[piece:, :].astype(F32)
+    total = rest[piece : 2 * piece, :].astype(F32)
+    total = total + got_b[piece:, :].astype(F32) + got_c[...].astype(F32)
     out[...] = total.astype(BF16)
 
 
@@ -358,13 +359,12 @@
             cost_estimate=cost(4 * piece * width, 8 * piece * width),
         )(*blocks)
 
-    (part_a,) = made(ORDER[:2], 2)
+    part_a, part_b, part_c, rest = made(ORDER, 2, 2, 1, 3)
     got_a = turn(part_a, 1)
-    part_b, part_c, rest = made(ORDER[2:], 2, 1, 3)
-    got_c = turn(part_c, -2)
+    got_c = turn(part_c, 2)
     got_b = turn(part_b, -1)
-    first = turn(summed(first_body, rest, got_a, got_c), -2)
-    second = turn(summed(second_body, rest, got_b), 2)
+    first = turn(summed(first_body, rest, got_a), -2)
+    second = turn(summed(second_body, rest, got_b, got_c), 2)
     return pl.pallas_call(
         last_body,
         out_shape=shape(piece, width),

time: 52.7 us -> 49.7 us (0.943)
  waiting for transfers between devices: 11.9 us -> 5.58 us
  starting transfers between devices: 28.8 us -> 33.3 us
  Pallas kernels: 11.5 us -> 10.3 us
    ppermute x5, waiting for transfers between devices: 11.9 us -> 5.57 us  [turn(): return lax.ppermute(block, ('seq', 'head'), route)]
    ppermute x5, starting transfers between devices: 13.1 us -> 17.7 us  [turn(): return lax.ppermute(block, ('seq', 'head'), route)]
    pallas_call x2 -> x1, Pallas kernels: 3.09 us -> 1.86 us  [made(): pl.pallas_call(functools.partial(out_body, head_dim, steps), out_shape=tu...]
  transfers between devices with their start and end apart: 8 -> 8, of which waited for: 2 -> 2; matrix products, arithmetic and copies ran while one was open for 0% -> 0% of each run, Pallas kernels for 12% -> 9%
where the time goes in v6:
time: 49.7 us; the launch traced here: 49.4 us
  starting transfers between devices  33.3 us (67%)
  Pallas kernels  10.3 us (21%)
  waiting for transfers between devices  5.58 us (11%)
    ppermute x5, starting transfers between devices, turn(): return lax.ppermute(block, ('seq', 'head'), route)  17.7 us
    ppermute x1, starting transfers between devices, shards(): below = lax.ppermute(own, 'seq', [(i, i ^ 1) for i in range(seq)])  9.74 us
    ppermute x5, waiting for transfers between devices, turn(): return lax.ppermute(block, ('seq', 'head'), route)  5.57 us
    ppermute x1, starting transfers between devices, shards(): near = lax.ppermute(own, 'seq', [(i, i + 2) for i in range(seq - 2)])  3.95 us
    pallas_call x1, Pallas kernels, shards(): pl.pallas_call(functools.partial(kv_body, head_dim, kv_share), out_shape=...  3.03 us
    pallas_call x1, Pallas kernels, shards(): pl.pallas_call(functools.partial(q_body, head_dim), out_shape=(held(stack...  3 us
    ppermute x1, starting transfers between devices, shards(): far = lax.ppermute(near, 'seq', [(i, i ^ 1) for i in range(seq)])  1.92 us
    pallas_call x1, Pallas kernels, made(): pl.pallas_call(functools.partial(out_body, head_dim, steps), out_shape=tu...  1.86 us
  transfers between devices with their start and end apart: 8, of which 2 were waited for; matrix products, arithmetic and copies ran while one was open for 0% of the time, Pallas kernels for 9%

profile of v6, /device:TPU:1, one launch (start us, length us, event | category | flops | bytes accessed | tf_op | source)
XLA Modules:
  0.0 49.4 jit_solution(10114509890827629399)
XLA Ops:
  0.0 0.0 copy-start.2
  0.0 0.0 copy-start.3
  0.0 3.0 %kv.1 = (bf16[256,512]{1,0:T(8,128)(2,1)S(1)}, f32[256,256]{1,0:T(8,128)S(1)}, bf16[256,2048]{1,0:T(8,128)(2,1)S(1)}, bf16[2048,512]{1,0:T(8,128)(2,1)S(1)}) custom-call(s32[1,48]{1,0:T(1,128)} %bitcast.6, f32[1,256]{1,0:T(1,128)} %bitcast.11, bf16[256,2048]{1,0:T(8,128)(2,1)} %tok_in.1, bf16[2048,512]{1,0:T(8,128)(2,1)} %kw_in.1, bf16[2048,512]{1,0:T(8,128)(2,1)} %vw_in.1, ...), custom_call_target="tpu_custom_call" | custom-call | flops 536870912 | bytes 5242880 | tf_op jit(solution)/shard_map/kv/pallas_call | solution.py:273
  3.0 4.0 %collective-permute-start = (bf16[256,512]{1,0:T(8,128)(2,1)S(1)}, bf16[256,512]{1,0:T(8,128)(2,1)S(1)}, u32[]{:S(2)}, u32[]{:S(2)}) collective-permute-start(bf16[256,512]{1,0:T(8,128)(2,1)S(1)} %get-tuple-element.21.kv), channel_id=1, source_target_pairs={{0,16},{8,24},{16,32},{24,40},{32,48},{40,56},{48,64},{56,72},{64,... | collective-permute-start | bytes 786440 | tf_op jit(solution)/shard_map/ppermute | solution.py:299
  7.0 9.7 %collective-permute-start.1 = (bf16[256,512]{1,0:T(8,128)(2,1)S(1)}, bf16[256,512]{1,0:T(8,128)(2,1)S(1)}, u32[]{:S(2)}, u32[]{:S(2)}) collective-permute-start(bf16[256,512]{1,0:T(8,128)(2,1)S(1)} %get-tuple-element.21.kv), channel_id=1, source_target_pairs={{0,8},{8,0},{16,24},{24,16},{32,40},{40,32},{48,56},{56,48},{64,72... | collective-permute-start | bytes 786440 | tf_op jit(solution)/shard_map/ppermute | solution.py:300
  16.8 0.0 copy-done.2
  16.8 0.0 copy-done.3
  16.8 0.0 copy-start.1
  16.8 0.0 copy-start
  16.8 3.0 %query.1 = (bf16[512,256]{1,0:T(8,128)(2,1)S(1)}, f32[512,256]{1,0:T(8,128)S(1)}, f32[512,256]{1,0:T(8,128)S(1)}, f32[512,128]{1,0:T(8,128)S(1)}) custom-call(s32[1,48]{1,0:T(1,128)S(1)} %bitcast.7, f32[1,256]{1,0:T(1,128)S(1)} %bitcast.10, f32[256,256]{1,0:T(8,128)S(1)} %get-tuple-element.22.trig, bf16[256,512]{1,0:T(8,128)(2,1)S(1)} %get-tuple-element.21.kv, ...), custom_call_target="tpu_custom_call" | custom-call | flops 1073741824 | bytes 5242880 | tf_op jit(solution)/shard_map/query/pallas_call | solution.py:302
  19.8 0.0 collective-permute-done.near
  19.8 1.9 %collective-permute-start.2 = (bf16[256,512]{1,0:T(8,128)(2,1)S(1)}, bf16[256,512]{1,0:T(8,128)(2,1)S(1)}, u32[]{:S(2)}, u32[]{:S(2)}) collective-permute-start(bf16[256,512]{1,0:T(8,128)(2,1)S(1)} %collective-permute-done.near), channel_id=1, source_target_pairs={{0,8},{8,0},{16,24},{24,16},{32,40},{40,32},{48,56},{56,48},{64,72... | collective-permute-start | bytes 786440 | tf_op jit(solution)/shard_map/ppermute | solution.py:319
  21.7 0.0 collective-permute-done.1.own
  21.8 0.0 copy-done.1
  21.8 1.6 %near.1 = (f32[512,256]{1,0:T(8,128)S(1)}, f32[512,128]{1,0:T(8,128)S(1)}) custom-call(s32[1,48]{1,0:T(1,128)S(1)} %bitcast.8, s32[3,96]{1,0:T(4,128)S(1)} %bitcast.4, bf16[512,256]{1,0:T(8,128)(2,1)S(1)} %get-tuple-element.26.query, f32[512,256]{1,0:T(8,128)S(1)} %get-tuple-element.28.num_in, f32[512,128]{1,0:T(8,128)S(1)} %get-tuple-element.29.den_in, ...), custom_call_target="tpu_custom_call" | custom-call | flops 134217728 | bytes 3145728 | tf_op jit(solution)/shard_map/near/pallas_call | solution.py:322
  23.4 0.0 collective-permute-done.2.far
  23.4 0.0 copy-done
  23.4 1.9 %shard_map.100 = (bf16[64,2048]{1,0:T(8,128)(2,1)S(1)}, bf16[64,2048]{1,0:T(8,128)(2,1)S(1)}, bf16[32,2048]{1,0:T(8,128)(2,1)S(1)}, bf16[96,2048]{1,0:T(8,128)(2,1)S(1)}) custom-call(s32[1,48]{1,0:T(1,128)S(1)} %bitcast.9, s32[3,96]{1,0:T(4,128)S(1)} %bitcast.5, bf16[512,256]{1,0:T(8,128)(2,1)S(1)} %get-tuple-element.26.query, ...), custom_call_target="tpu_custom_call" | custom-call | flops 536870912 | bytes 4194304 | tf_op jit(solution)/shard_map/pallas_call | solution.py:335
  25.2 1.9 %collective-permute-start.3 = (bf16[64,2048]{1,0:T(8,128)(2,1)S(1)}, bf16[64,2048]{1,0:T(8,128)(2,1)S(1)}, u32[]{:S(2)}, u32[]{:S(2)}) collective-permute-start(bf16[64,2048]{1,0:T(8,128)(2,1)S(1)} %get-tuple-element.34), channel_id=1, source_target_pairs={{0,1},{1,0},{2,3},{3,2},{4,5},{5,4},{6,7},{7,6},{8,15},{9,10},{10,... | collective-permute-start | bytes 786440 | tf_op jit(solution)/shard_map/ppermute | solution.py:350
  27.2 1.9 %collective-permute-start.4 = (bf16[64,2048]{1,0:T(8,128)(2,1)S(1)}, bf16[64,2048]{1,0:T(8,128)(2,1)S(1)}, u32[]{:S(2)}, u32[]{:S(2)}) collective-permute-start(bf16[64,2048]{1,0:T(8,128)(2,1)S(1)} %get-tuple-element.35), channel_id=1, source_target_pairs={{0,7},{1,2},{2,1},{3,4},{4,3},{5,6},{6,5},{7,0},{8,9},{9,8},{10,11... | collective-permute-start | bytes 786440 | tf_op jit(solution)/shard_map/ppermute | solution.py:350
  29.1 5.7 %collective-permute-start.6 = (bf16[32,2048]{1,0:T(8,128)(2,1)S(1)}, bf16[32,2048]{1,0:T(8,128)(2,1)S(1)}, u32[]{:S(2)}, u32[]{:S(2)}) collective-permute-start(bf16[32,2048]{1,0:T(8,128)(2,1)S(1)} %get-tuple-element.36), channel_id=1, source_target_pairs={{0,2},{1,7},{2,4},{3,1},{4,6},{5,3},{6,0},{7,5},{8,14},{9,11},{10,... | collective-permute-start | bytes 393224 | tf_op jit(solution)/shard_map/ppermute | solution.py:350
  34.8 0.0 collective-permute-done.3.got_a
  34.9 1.9 %collective-permute-start.5 = (bf16[32,2048]{1,0:T(8,128)(2,1)S(1)}, bf16[32,2048]{1,0:T(8,128)(2,1)S(1)}, u32[]{:S(2)}, u32[]{:S(2)}) collective-permute-start(bf16[32,2048]{1,0:T(8,128)(2,1)S(1)} %shard_map.101), channel_id=1, source_target_pairs={{0,6},{1,3},{2,0},{3,5},{4,2},{5,7},{6,4},{7,1},{8,10},{9,15},{10,... | collective-permute-start | bytes 393224 | tf_op jit(solution)/shard_map/ppermute | solution.py:350
  36.8 3.1 %collective-permute-done.6.got_c = bf16[32,2048]{1,0:T(8,128)(2,1)S(1)} collective-permute-done((bf16[32,2048]{1,0:T(8,128)(2,1)S(1)}, bf16[32,2048]{1,0:T(8,128)(2,1)S(1)}, u32[]{:S(2)}, u32[]{:S(2)}) %collective-permute-start.6) | collective-permute-done | bytes 131104 | tf_op jit(solution)/shard_map/ppermute | solution.py:350
  39.9 0.0 collective-permute-done.4.got_b
  39.9 0.1 shard_map.102
  40.0 6.2 %collective-permute-start.7 = (bf16[32,2048]{1,0:T(8,128)(2,1)S(1)}, bf16[32,2048]{1,0:T(8,128)(2,1)S(1)}, u32[]{:S(2)}, u32[]{:S(2)}) collective-permute-start(bf16[32,2048]{1,0:T(8,128)(2,1)S(1)} %shard_map.102), channel_id=1, source_target_pairs={{0,2},{1,7},{2,4},{3,1},{4,6},{5,3},{6,0},{7,5},{8,14},{9,11},{10,... | collective-permute-start | bytes 393224 | tf_op jit(solution)/shard_map/ppermute | solution.py:350
  46.2 0.0 collective-permute-done.5.first
  46.2 2.5 %collective-permute-done.7.second = bf16[32,2048]{1,0:T(8,128)(2,1)S(1)} collective-permute-done((bf16[32,2048]{1,0:T(8,128)(2,1)S(1)}, bf16[32,2048]{1,0:T(8,128)(2,1)S(1)}, u32[]{:S(2)}, u32[]{:S(2)}) %collective-permute-start.7) | collective-permute-done | bytes 131104 | tf_op jit(solution)/shard_map/ppermute | solution.py:350
  48.7 0.7 %last.1 = bf16[32,2048]{1,0:T(8,128)(2,1)} custom-call(bf16[96,2048]{1,0:T(8,128)(2,1)S(1)} %get-tuple-element.33.rest, bf16[64,2048]{1,0:T(8,128)(2,1)S(1)} %collective-permute-done.3.got_a, bf16[64,2048]{1,0:T(8,128)(2,1)S(1)} %collective-permute-done.4.got_b, bf16[32,2048]{1,0:T(8,128)(2,1)S(1)} %collective-permute-done.5.first, ...), custom_call_target="tpu_custom_call" | custom-call | tf_op jit(solution)/shard_map/last/pallas_call | solution.py:368
  (1 shorter events, 0.0 us)
Async XLA Ops:
  0.0 16.8 %copy-start.2 = (s32[48]{0:T(128)S(1)}, s32[48]{0:T(128)}, u32[]{:S(2)}) copy-start(s32[48]{0:T(128)} %param.18) | copy-start | bytes 580
  0.0 16.8 %copy-start.3 = (f32[256]{0:T(256)S(1)}, f32[256]{0:T(256)}, u32[]{:S(2)}) copy-start(f32[256]{0:T(256)} %param.15) | copy-start | bytes 3076
  3.0 16.8 %collective-permute-start = (bf16[256,512]{1,0:T(8,128)(2,1)S(1)}, bf16[256,512]{1,0:T(8,128)(2,1)S(1)}, u32[]{:S(2)}, u32[]{:S(2)}) collective-permute-start(bf16[256,512]{1,0:T(8,128)(2,1)S(1)} %get-tuple-element.21.kv), channel_id=1, source_target_pairs={{0,16},{8,24},{16,32},{24,40},{32,48},{40,56},{48,64},{56,72},{64,... | collective-permute-start | bytes 786440 | tf_op jit(solution)/shard_map/ppermute | solution.py:299
  7.0 14.7 %collective-permute-start.1 = (bf16[256,512]{1,0:T(8,128)(2,1)S(1)}, bf16[256,512]{1,0:T(8,128)(2,1)S(1)}, u32[]{:S(2)}, u32[]{:S(2)}) collective-permute-start(bf16[256,512]{1,0:T(8,128)(2,1)S(1)} %get-tuple-element.21.kv), channel_id=1, source_target_pairs={{0,8},{8,0},{16,24},{24,16},{32,40},{40,32},{48,56},{56,48},{64,72... | collective-permute-start | bytes 786440 | tf_op jit(solution)/shard_map/ppermute | solution.py:300
  16.8 5.0 %copy-start.1 = (s32[96,3]{0,1:T(4,128)S(1)}, s32[96,3]{0,1:T(4,128)}, u32[]{:S(2)}) copy-start(s32[96,3]{0,1:T(4,128)} %param.19) | copy-start | bytes 3460
  16.8 6.6 %copy-start = (bf16[512,2048]{1,0:T(8,128)(2,1)S(1)}, bf16[512,2048]{1,0:T(8,128)(2,1)}, u32[]{:S(2)}) copy-start(bf16[512,2048]{1,0:T(8,128)(2,1)} %ow.1) | copy-start | bytes 6291460
  19.8 3.5 %collective-permute-start.2 = (bf16[256,512]{1,0:T(8,128)(2,1)S(1)}, bf16[256,512]{1,0:T(8,128)(2,1)S(1)}, u32[]{:S(2)}, u32[]{:S(2)}) collective-permute-start(bf16[256,512]{1,0:T(8,128)(2,1)S(1)} %collective-permute-done.near), channel_id=1, source_target_pairs={{0,8},{8,0},{16,24},{24,16},{32,40},{40,32},{48,56},{56,48},{64,72... | collective-permute-start | bytes 786440 | tf_op jit(solution)/shard_map/ppermute | solution.py:319
  25.2 9.6 %collective-permute-start.3 = (bf16[64,2048]{1,0:T(8,128)(2,1)S(1)}, bf16[64,2048]{1,0:T(8,128)(2,1)S(1)}, u32[]{:S(2)}, u32[]{:S(2)}) collective-permute-start(bf16[64,2048]{1,0:T(8,128)(2,1)S(1)} %get-tuple-element.34), channel_id=1, source_target_pairs={{0,1},{1,0},{2,3},{3,2},{4,5},{5,4},{6,7},{7,6},{8,15},{9,10},{10,... | collective-permute-start | bytes 786440 | tf_op jit(solution)/shard_map/ppermute | solution.py:350
  27.2 12.8 %collective-permute-start.4 = (bf16[64,2048]{1,0:T(8,128)(2,1)S(1)}, bf16[64,2048]{1,0:T(8,128)(2,1)S(1)}, u32[]{:S(2)}, u32[]{:S(2)}) collective-permute-start(bf16[64,2048]{1,0:T(8,128)(2,1)S(1)} %get-tuple-element.35), channel_id=1, source_target_pairs={{0,7},{1,2},{2,1},{3,4},{4,3},{5,6},{6,5},{7,0},{8,9},{9,8},{10,11... | collective-permute-start | bytes 786440 | tf_op jit(solution)/shard_map/ppermute | solution.py:350
  29.1 10.8 %collective-permute-start.6 = (bf16[32,2048]{1,0:T(8,128)(2,1)S(1)}, bf16[32,2048]{1,0:T(8,128)(2,1)S(1)}, u32[]{:S(2)}, u32[]{:S(2)}) collective-permute-start(bf16[32,2048]{1,0:T(8,128)(2,1)S(1)} %get-tuple-element.36), channel_id=1, source_target_pairs={{0,2},{1,7},{2,4},{3,1},{4,6},{5,3},{6,0},{7,5},{8,14},{9,11},{10,... | collective-permute-start | bytes 393224 | tf_op jit(solution)/shard_map/ppermute | solution.py:350
  34.9 11.3 %collective-permute-start.5 = (bf16[32,2048]{1,0:T(8,128)(2,1)S(1)}, bf16[32,2048]{1,0:T(8,128)(2,1)S(1)}, u32[]{:S(2)}, u32[]{:S(2)}) collective-permute-start(bf16[32,2048]{1,0:T(8,128)(2,1)S(1)} %shard_map.101), channel_id=1, source_target_pairs={{0,6},{1,3},{2,0},{3,5},{4,2},{5,7},{6,4},{7,1},{8,10},{9,15},{10,... | collective-permute-start | bytes 393224 | tf_op jit(solution)/shard_map/ppermute | solution.py:350
  40.0 8.7 %collective-permute-start.7 = (bf16[32,2048]{1,0:T(8,128)(2,1)S(1)}, bf16[32,2048]{1,0:T(8,128)(2,1)S(1)}, u32[]{:S(2)}, u32[]{:S(2)}) collective-permute-start(bf16[32,2048]{1,0:T(8,128)(2,1)S(1)} %shard_map.102), channel_id=1, source_target_pairs={{0,2},{1,7},{2,4},{3,1},{4,6},{5,3},{6,0},{7,5},{8,14},{9,11},{10,... | collective-permute-start | bytes 393224 | tf_op jit(solution)/shard_map/ppermute | solution.py:350

commit v7 on v6

--- a/solution.py
+++ b/solution.py
@@ -221,21 +221,21 @@
 
 def first_body(rest, got_a, out):
     piece = out.shape[0]
-    total = rest[:piece, :].astype(F32) + got_a[piece:, :].astype(F32)
+    total = rest[:piece, :].astype(F32) + got_a[piece : 2 * piece, :].astype(F32)
     out[...] = total.astype(BF16)
 
 
-def second_body(rest, got_b, got_c, out):
+def second_body(rest, got_a, got_b, got_c, out):
     piece = out.shape[0]
-    total = rest[piece : 2 * piece, :].astype(F32)
-    total = total + got_b[piece:, :].astype(F32) + got_c[...].astype(F32)
+    total = rest[piece : 2 * piece, :].astype(F32) + got_a[2 * piece :, :].astype(F32)
+    total = total + got_b[...].astype(F32) + got_c[...].astype(F32)
     out[...] = total.astype(BF16)
 
 
-def last_body(rest, got_a, got_b, first, second, out):
+def last_body(rest, got_a, first, second, out):
     piece = out.shape[0]
     total = rest[2 * piece :, :].astype(F32)
-    for ref in (got_a, got_b, first, second):
+    for ref in (got_a, first, second):
         total = total + ref[:piece, :].astype(F32)
     out[...] = total.astype(BF16)
 
@@ -359,20 +359,20 @@
             cost_estimate=cost(4 * piece * width, 8 * piece * width),
         )(*blocks)
 
-    part_a, part_b, part_c, rest = made(ORDER, 2, 2, 1, 3)
+    part_a, part_b, part_c, rest = made(ORDER, 3, 1, 1, 3)
     got_a = turn(part_a, 1)
     got_c = turn(part_c, 2)
     got_b = turn(part_b, -1)
     first = turn(summed(first_body, rest, got_a), -2)
-    second = turn(summed(second_body, rest, got_b, got_c), 2)
+    second = turn(summed(second_body, rest, got_a, got_b, got_c), 2)
     return pl.pallas_call(
         last_body,
         out_shape=shape(piece, width),
-        in_specs=[VMEM] * 5,
+        in_specs=[VMEM] * 4,
         out_specs=VMEM,
         compiler_params=params(8),
         name="last",
-    )(rest, got_a, got_b, first, second)
+    )(rest, got_a, first, second)
 
 
 def solution(mesh):

time: 49.7 us -> 49.8 us (level); the launches traced: 49.4 us -> 48.9 us
  starting transfers between devices: 33.3 us -> 32.6 us
    ppermute x5, starting transfers between devices: 17.7 us -> 17 us  [turn(): return lax.ppermute(block, ('seq', 'head'), route)]
  transfers between devices with their start and end apart: 8 -> 8, of which waited for: 2 -> 3; matrix products, arithmetic and copies ran while one was open for 0% -> 0% of each run, Pallas kernels for 9% -> 10%
where the time goes in v7:
time: 49.8 us; the launch traced here: 48.9 us
  starting transfers between devices  32.6 us (65%)
  Pallas kernels  10.3 us (21%)
  waiting for transfers between devices  5.84 us (12%)
    ppermute x5, starting transfers between devices, turn(): return lax.ppermute(block, ('seq', 'head'), route)  17 us
    ppermute x1, starting transfers between devices, shards(): below = lax.ppermute(own, 'seq', [(i, i ^ 1) for i in range(seq)])  9.74 us
    ppermute x5, waiting for transfers between devices, turn(): return lax.ppermute(block, ('seq', 'head'), route)  5.83 us
    ppermute x1, starting transfers between devices, shards(): near = lax.ppermute(own, 'seq', [(i, i + 2) for i in range(seq - 2)])  3.95 us
    pallas_call x1, Pallas kernels, shards(): pl.pallas_call(functools.partial(kv_body, head_dim, kv_share), out_shape=...  3.03 us
    pallas_call x1, Pallas kernels, shards(): pl.pallas_call(functools.partial(q_body, head_dim), out_shape=(held(stack...  3 us
    ppermute x1, starting transfers between devices, shards(): far = lax.ppermute(near, 'seq', [(i, i ^ 1) for i in range(seq)])  1.92 us
    pallas_call x1, Pallas kernels, made(): pl.pallas_call(functools.partial(out_body, head_dim, steps), out_shape=tu...  1.86 us
  transfers between devices with their start and end apart: 8, of which 3 were waited for; matrix products, arithmetic and copies ran while one was open for 0% of the time, Pallas kernels for 10%

profile of v7, /device:TPU:1, one launch (start us, length us, event | category | flops | bytes accessed | tf_op | source)
XLA Modules:
  0.0 48.9 jit_solution(15473731844173404074)
XLA Ops:
  0.0 0.0 copy-start.2
  0.0 0.0 copy-start.3
  0.0 3.0 %kv.1 = (bf16[256,512]{1,0:T(8,128)(2,1)S(1)}, f32[256,256]{1,0:T(8,128)S(1)}, bf16[256,2048]{1,0:T(8,128)(2,1)S(1)}, bf16[2048,512]{1,0:T(8,128)(2,1)S(1)}) custom-call(s32[1,48]{1,0:T(1,128)} %bitcast.6, f32[1,256]{1,0:T(1,128)} %bitcast.11, bf16[256,2048]{1,0:T(8,128)(2,1)} %tok_in.1, bf16[2048,512]{1,0:T(8,128)(2,1)} %kw_in.1, bf16[2048,512]{1,0:T(8,128)(2,1)} %vw_in.1, ...), custom_call_target="tpu_custom_call" | custom-call | flops 536870912 | bytes 5242880 | tf_op jit(solution)/shard_map/kv/pallas_call | solution.py:273
  3.0 4.0 %collective-permute-start = (bf16[256,512]{1,0:T(8,128)(2,1)S(1)}, bf16[256,512]{1,0:T(8,128)(2,1)S(1)}, u32[]{:S(2)}, u32[]{:S(2)}) collective-permute-start(bf16[256,512]{1,0:T(8,128)(2,1)S(1)} %get-tuple-element.21.kv), channel_id=1, source_target_pairs={{0,16},{8,24},{16,32},{24,40},{32,48},{40,56},{48,64},{56,72},{64,... | collective-permute-start | bytes 786440 | tf_op jit(solution)/shard_map/ppermute | solution.py:299
  7.0 9.7 %collective-permute-start.1 = (bf16[256,512]{1,0:T(8,128)(2,1)S(1)}, bf16[256,512]{1,0:T(8,128)(2,1)S(1)}, u32[]{:S(2)}, u32[]{:S(2)}) collective-permute-start(bf16[256,512]{1,0:T(8,128)(2,1)S(1)} %get-tuple-element.21.kv), channel_id=1, source_target_pairs={{0,8},{8,0},{16,24},{24,16},{32,40},{40,32},{48,56},{56,48},{64,72... | collective-permute-start | bytes 786440 | tf_op jit(solution)/shard_map/ppermute | solution.py:300
  16.8 0.0 copy-done.2
  16.8 0.0 copy-done.3
  16.8 0.0 copy-start.1
  16.8 0.0 copy-start
  16.8 3.0 %query.1 = (bf16[512,256]{1,0:T(8,128)(2,1)S(1)}, f32[512,256]{1,0:T(8,128)S(1)}, f32[512,256]{1,0:T(8,128)S(1)}, f32[512,128]{1,0:T(8,128)S(1)}) custom-call(s32[1,48]{1,0:T(1,128)S(1)} %bitcast.7, f32[1,256]{1,0:T(1,128)S(1)} %bitcast.10, f32[256,256]{1,0:T(8,128)S(1)} %get-tuple-element.22.trig, bf16[256,512]{1,0:T(8,128)(2,1)S(1)} %get-tuple-element.21.kv, ...), custom_call_target="tpu_custom_call" | custom-call | flops 1073741824 | bytes 5242880 | tf_op jit(solution)/shard_map/query/pallas_call | solution.py:302
  19.8 0.0 collective-permute-done.near
  19.8 1.9 %collective-permute-start.2 = (bf16[256,512]{1,0:T(8,128)(2,1)S(1)}, bf16[256,512]{1,0:T(8,128)(2,1)S(1)}, u32[]{:S(2)}, u32[]{:S(2)}) collective-permute-start(bf16[256,512]{1,0:T(8,128)(2,1)S(1)} %collective-permute-done.near), channel_id=1, source_target_pairs={{0,8},{8,0},{16,24},{24,16},{32,40},{40,32},{48,56},{56,48},{64,72... | collective-permute-start | bytes 786440 | tf_op jit(solution)/shard_map/ppermute | solution.py:319
  21.7 0.0 collective-permute-done.1.own
  21.8 0.0 copy-done.1
  21.8 1.6 %near.1 = (f32[512,256]{1,0:T(8,128)S(1)}, f32[512,128]{1,0:T(8,128)S(1)}) custom-call(s32[1,48]{1,0:T(1,128)S(1)} %bitcast.8, s32[3,96]{1,0:T(4,128)S(1)} %bitcast.4, bf16[512,256]{1,0:T(8,128)(2,1)S(1)} %get-tuple-element.26.query, f32[512,256]{1,0:T(8,128)S(1)} %get-tuple-element.28.num_in, f32[512,128]{1,0:T(8,128)S(1)} %get-tuple-element.29.den_in, ...), custom_call_target="tpu_custom_call" | custom-call | flops 134217728 | bytes 3145728 | tf_op jit(solution)/shard_map/near/pallas_call | solution.py:322
  23.4 0.0 collective-permute-done.2.far
  23.4 0.0 copy-done
  23.4 1.9 %shard_map.100 = (bf16[96,2048]{1,0:T(8,128)(2,1)S(1)}, bf16[32,2048]{1,0:T(8,128)(2,1)S(1)}, bf16[32,2048]{1,0:T(8,128)(2,1)S(1)}, bf16[96,2048]{1,0:T(8,128)(2,1)S(1)}) custom-call(s32[1,48]{1,0:T(1,128)S(1)} %bitcast.9, s32[3,96]{1,0:T(4,128)S(1)} %bitcast.5, bf16[512,256]{1,0:T(8,128)(2,1)S(1)} %get-tuple-element.26.query, ...), custom_call_target="tpu_custom_call" | custom-call | flops 536870912 | bytes 4194304 | tf_op jit(solution)/shard_map/pallas_call | solution.py:335
  25.2 1.9 %collective-permute-start.3 = (bf16[96,2048]{1,0:T(8,128)(2,1)S(1)}, bf16[96,2048]{1,0:T(8,128)(2,1)S(1)}, u32[]{:S(2)}, u32[]{:S(2)}) collective-permute-start(bf16[96,2048]{1,0:T(8,128)(2,1)S(1)} %get-tuple-element.34), channel_id=1, source_target_pairs={{0,1},{1,0},{2,3},{3,2},{4,5},{5,4},{6,7},{7,6},{8,15},{9,10},{10,... | collective-permute-start | bytes 1179656 | tf_op jit(solution)/shard_map/ppermute | solution.py:350
  27.2 1.9 %collective-permute-start.5 = (bf16[32,2048]{1,0:T(8,128)(2,1)S(1)}, bf16[32,2048]{1,0:T(8,128)(2,1)S(1)}, u32[]{:S(2)}, u32[]{:S(2)}) collective-permute-start(bf16[32,2048]{1,0:T(8,128)(2,1)S(1)} %get-tuple-element.35), channel_id=1, source_target_pairs={{0,7},{1,2},{2,1},{3,4},{4,3},{5,6},{6,5},{7,0},{8,9},{9,8},{10,11... | collective-permute-start | bytes 393224 | tf_op jit(solution)/shard_map/ppermute | solution.py:350
  29.1 5.7 %collective-permute-start.6 = (bf16[32,2048]{1,0:T(8,128)(2,1)S(1)}, bf16[32,2048]{1,0:T(8,128)(2,1)S(1)}, u32[]{:S(2)}, u32[]{:S(2)}) collective-permute-start(bf16[32,2048]{1,0:T(8,128)(2,1)S(1)} %get-tuple-element.36), channel_id=1, source_target_pairs={{0,2},{1,7},{2,4},{3,1},{4,6},{5,3},{6,0},{7,5},{8,14},{9,11},{10,... | collective-permute-start | bytes 393224 | tf_op jit(solution)/shard_map/ppermute | solution.py:350
  34.8 3.0 %collective-permute-done.3.got_a = bf16[96,2048]{1,0:T(8,128)(2,1)S(1)} collective-permute-done((bf16[96,2048]{1,0:T(8,128)(2,1)S(1)}, bf16[96,2048]{1,0:T(8,128)(2,1)S(1)}, u32[]{:S(2)}, u32[]{:S(2)}) %collective-permute-start.3) | collective-permute-done | bytes 393248 | tf_op jit(solution)/shard_map/ppermute | solution.py:350
  37.9 1.9 %collective-permute-start.4 = (bf16[32,2048]{1,0:T(8,128)(2,1)S(1)}, bf16[32,2048]{1,0:T(8,128)(2,1)S(1)}, u32[]{:S(2)}, u32[]{:S(2)}) collective-permute-start(bf16[32,2048]{1,0:T(8,128)(2,1)S(1)} %shard_map.101), channel_id=1, source_target_pairs={{0,6},{1,3},{2,0},{3,5},{4,2},{5,7},{6,4},{7,1},{8,10},{9,15},{10,... | collective-permute-start | bytes 393224 | tf_op jit(solution)/shard_map/ppermute | solution.py:350
  39.8 0.0 collective-permute-done.5.got_b
  39.8 0.0 collective-permute-done.6.got_c
  39.8 0.1 shard_map.102
  39.9 5.5 %collective-permute-start.7 = (bf16[32,2048]{1,0:T(8,128)(2,1)S(1)}, bf16[32,2048]{1,0:T(8,128)(2,1)S(1)}, u32[]{:S(2)}, u32[]{:S(2)}) collective-permute-start(bf16[32,2048]{1,0:T(8,128)(2,1)S(1)} %shard_map.102), channel_id=1, source_target_pairs={{0,2},{1,7},{2,4},{3,1},{4,6},{5,3},{6,0},{7,5},{8,14},{9,11},{10,... | collective-permute-start | bytes 393224 | tf_op jit(solution)/shard_map/ppermute | solution.py:350
  45.4 2.5 %collective-permute-done.4.first = bf16[32,2048]{1,0:T(8,128)(2,1)S(1)} collective-permute-done((bf16[32,2048]{1,0:T(8,128)(2,1)S(1)}, bf16[32,2048]{1,0:T(8,128)(2,1)S(1)}, u32[]{:S(2)}, u32[]{:S(2)}) %collective-permute-start.4) | collective-permute-done | bytes 131104 | tf_op jit(solution)/shard_map/ppermute | solution.py:350
  47.9 0.3 collective-permute-done.7.second
  48.2 0.7 %last.1 = bf16[32,2048]{1,0:T(8,128)(2,1)} custom-call(bf16[96,2048]{1,0:T(8,128)(2,1)S(1)} %get-tuple-element.33.rest, bf16[96,2048]{1,0:T(8,128)(2,1)S(1)} %collective-permute-done.3.got_a, bf16[32,2048]{1,0:T(8,128)(2,1)S(1)} %collective-permute-done.4.first, bf16[32,2048]{1,0:T(8,128)(2,1)S(1)} %collective-permute-done.7.second), custom_call_target="tpu_custom_call" | custom-call | tf_op jit(solution)/shard_map/last/pallas_call | solution.py:368
  (1 shorter events, 0.0 us)
Async XLA Ops:
  0.0 16.8 %copy-start.2 = (s32[48]{0:T(128)S(1)}, s32[48]{0:T(128)}, u32[]{:S(2)}) copy-start(s32[48]{0:T(128)} %param.18) | copy-start | bytes 580
  0.0 16.8 %copy-start.3 = (f32[256]{0:T(256)S(1)}, f32[256]{0:T(256)}, u32[]{:S(2)}) copy-start(f32[256]{0:T(256)} %param.15) | copy-start | bytes 3076
  3.0 16.8 %collective-permute-start = (bf16[256,512]{1,0:T(8,128)(2,1)S(1)}, bf16[256,512]{1,0:T(8,128)(2,1)S(1)}, u32[]{:S(2)}, u32[]{:S(2)}) collective-permute-start(bf16[256,512]{1,0:T(8,128)(2,1)S(1)} %get-tuple-element.21.kv), channel_id=1, source_target_pairs={{0,16},{8,24},{16,32},{24,40},{32,48},{40,56},{48,64},{56,72},{64,... | collective-permute-start | bytes 786440 | tf_op jit(solution)/shard_map/ppermute | solution.py:299
  7.0 14.7 %collective-permute-start.1 = (bf16[256,512]{1,0:T(8,128)(2,1)S(1)}, bf16[256,512]{1,0:T(8,128)(2,1)S(1)}, u32[]{:S(2)}, u32[]{:S(2)}) collective-permute-start(bf16[256,512]{1,0:T(8,128)(2,1)S(1)} %get-tuple-element.21.kv), channel_id=1, source_target_pairs={{0,8},{8,0},{16,24},{24,16},{32,40},{40,32},{48,56},{56,48},{64,72... | collective-permute-start | bytes 786440 | tf_op jit(solution)/shard_map/ppermute | solution.py:300
  16.8 5.0 %copy-start.1 = (s32[96,3]{0,1:T(4,128)S(1)}, s32[96,3]{0,1:T(4,128)}, u32[]{:S(2)}) copy-start(s32[96,3]{0,1:T(4,128)} %param.19) | copy-start | bytes 3460
  16.8 6.6 %copy-start = (bf16[512,2048]{1,0:T(8,128)(2,1)S(1)}, bf16[512,2048]{1,0:T(8,128)(2,1)}, u32[]{:S(2)}) copy-start(bf16[512,2048]{1,0:T(8,128)(2,1)} %ow.1) | copy-start | bytes 6291460
  19.8 3.5 %collective-permute-start.2 = (bf16[256,512]{1,0:T(8,128)(2,1)S(1)}, bf16[256,512]{1,0:T(8,128)(2,1)S(1)}, u32[]{:S(2)}, u32[]{:S(2)}) collective-permute-start(bf16[256,512]{1,0:T(8,128)(2,1)S(1)} %collective-permute-done.near), channel_id=1, source_target_pairs={{0,8},{8,0},{16,24},{24,16},{32,40},{40,32},{48,56},{56,48},{64,72... | collective-permute-start | bytes 786440 | tf_op jit(solution)/shard_map/ppermute | solution.py:319
  25.2 12.6 %collective-permute-start.3 = (bf16[96,2048]{1,0:T(8,128)(2,1)S(1)}, bf16[96,2048]{1,0:T(8,128)(2,1)S(1)}, u32[]{:S(2)}, u32[]{:S(2)}) collective-permute-start(bf16[96,2048]{1,0:T(8,128)(2,1)S(1)} %get-tuple-element.34), channel_id=1, source_target_pairs={{0,1},{1,0},{2,3},{3,2},{4,5},{5,4},{6,7},{7,6},{8,15},{9,10},{10,... | collective-permute-start | bytes 1179656 | tf_op jit(solution)/shard_map/ppermute | solution.py:350
  27.2 12.7 %collective-permute-start.5 = (bf16[32,2048]{1,0:T(8,128)(2,1)S(1)}, bf16[32,2048]{1,0:T(8,128)(2,1)S(1)}, u32[]{:S(2)}, u32[]{:S(2)}) collective-permute-start(bf16[32,2048]{1,0:T(8,128)(2,1)S(1)} %get-tuple-element.35), channel_id=1, source_target_pairs={{0,7},{1,2},{2,1},{3,4},{4,3},{5,6},{6,5},{7,0},{8,9},{9,8},{10,11... | collective-permute-start | bytes 393224 | tf_op jit(solution)/shard_map/ppermute | solution.py:350
  29.1 10.7 %collective-permute-start.6 = (bf16[32,2048]{1,0:T(8,128)(2,1)S(1)}, bf16[32,2048]{1,0:T(8,128)(2,1)S(1)}, u32[]{:S(2)}, u32[]{:S(2)}) collective-permute-start(bf16[32,2048]{1,0:T(8,128)(2,1)S(1)} %get-tuple-element.36), channel_id=1, source_target_pairs={{0,2},{1,7},{2,4},{3,1},{4,6},{5,3},{6,0},{7,5},{8,14},{9,11},{10,... | collective-permute-start | bytes 393224 | tf_op jit(solution)/shard_map/ppermute | solution.py:350
  37.9 10.0 %collective-permute-start.4 = (bf16[32,2048]{1,0:T(8,128)(2,1)S(1)}, bf16[32,2048]{1,0:T(8,128)(2,1)S(1)}, u32[]{:S(2)}, u32[]{:S(2)}) collective-permute-start(bf16[32,2048]{1,0:T(8,128)(2,1)S(1)} %shard_map.101), channel_id=1, source_target_pairs={{0,6},{1,3},{2,0},{3,5},{4,2},{5,7},{6,4},{7,1},{8,10},{9,15},{10,... | collective-permute-start | bytes 393224 | tf_op jit(solution)/shard_map/ppermute | solution.py:350
  39.9 8.3 %collective-permute-start.7 = (bf16[32,2048]{1,0:T(8,128)(2,1)S(1)}, bf16[32,2048]{1,0:T(8,128)(2,1)S(1)}, u32[]{:S(2)}, u32[]{:S(2)}) collective-permute-start(bf16[32,2048]{1,0:T(8,128)(2,1)S(1)} %shard_map.102), channel_id=1, source_target_pairs={{0,2},{1,7},{2,4},{3,1},{4,6},{5,3},{6,0},{7,5},{8,14},{9,11},{10,... | collective-permute-start | bytes 393224 | tf_op jit(solution)/shard_map/ppermute | solution.py:350
